TPU v7x, 32 devices: a whole 2x2x4 slice. The times are simulated.
32 devices in a mesh: gx: 4 (over z), gy: 8 (over y, x, core).
Axes of the slice: x: 2, y: 2, z: 4, core: 2. Of those that a mesh axis runs over, the one named last changes fastest.
Arguments:
- die_basis: float32 [64, 256, 512], P('gx', 'gy'), may hold values from -0.078125 to 0.078125
- die_coeff: float32 [5, 64, 256], P(None, 'gx', 'gy'), may hold values from 0.2 to 5
- pkg_basis: float32 [1024, 64, 512], P(('gx', 'gy')), may hold values from -0.09375 to 0.09375
- send_blocks: int32 [32, 4, 4], P(('gx', 'gy')), may hold values from 0 to 31
- columns: int32 [5, 1024, 4], P(None, ('gx', 'gy')), may hold values from 0 to 47
- counts: int32 [5, 1024], P(None, ('gx', 'gy')), may hold values from 1 to 4
- pkg_blocks: float32 [5, 1024, 64, 256], P(None, ('gx', 'gy')), may hold values from -48 to 48
Outputs:
- reduced: float32 [5, 512, 512], replicated
Inputs may be any that keep to these rules, and one draw needn't show every extreme that they name: `columns`: indices below 32 name the partition's own blocks, the others its ghost blocks in the order of the statement.
All inputs are finite; a program needn't handle non-finite values.
Results may differ from a plain program's by a relative error of at most 0.0001.
Values sent between devices are 32-bit elements; how exact they have to be, the bound alone decides.
No kernel may reach another device: no remote copies, remote signals or barrier semaphores. Data moves between devices by JAX's collectives and lax.ppermute only.
A program may use at most 256 MiB of HBM per device.

v0:
```python
import jax
import jax.numpy as jnp
from jax import lax
from jax.experimental import pallas as pl
from jax.experimental.pallas import tpu as pltpu
from jax.sharding import PartitionSpec as P

ROWS = 4
BF16 = jnp.bfloat16
F32 = jnp.float32


def from_behind(value, axis, steps):
    count = lax.axis_size(axis)
    leading, last = (max(0, -steps), min(count, count - steps))
    return lax.ppermute(value, axis, [(source, source + steps) for source in range(leading, last)])


def passed_along(value, axis, steps):
    count = lax.axis_size(axis)
    pairs = [(source, (source + steps) % count) for source in range(count)]
    return lax.ppermute(value, axis, pairs)


def split(value):
    high = value.astype(BF16)
    return high, (value - high.astype(F32)).astype(BF16)


def mm(a, b):
    return lax.dot_general(a, b, (((1,), (0,)), ((), ())), preferred_element_type=F32)


def gather_kernel(lists, table, *rest):
    outs, sem = rest[:-1], rest[-1]
    copies = []
    for side_index, out in enumerate(outs):
        for k in range(out.shape[0]):
            copies.append(
                pltpu.make_async_copy(
                    table.at[lists[side_index, k]], out.at[k], sem.at[side_index, k]
                )
            )
    for copy in copies:
        copy.start()
    for copy in copies:
        copy.wait()


def gather_sends(table, lists):
    sides, cap = lists.shape
    shape = jax.ShapeDtypeStruct((cap,) + table.shape[1:], table.dtype)
    return pl.pallas_call(
        gather_kernel,
        out_shape=[shape] * sides,
        grid_spec=pltpu.PrefetchScalarGridSpec(
            num_scalar_prefetch=1,
            grid=(),
            in_specs=[pl.BlockSpec(memory_space=pl.ANY)],
            out_specs=[pl.BlockSpec(memory_space=pl.ANY)] * sides,
            scratch_shapes=[pltpu.SemaphoreType.DMA((sides, cap))],
        ),
        name="gather_sends",
    )(lists, table)


def own_kernel(owned, high, low, turned):
    group, block, width = owned.shape
    value = owned[...]
    top, rest = split(value)
    high[...] = top
    low[...] = rest
    flat = value.reshape(group * block, width)
    t_high, t_low = split(flat.T)
    turned[0, :, : group * block] = t_high
    turned[0, :, group * block :] = t_low


def split_own(owned, entries):
    count, block, width = owned.shape
    steps = count // ROWS
    depth = ROWS * block
    table = jax.ShapeDtypeStruct((entries, block, width), BF16)
    table_spec = pl.BlockSpec((ROWS, block, width), lambda i: (i, 0, 0))
    return pl.pallas_call(
        own_kernel,
        out_shape=[table, table, jax.ShapeDtypeStruct((steps, width, 2 * depth), BF16)],
        grid=(steps,),
        in_specs=[table_spec],
        out_specs=[
            table_spec,
            table_spec,
            pl.BlockSpec((1, width, 2 * depth), lambda i: (i, 0, 0)),
        ],
        name="split_own",
    )(owned)


def ghost_kernel(*refs):
    ghosts, high, low = refs[:-4], refs[-2], refs[-1]
    for k, ghost in enumerate(ghosts):
        @pl.when(pl.program_id(0) == k)
        def _():
            top, rest = split(ghost[...])
            high[...] = top
            low[...] = rest


def split_ghosts(ghosts, high, low, count):
    cap, block, width = ghosts[0].shape
    whole = pl.BlockSpec(ghosts[0].shape, lambda i: (0, 0, 0))
    out_spec = pl.BlockSpec(ghosts[0].shape, lambda i: (count // cap + i, 0, 0))
    n = len(ghosts)
    return pl.pallas_call(
        ghost_kernel,
        out_shape=[jax.ShapeDtypeStruct(high.shape, BF16)] * 2,
        grid=(n,),
        in_specs=[whole] * n + [pl.BlockSpec(memory_space=pl.ANY)] * 2,
        out_specs=[out_spec] * 2,
        input_output_aliases={n: 0, n + 1: 1},
        name="split_ghosts",
    )(*ghosts, high, low)


def die_kernel(basis, next_row, next_col, fields, turned):
    nx, ny, width = basis.shape
    value = basis[...]
    below = jnp.concatenate([value[1:], next_row[...]], axis=0)
    right = jnp.concatenate([value[:, 1:], next_col[...]], axis=1)
    for k, field in enumerate((value, value - below, value - right)):
        flat = field.reshape(nx * ny, width)
        fields[k] = flat
        t_high, t_low = split(flat.T)
        turned[k, :, : nx * ny] = t_high
        turned[k, :, nx * ny :] = t_low


def split_die(basis, next_row, next_col):
    nx, ny, width = basis.shape
    cells = nx * ny
    return pl.pallas_call(
        die_kernel,
        out_shape=[
            jax.ShapeDtypeStruct((3, cells, width), F32),
            jax.ShapeDtypeStruct((3, width, 2 * cells), BF16),
        ],
        name="split_die",
    )(basis, next_row, next_col)


def gram(turned, weights, field):
    cells = field.shape[0]
    w_high, w_low = split(weights * field)
    t_high, t_low = turned[:, :cells], turned[:, cells:]
    return mm(t_high, w_high) + mm(t_low, w_high) + mm(t_high, w_low)


def term_kernel(
    columns, counts, fields, die_turned, weights, turned, high, low, blocks, out,
    image_high, image_low, *, first, picks,
):
    term = first + pl.program_id(0)
    count = blocks.shape[1]
    block, wide = blocks.shape[2:]
    entries = wide // block
    groups = turned.shape[0]
    per = count // groups
    depth = per * block
    width = out.shape[2]
    lane = lax.broadcasted_iota(jnp.int32, (block, wide), 1)

    def image_rows(group, slot):
        for k in range(per):
            row = group * per + k
            picked = [columns[term, row * entries + e] for e in range(entries)]
            live = counts[term, row] * block
            matrix = jnp.where(lane < live, blocks[0, row], 0.0)
            a_high, a_low = split(matrix)
            b_high = jnp.concatenate([high[c] for c in picked], axis=0)
            b_low = jnp.concatenate([low[c] for c in picked], axis=0)
            both = mm(jnp.concatenate([a_high, a_low], axis=0), b_high)
            image = both[:block] + both[block:] + mm(a_high, b_low)
            top, rest = split(image)
            image_high[slot, k * block : (k + 1) * block, :] = top
            image_low[slot, k * block : (k + 1) * block, :] = rest

    def project(group, slot):
        top, rest = image_high[slot], image_low[slot]
        pair = turned[group]
        left = jnp.concatenate([pair, pair[:, :depth]], axis=1)
        right = jnp.concatenate([top, top, rest], axis=0)
        out[0] += mm(left, right)

    image_rows(0, 0)
    for which, (q, die) in enumerate(picks):
        @pl.when(term == q)
        def _():
            total = gram(die_turned[die[0]], weights[0], fields[die[0]])
            for k in die[1:]:
                total += gram(die_turned[k], weights[0], fields[k])
            out[0] = total

    def step(group, carry):
        project(group - 1, (group - 1) % 2)
        image_rows(group, group % 2)
        return carry

    lax.fori_loop(1, groups, step, 0)
    project(groups - 1, (groups - 1) % 2)


DIE_FIELDS = ((0,), (1,), (2,), (0,), (1, 2))


def project_terms(first, number, columns, counts, fields, die_turned, weights, turned, high, low, blocks):
    terms, count, block, wide = blocks.shape
    width = high.shape[2]
    depth = turned.shape[2] // 2
    picks = tuple((q, DIE_FIELDS[q]) for q in range(first, first + number))

    def whole(array):
        return pl.BlockSpec(array.shape, lambda i, *_: (0,) * array.ndim, pipeline_mode=pl.Buffered(1))

    def kernel(*refs):
        term_kernel(*refs, first=first, picks=picks)

    return pl.pallas_call(
        kernel,
        out_shape=jax.ShapeDtypeStruct((number, width, width), F32),
        grid_spec=pltpu.PrefetchScalarGridSpec(
            num_scalar_prefetch=2,
            grid=(number,),
            in_specs=[
                whole(fields),
                whole(die_turned),
                pl.BlockSpec((1,) + weights.shape[1:], lambda i, *_: (first + i, 0, 0)),
                whole(turned),
                whole(high),
                whole(low),
                pl.BlockSpec((1, count, block, wide), lambda i, *_: (first + i, 0, 0, 0)),
            ],
            out_specs=pl.BlockSpec((1, width, width), lambda i, *_: (i, 0, 0)),
            scratch_shapes=[pltpu.VMEM((2, depth, width), BF16)] * 2,
        ),
        compiler_params=pltpu.CompilerParams(vmem_limit_bytes=60 << 20),
        name=f"terms_{first}_{number}",
    )(columns, counts, fields, die_turned, weights, turned, high, low, blocks)


def flip(value, axis, mask):
    count = lax.axis_size(axis)
    return lax.ppermute(value, axis, [(i, i ^ mask) for i in range(count)])


def side(axis, mask):
    return (lax.axis_index(axis) // mask) % 2


def halve(value, dim):
    axis, mask = dim
    mine = side(axis, mask)
    halves = value.reshape((2, value.shape[0] // 2) + value.shape[1:])
    send = lax.dynamic_index_in_dim(halves, 1 - mine, 0, keepdims=False)
    keep = lax.dynamic_index_in_dim(halves, mine, 0, keepdims=False)
    return keep + flip(send, axis, mask)


def double(value, dim):
    axis, mask = dim
    other = flip(value, axis, mask)
    low = jnp.concatenate([value, other], axis=0)
    high = jnp.concatenate([other, value], axis=0)
    return jnp.where(side(axis, mask) == 0, low, high)


def masks(axis):
    count = lax.axis_size(axis)
    return [(axis, 1 << k) for k in range(count.bit_length() - 1)]


def total_of(terms):
    flat = terms.reshape(-1, terms.shape[-1])
    core, *plane = masks("gy")
    line = masks("gx")
    orders = [plane + line, plane[1:] + line + plane[:1], line + plane]
    flat = halve(flat, core)
    rows = flat.shape[0]
    unit = 8 << len(plane + line)
    if rows % unit or rows // unit < 3:
        orders, sizes = orders[:1], [rows]
    else:
        each = rows // unit // 3
        sizes = [rows - 2 * each * unit, each * unit, each * unit]
    starts = [sum(sizes[:k]) for k in range(len(sizes))]
    parts = [lax.slice_in_dim(flat, a, a + n) for a, n in zip(starts, sizes)]
    stages = len(plane + line)
    for k in range(stages):
        parts = [halve(p, o[k]) for p, o in zip(parts, orders)]
    for k in reversed(range(stages)):
        parts = [double(p, o[k]) for p, o in zip(parts, orders)]
    return double(jnp.concatenate(parts, axis=0), core).reshape(terms.shape)


def body(die_basis, die_coeff, pkg_basis, send_blocks, columns, counts, pkg_blocks):
    next_x_row = from_behind(die_basis[:1], "gx", -1)
    next_y_col = from_behind(die_basis[:, :1], "gy", -1)
    lists = send_blocks[0]
    sends = gather_sends(pkg_basis, lists)
    ghosts = [
        passed_along(sends[0], "gx", 1),
        passed_along(sends[1], "gx", -1),
        passed_along(sends[2], "gy", 1),
        passed_along(sends[3], "gy", -1),
    ]
    count = pkg_basis.shape[0]
    terms = columns.shape[0]
    high, low, turned = split_own(pkg_basis, count + lists.shape[0] * lists.shape[1])
    fields, die_turned = split_die(die_basis, next_x_row, next_y_col)
    high, low = split_ghosts(ghosts, high, low, count)
    weights = die_coeff.reshape(terms, -1, 1)
    columns = columns.reshape(terms, -1)
    parts = project_terms(
        0, terms, columns, counts, fields, die_turned, weights, turned, high, low, pkg_blocks
    )
    return total_of(parts)


def solution(mesh):
    placed = (
        P("gx", "gy", None),
        P(None, "gx", "gy"),
        P(("gx", "gy"), None, None),
        P(("gx", "gy"), None, None),
        P(None, ("gx", "gy"), None),
        P(None, ("gx", "gy")),
        P(None, ("gx", "gy"), None, None),
    )
    return jax.shard_map(body, mesh=mesh, in_specs=placed, out_specs=P(), check_vma=False)
```

profile of v0, /device:TPU:0, one launch (start us, length us, event | category | flops | bytes accessed | tf_op | source)
XLA Modules:
  0.0 259.7 jit_solution(7738011085669594699)
XLA Ops:
  0.0 65.5 %gather_sends.1 = (f32[4,64,512]{2,1,0:T(8,128)}, f32[4,64,512]{2,1,0:T(8,128)}, f32[4,64,512]{2,1,0:T(8,128)}, f32[4,64,512]{2,1,0:T(8,128)}) custom-call(s32[4,4]{1,0:T(4,128)} %bitcast.93, f32[32,64,512]{2,1,0:T(8,128)} %table.1), custom_call_target="tpu_custom_call" | custom-call | tf_op jit(solution)/shard_map/gather_sends/pallas_call | solution.py:53
  65.5 3.1 %collective-permute-start.2 = (f32[4,64,512]{2,1,0:T(8,128)}, f32[4,64,512]{2,1,0:T(8,128)S(1)}, u32[]{:S(2)}, u32[]{:S(2)}) collective-permute-start(f32[4,64,512]{2,1,0:T(8,128)} %get-tuple-element.19), channel_id=1, source_target_pairs={{0,8},{8,16},{16,24},{24,0},{1,9},{9,17},{17,25},{25,1},{2,10},{10... | collective-permute-start | bytes 1572872 | tf_op jit(solution)/shard_map/ppermute | solution.py:22
  68.6 2.1 collective-permute-start.3
  70.7 2.6 %collective-permute-start.5 = (f32[4,64,512]{2,1,0:T(8,128)}, f32[4,64,512]{2,1,0:T(8,128)S(1)}, u32[]{:S(2)}, u32[]{:S(2)}) collective-permute-start(f32[4,64,512]{2,1,0:T(8,128)} %get-tuple-element.22), channel_id=1, source_target_pairs={{0,7},{1,0},{2,1},{3,2},{4,3},{5,4},{6,5},{7,6},{8,15},{9,8},{10,9... | collective-permute-start | bytes 1572872 | tf_op jit(solution)/shard_map/ppermute | solution.py:22
  78.7 7.5 %split_own.1 = (bf16[48,64,512]{2,1,0:T(8,128)(2,1)}, bf16[48,64,512]{2,1,0:T(8,128)(2,1)}, bf16[8,512,512]{2,1,0:T(8,128)(2,1)}) custom-call(f32[32,64,512]{2,1,0:T(8,128)} %table.1), custom_call_target="tpu_custom_call" | custom-call | tf_op jit(solution)/shard_map/split_own/pallas_call | solution.py:85
  86.2 2.5 reshape.61.refs_4_
  89.5 5.3 %collective-permute-done.next_row = f32[1,32,512]{2,1,0:T(8,128)S(1)} collective-permute-done((f32[1,32,512]{2,1,0:T(8,128)S(1)}, f32[1,32,512]{2,1,0:T(8,128)S(1)}, u32[]{:S(2)}, u32[]{:S(2)}) %collective-permute-start) | collective-permute-done | bytes 65568 | tf_op jit(solution)/shard_map/ppermute | solution.py:16
  95.5 4.7 %split_die.1 = (f32[3,512,512]{2,1,0:T(8,128)}, bf16[3,512,1024]{2,1,0:T(8,128)(2,1)}) custom-call(f32[16,32,512]{2,1,0:T(8,128)} %basis.1, f32[1,32,512]{2,1,0:T(8,128)} %copy-done.6, f32[16,1,512]{2,1,0:T(1,128)} %copy-done.8), custom_call_target="tpu_custom_call" | custom-call | tf_op jit(solution)/shard_map/split_die/pallas_call | solution.py:141
  101.5 3.5 %split_ghosts.1 = (bf16[48,64,512]{2,1,0:T(8,128)(2,1)}, bf16[48,64,512]{2,1,0:T(8,128)(2,1)}) custom-call(f32[4,64,512]{2,1,0:T(8,128)} %copy-done.2, f32[4,64,512]{2,1,0:T(8,128)} %copy-done.3, f32[4,64,512]{2,1,0:T(8,128)} %copy-done.4, f32[4,64,512]{2,1,0:T(8,128)} %copy-done.5, ...), custom_call_target="tpu_custom_call", output_to_operand_aliasing={{0}: (4, {}), {1}: (5, {})} | custom-call | tf_op jit(solution)/shard_map/split_ghosts/pallas_call | solution.py:114
  105.0 51.1 %terms_0_5.1 = f32[5,512,512]{2,1,0:T(8,128)} custom-call(s32[5,128]{1,0:T(8,128)} %reshape.47.refs_0_, s32[5,32]{1,0:T(8,128)} %refs_1_.1, f32[3,512,512]{2,1,0:T(8,128)} %get-tuple-element.16.refs_2_, bf16[3,512,1024]{2,1,0:T(8,128)(2,1)} %get-tuple-element.17.refs_3_, f32[5,512,1]{2,1,0:T(8,128)} %reshape.61.refs_4_, ...), custom_call_target="tpu_custom_call" | custom-call | tf_op jit(solution)/shard_map/terms_0_5/pallas_call | solution.py:227
  156.2 2.0 dynamic-slice_bitcast_fusion
  158.1 4.0 %collective-permute-start.6 = (f32[1280,512]{1,0:T(8,128)S(1)}, f32[1280,512]{1,0:T(8,128)}, u32[]{:S(2)}, u32[]{:S(2)}) collective-permute-start(f32[1280,512]{1,0:T(8,128)S(1)} %dynamic-slice_bitcast_fusion), channel_id=1, source_target_pairs={{0,1},{1,0},{2,3},{3,2},{4,5},{5,4},{6,7},{7,6},{8,9},{9,8},{10,11... | collective-permute-start | bytes 7864328 | tf_op jit(solution)/shard_map/ppermute | solution.py:252
  162.2 4.7 %collective-permute-done.6 = f32[1280,512]{1,0:T(8,128)} collective-permute-done((f32[1280,512]{1,0:T(8,128)S(1)}, f32[1280,512]{1,0:T(8,128)}, u32[]{:S(2)}, u32[]{:S(2)}) %collective-permute-start.6) | collective-permute-done | bytes 2621472 | tf_op jit(solution)/shard_map/ppermute | solution.py:252
  166.8 3.1 %bitcast_add_fusion = f32[1280,512]{1,0:T(8,128)S(1)} fusion(f32[1280,512]{1,0:T(8,128)} %collective-permute-done.6, f32[2,1280,512]{2,1,0:T(8,128)} %bitcast.68, s32[]{:T(128)S(6)} %select_n.266), kind=kLoop, calls=%fused_computation.2 | loop fusion | flops 655360 | bytes 7864324 | tf_op jit(solution)/shard_map/add | solution.py:265
  172.2 2.4 collective-permute-start.23
  175.6 7.9 %collective-permute-done.15 = f32[192,512]{1,0:T(8,128)} collective-permute-done((f32[192,512]{1,0:T(8,128)}, f32[192,512]{1,0:T(8,128)}, u32[]{:S(2)}, u32[]{:S(2)}) %collective-permute-start.15) | collective-permute-done | bytes 393248 | tf_op jit(solution)/shard_map/ppermute | solution.py:252
  184.6 2.4 collective-permute-start.16
  190.3 3.5 %collective-permute-done.16 = f32[96,512]{1,0:T(8,128)S(1)} collective-permute-done((f32[96,512]{1,0:T(8,128)S(1)}, f32[96,512]{1,0:T(8,128)S(1)}, u32[]{:S(2)}, u32[]{:S(2)}) %collective-permute-start.16) | collective-permute-done | bytes 196640 | tf_op jit(solution)/shard_map/ppermute | solution.py:252
  193.8 2.1 collective-permute-start.17
  196.0 5.5 %collective-permute-done.24 = f32[96,512]{1,0:T(8,128)S(1)} collective-permute-done((f32[96,512]{1,0:T(8,128)S(1)}, f32[96,512]{1,0:T(8,128)S(1)}, u32[]{:S(2)}, u32[]{:S(2)}) %collective-permute-start.24) | collective-permute-done | bytes 196640 | tf_op jit(solution)/shard_map/ppermute | solution.py:252
  203.8 2.4 collective-permute-done.25
  208.3 2.1 collective-permute-done.26
  210.8 2.4 collective-permute-done.9
  213.4 3.0 %collective-permute-start.20 = (f32[48,512]{1,0:T(8,128)S(1)}, f32[48,512]{1,0:T(8,128)S(1)}, u32[]{:S(2)}, u32[]{:S(2)}) collective-permute-start(f32[48,512]{1,0:T(8,128)S(1)} %maximum_select_fusion.11), channel_id=1, source_target_pairs={{0,16},{8,24},{16,0},{24,8},{1,17},{9,25},{17,1},{25,9},{2,18},{10... | collective-permute-start | bytes 294920 | tf_op jit(solution)/shard_map/ppermute | solution.py:252
  216.4 4.4 %collective-permute-done.10 = f32[32,512]{1,0:T(8,128)S(1)} collective-permute-done((f32[32,512]{1,0:T(8,128)S(1)}, f32[32,512]{1,0:T(8,128)S(1)}, u32[]{:S(2)}, u32[]{:S(2)}) %collective-permute-start.10) | collective-permute-done | bytes 65568 | tf_op jit(solution)/shard_map/ppermute | solution.py:252
  222.1 4.0 %collective-permute-done.11 = f32[32,512]{1,0:T(8,128)S(1)} collective-permute-done((f32[32,512]{1,0:T(8,128)S(1)}, f32[32,512]{1,0:T(8,128)S(1)}, u32[]{:S(2)}, u32[]{:S(2)}) %collective-permute-start.11) | collective-permute-done | bytes 65568 | tf_op jit(solution)/shard_map/ppermute | solution.py:252
  226.3 2.1 collective-permute-start.21
  229.0 3.2 %collective-permute-done.12 = f32[64,512]{1,0:T(8,128)S(1)} collective-permute-done((f32[64,512]{1,0:T(8,128)S(1)}, f32[64,512]{1,0:T(8,128)S(1)}, u32[]{:S(2)}, u32[]{:S(2)}) %collective-permute-start.12) | collective-permute-done | bytes 131104 | tf_op jit(solution)/shard_map/ppermute | solution.py:252
  233.3 4.4 %collective-permute-done.21 = f32[96,512]{1,0:T(8,128)S(1)} collective-permute-done((f32[96,512]{1,0:T(8,128)S(1)}, f32[96,512]{1,0:T(8,128)S(1)}, u32[]{:S(2)}, u32[]{:S(2)}) %collective-permute-start.21) | collective-permute-done | bytes 196640 | tf_op jit(solution)/shard_map/ppermute | solution.py:252
  239.7 5.9 %collective-permute-done.22 = f32[192,512]{1,0:T(8,128)S(1)} collective-permute-done((f32[192,512]{1,0:T(8,128)S(1)}, f32[192,512]{1,0:T(8,128)S(1)}, u32[]{:S(2)}, u32[]{:S(2)}) %collective-permute-start.22) | collective-permute-done | bytes 393248 | tf_op jit(solution)/shard_map/ppermute | solution.py:252
  249.8 5.2 %collective-permute-done.31 = f32[1280,512]{1,0:T(8,128)} collective-permute-done((f32[1280,512]{1,0:T(8,128)}, f32[1280,512]{1,0:T(8,128)}, u32[]{:S(2)}, u32[]{:S(2)}) %collective-permute-start.31) | collective-permute-done | bytes 2621472 | tf_op jit(solution)/shard_map/ppermute | solution.py:252
  255.0 4.7 %maximum_select_fusion = f32[2560,512]{1,0:T(8,128)} fusion(f32[1280,512]{1,0:T(8,128)} %collective-permute-done.31, f32[384,512]{1,0:T(8,128)S(1)} %maximum_select_fusion.3, f32[384,512]{1,0:T(8,128)S(1)} %maximum_select_fusion.2, f32[512,512]{1,0:T(8,128)S(1)} %maximum_select_fusion.1, pred[]{:T(512)S(6)} %eq.50), kind=kLoop, calls=%fused_computation | loop fusion | flops 9175040 | bytes 10485761 | tf_op jit(solution)/shard_map/jit(_where)/select_n | solution.py:273
  (104 shorter events, 29.8 us)
Async XLA Ops:
  65.5 34.7 %collective-permute-start.2 = (f32[4,64,512]{2,1,0:T(8,128)}, f32[4,64,512]{2,1,0:T(8,128)S(1)}, u32[]{:S(2)}, u32[]{:S(2)}) collective-permute-start(f32[4,64,512]{2,1,0:T(8,128)} %get-tuple-element.19), channel_id=1, source_target_pairs={{0,8},{8,16},{16,24},{24,0},{1,9},{9,17},{17,25},{25,1},{2,10},{10... | collective-permute-start | bytes 1572872 | tf_op jit(solution)/shard_map/ppermute | solution.py:22
  68.6 31.6 %collective-permute-start.3 = (f32[4,64,512]{2,1,0:T(8,128)}, f32[4,64,512]{2,1,0:T(8,128)S(1)}, u32[]{:S(2)}, u32[]{:S(2)}) collective-permute-start(f32[4,64,512]{2,1,0:T(8,128)} %get-tuple-element.20), channel_id=1, source_target_pairs={{0,24},{8,0},{16,8},{24,16},{1,25},{9,1},{17,9},{25,17},{2,26},{10... | collective-permute-start | bytes 1572872 | tf_op jit(solution)/shard_map/ppermute | solution.py:22
  70.7 29.5 %collective-permute-start.4 = (f32[4,64,512]{2,1,0:T(8,128)}, f32[4,64,512]{2,1,0:T(8,128)S(1)}, u32[]{:S(2)}, u32[]{:S(2)}) collective-permute-start(f32[4,64,512]{2,1,0:T(8,128)} %get-tuple-element.21), channel_id=1, source_target_pairs={{0,1},{1,2},{2,3},{3,4},{4,5},{5,6},{6,7},{7,0},{8,9},{9,10},{10,1... | collective-permute-start | bytes 1572872 | tf_op jit(solution)/shard_map/ppermute | solution.py:22
  70.7 29.5 %collective-permute-start.5 = (f32[4,64,512]{2,1,0:T(8,128)}, f32[4,64,512]{2,1,0:T(8,128)S(1)}, u32[]{:S(2)}, u32[]{:S(2)}) collective-permute-start(f32[4,64,512]{2,1,0:T(8,128)} %get-tuple-element.22), channel_id=1, source_target_pairs={{0,7},{1,0},{2,1},{3,2},{4,3},{5,4},{6,5},{7,6},{8,15},{9,8},{10,9... | collective-permute-start | bytes 1572872 | tf_op jit(solution)/shard_map/ppermute | solution.py:22
  74.3 3.1 %collective-permute-start.1 = (f32[16,1,512]{2,1,0:T(1,128)S(1)}, f32[16,1,512]{2,1,0:T(1,128)S(1)}, u32[]{:S(2)}, u32[]{:S(2)}) collective-permute-start(f32[16,1,512]{2,1,0:T(1,128)S(1)} %slice.16), channel_id=1, source_target_pairs={{1,0},{2,1},{3,2},{4,3},{5,4},{6,5},{7,6},{9,8},{10,9},{11,10},{12... | collective-permute-start | bytes 98312 | tf_op jit(solution)/shard_map/ppermute | solution.py:16
  77.4 17.4 %collective-permute-start = (f32[1,32,512]{2,1,0:T(8,128)S(1)}, f32[1,32,512]{2,1,0:T(8,128)S(1)}, u32[]{:S(2)}, u32[]{:S(2)}) collective-permute-start(f32[1,32,512]{2,1,0:T(8,128)S(1)} %slice.15), channel_id=1, source_target_pairs={{8,0},{16,8},{24,16},{9,1},{17,9},{25,17},{10,2},{18,10},{26,18},{... | collective-permute-start | bytes 196616 | tf_op jit(solution)/shard_map/ppermute | solution.py:16
  158.1 8.7 %collective-permute-start.6 = (f32[1280,512]{1,0:T(8,128)S(1)}, f32[1280,512]{1,0:T(8,128)}, u32[]{:S(2)}, u32[]{:S(2)}) collective-permute-start(f32[1280,512]{1,0:T(8,128)S(1)} %dynamic-slice_bitcast_fusion), channel_id=1, source_target_pairs={{0,1},{1,0},{2,3},{3,2},{4,5},{5,4},{6,7},{7,6},{8,9},{9,8},{10,11... | collective-permute-start | bytes 7864328 | tf_op jit(solution)/shard_map/ppermute | solution.py:252
  171.8 11.7 %collective-permute-start.15 = (f32[192,512]{1,0:T(8,128)}, f32[192,512]{1,0:T(8,128)}, u32[]{:S(2)}, u32[]{:S(2)}) collective-permute-start(f32[192,512]{1,0:T(8,128)} %dynamic-slice_bitcast_fusion.3), channel_id=1, source_target_pairs={{0,4},{1,5},{2,6},{3,7},{4,0},{5,1},{6,2},{7,3},{8,12},{9,13},{10,... | collective-permute-start | bytes 1179656 | tf_op jit(solution)/shard_map/ppermute | solution.py:252
  172.2 14.8 %collective-permute-start.23 = (f32[192,512]{1,0:T(8,128)S(1)}, f32[192,512]{1,0:T(8,128)S(1)}, u32[]{:S(2)}, u32[]{:S(2)}) collective-permute-start(f32[192,512]{1,0:T(8,128)S(1)} %dynamic-slice_bitcast_fusion.2), channel_id=1, source_target_pairs={{0,8},{8,0},{16,24},{24,16},{1,9},{9,1},{17,25},{25,17},{2,10},{10... | collective-permute-start | bytes 1179656 | tf_op jit(solution)/shard_map/ppermute | solution.py:252
  174.7 13.7 %collective-permute-start.7 = (f32[256,512]{1,0:T(8,128)S(1)}, f32[256,512]{1,0:T(8,128)S(1)}, u32[]{:S(2)}, u32[]{:S(2)}) collective-permute-start(f32[256,512]{1,0:T(8,128)S(1)} %dynamic-slice_bitcast_fusion.1), channel_id=1, source_target_pairs={{0,2},{1,3},{2,0},{3,1},{4,6},{5,7},{6,4},{7,5},{8,10},{9,11},{10,... | collective-permute-start | bytes 1572872 | tf_op jit(solution)/shard_map/ppermute | solution.py:252
  184.6 9.2 %collective-permute-start.16 = (f32[96,512]{1,0:T(8,128)S(1)}, f32[96,512]{1,0:T(8,128)S(1)}, u32[]{:S(2)}, u32[]{:S(2)}) collective-permute-start(f32[96,512]{1,0:T(8,128)S(1)} %dynamic-slice_bitcast_fusion.6), channel_id=1, source_target_pairs={{0,8},{8,0},{16,24},{24,16},{1,9},{9,1},{17,25},{25,17},{2,10},{10... | collective-permute-start | bytes 589832 | tf_op jit(solution)/shard_map/ppermute | solution.py:252
  187.1 14.4 %collective-permute-start.24 = (f32[96,512]{1,0:T(8,128)S(1)}, f32[96,512]{1,0:T(8,128)S(1)}, u32[]{:S(2)}, u32[]{:S(2)}) collective-permute-start(f32[96,512]{1,0:T(8,128)S(1)} %dynamic-slice_bitcast_fusion.5), channel_id=1, source_target_pairs={{0,16},{8,24},{16,0},{24,8},{1,17},{9,25},{17,1},{25,9},{2,18},{10... | collective-permute-start | bytes 589832 | tf_op jit(solution)/shard_map/ppermute | solution.py:252
  188.5 19.6 %collective-permute-start.8 = (f32[128,512]{1,0:T(8,128)S(1)}, f32[128,512]{1,0:T(8,128)S(1)}, u32[]{:S(2)}, u32[]{:S(2)}) collective-permute-start(f32[128,512]{1,0:T(8,128)S(1)} %dynamic-slice_bitcast_fusion.4), channel_id=1, source_target_pairs={{0,4},{1,5},{2,6},{3,7},{4,0},{5,1},{6,2},{7,3},{8,12},{9,13},{10,... | collective-permute-start | bytes 786440 | tf_op jit(solution)/shard_map/ppermute | solution.py:252
  193.8 9.0 %collective-permute-start.17 = (f32[48,512]{1,0:T(8,128)S(1)}, f32[48,512]{1,0:T(8,128)S(1)}, u32[]{:S(2)}, u32[]{:S(2)}) collective-permute-start(f32[48,512]{1,0:T(8,128)S(1)} %dynamic-slice_bitcast_fusion.9), channel_id=1, source_target_pairs={{0,16},{8,24},{16,0},{24,8},{1,17},{9,25},{17,1},{25,9},{2,18},{10... | collective-permute-start | bytes 294920 | tf_op jit(solution)/shard_map/ppermute | solution.py:252
  201.5 4.7 %collective-permute-start.25 = (f32[48,512]{1,0:T(8,128)S(1)}, f32[48,512]{1,0:T(8,128)S(1)}, u32[]{:S(2)}, u32[]{:S(2)}) collective-permute-start(f32[48,512]{1,0:T(8,128)S(1)} %dynamic-slice_bitcast_fusion.8), channel_id=1, source_target_pairs={{0,2},{1,3},{2,0},{3,1},{4,6},{5,7},{6,4},{7,5},{8,10},{9,11},{10,... | collective-permute-start | bytes 294920 | tf_op jit(solution)/shard_map/ppermute | solution.py:252
  202.8 4.2 %collective-permute-start.18 = (f32[24,512]{1,0:T(8,128)S(1)}, f32[24,512]{1,0:T(8,128)S(1)}, u32[]{:S(2)}, u32[]{:S(2)}) collective-permute-start(f32[24,512]{1,0:T(8,128)S(1)} %dynamic-slice_bitcast_fusion.12), channel_id=1, source_target_pairs={{0,2},{1,3},{2,0},{3,1},{4,6},{5,7},{6,4},{7,5},{8,10},{9,11},{10,... | collective-permute-start | bytes 147464 | tf_op jit(solution)/shard_map/ppermute | solution.py:252
  206.3 4.2 %collective-permute-start.26 = (f32[24,512]{1,0:T(8,128)S(1)}, f32[24,512]{1,0:T(8,128)S(1)}, u32[]{:S(2)}, u32[]{:S(2)}) collective-permute-start(f32[24,512]{1,0:T(8,128)S(1)} %dynamic-slice_bitcast_fusion.11), channel_id=1, source_target_pairs={{0,4},{1,5},{2,6},{3,7},{4,0},{5,1},{6,2},{7,3},{8,12},{9,13},{10,... | collective-permute-start | bytes 147464 | tf_op jit(solution)/shard_map/ppermute | solution.py:252
  207.0 6.4 %collective-permute-start.19 = (f32[24,512]{1,0:T(8,128)S(1)}, f32[24,512]{1,0:T(8,128)S(1)}, u32[]{:S(2)}, u32[]{:S(2)}) collective-permute-start(f32[24,512]{1,0:T(8,128)S(1)} %bitcast_add_fusion.12), channel_id=1, source_target_pairs={{0,2},{1,3},{2,0},{3,1},{4,6},{5,7},{6,4},{7,5},{8,10},{9,11},{10,... | collective-permute-start | bytes 147464 | tf_op jit(solution)/shard_map/ppermute | solution.py:252
  208.2 5.1 %collective-permute-start.9 = (f32[64,512]{1,0:T(8,128)S(1)}, f32[64,512]{1,0:T(8,128)S(1)}, u32[]{:S(2)}, u32[]{:S(2)}) collective-permute-start(f32[64,512]{1,0:T(8,128)S(1)} %dynamic-slice_bitcast_fusion.7), channel_id=1, source_target_pairs={{0,8},{8,0},{16,24},{24,16},{1,9},{9,1},{17,25},{25,17},{2,10},{10... | collective-permute-start | bytes 393224 | tf_op jit(solution)/shard_map/ppermute | solution.py:252
  210.4 10.5 %collective-permute-start.27 = (f32[24,512]{1,0:T(8,128)S(1)}, f32[24,512]{1,0:T(8,128)S(1)}, u32[]{:S(2)}, u32[]{:S(2)}) collective-permute-start(f32[24,512]{1,0:T(8,128)S(1)} %bitcast_add_fusion.11), channel_id=1, source_target_pairs={{0,4},{1,5},{2,6},{3,7},{4,0},{5,1},{6,2},{7,3},{8,12},{9,13},{10,... | collective-permute-start | bytes 147464 | tf_op jit(solution)/shard_map/ppermute | solution.py:252
  213.3 7.5 %collective-permute-start.10 = (f32[32,512]{1,0:T(8,128)S(1)}, f32[32,512]{1,0:T(8,128)S(1)}, u32[]{:S(2)}, u32[]{:S(2)}) collective-permute-start(f32[32,512]{1,0:T(8,128)S(1)} %dynamic-slice_bitcast_fusion.10), channel_id=1, source_target_pairs={{0,16},{8,24},{16,0},{24,8},{1,17},{9,25},{17,1},{25,9},{2,18},{10... | collective-permute-start | bytes 196616 | tf_op jit(solution)/shard_map/ppermute | solution.py:252
  213.4 12.8 %collective-permute-start.20 = (f32[48,512]{1,0:T(8,128)S(1)}, f32[48,512]{1,0:T(8,128)S(1)}, u32[]{:S(2)}, u32[]{:S(2)}) collective-permute-start(f32[48,512]{1,0:T(8,128)S(1)} %maximum_select_fusion.11), channel_id=1, source_target_pairs={{0,16},{8,24},{16,0},{24,8},{1,17},{9,25},{17,1},{25,9},{2,18},{10... | collective-permute-start | bytes 294920 | tf_op jit(solution)/shard_map/ppermute | solution.py:252
  220.8 5.3 %collective-permute-start.11 = (f32[32,512]{1,0:T(8,128)S(1)}, f32[32,512]{1,0:T(8,128)S(1)}, u32[]{:S(2)}, u32[]{:S(2)}) collective-permute-start(f32[32,512]{1,0:T(8,128)S(1)} %bitcast_add_fusion.10), channel_id=1, source_target_pairs={{0,16},{8,24},{16,0},{24,8},{1,17},{9,25},{17,1},{25,9},{2,18},{10... | collective-permute-start | bytes 196616 | tf_op jit(solution)/shard_map/ppermute | solution.py:252
  220.9 7.4 %collective-permute-start.28 = (f32[48,512]{1,0:T(8,128)S(1)}, f32[48,512]{1,0:T(8,128)S(1)}, u32[]{:S(2)}, u32[]{:S(2)}) collective-permute-start(f32[48,512]{1,0:T(8,128)S(1)} %maximum_select_fusion.12), channel_id=1, source_target_pairs={{0,2},{1,3},{2,0},{3,1},{4,6},{5,7},{6,4},{7,5},{8,10},{9,11},{10,... | collective-permute-start | bytes 294920 | tf_op jit(solution)/shard_map/ppermute | solution.py:252
  226.2 6.0 %collective-permute-start.12 = (f32[64,512]{1,0:T(8,128)S(1)}, f32[64,512]{1,0:T(8,128)S(1)}, u32[]{:S(2)}, u32[]{:S(2)}) collective-permute-start(f32[64,512]{1,0:T(8,128)S(1)} %maximum_select_fusion.10), channel_id=1, source_target_pairs={{0,8},{8,0},{16,24},{24,16},{1,9},{9,1},{17,25},{25,17},{2,10},{10... | collective-permute-start | bytes 393224 | tf_op jit(solution)/shard_map/ppermute | solution.py:252
  226.3 11.4 %collective-permute-start.21 = (f32[96,512]{1,0:T(8,128)S(1)}, f32[96,512]{1,0:T(8,128)S(1)}, u32[]{:S(2)}, u32[]{:S(2)}) collective-permute-start(f32[96,512]{1,0:T(8,128)S(1)} %maximum_select_fusion.8), channel_id=1, source_target_pairs={{0,8},{8,0},{16,24},{24,16},{1,9},{9,1},{17,25},{25,17},{2,10},{10... | collective-permute-start | bytes 589832 | tf_op jit(solution)/shard_map/ppermute | solution.py:252
  228.4 10.1 %collective-permute-start.29 = (f32[96,512]{1,0:T(8,128)S(1)}, f32[96,512]{1,0:T(8,128)S(1)}, u32[]{:S(2)}, u32[]{:S(2)}) collective-permute-start(f32[96,512]{1,0:T(8,128)S(1)} %maximum_select_fusion.9), channel_id=1, source_target_pairs={{0,16},{8,24},{16,0},{24,8},{1,17},{9,25},{17,1},{25,9},{2,18},{10... | collective-permute-start | bytes 589832 | tf_op jit(solution)/shard_map/ppermute | solution.py:252
  232.2 6.4 %collective-permute-start.13 = (f32[128,512]{1,0:T(8,128)S(1)}, f32[128,512]{1,0:T(8,128)S(1)}, u32[]{:S(2)}, u32[]{:S(2)}) collective-permute-start(f32[128,512]{1,0:T(8,128)S(1)} %maximum_select_fusion.7), channel_id=1, source_target_pairs={{0,4},{1,5},{2,6},{3,7},{4,0},{5,1},{6,2},{7,3},{8,12},{9,13},{10,... | collective-permute-start | bytes 786440 | tf_op jit(solution)/shard_map/ppermute | solution.py:252
  237.7 7.8 %collective-permute-start.22 = (f32[192,512]{1,0:T(8,128)S(1)}, f32[192,512]{1,0:T(8,128)S(1)}, u32[]{:S(2)}, u32[]{:S(2)}) collective-permute-start(f32[192,512]{1,0:T(8,128)S(1)} %maximum_select_fusion.5), channel_id=1, source_target_pairs={{0,4},{1,5},{2,6},{3,7},{4,0},{5,1},{6,2},{7,3},{8,12},{9,13},{10,... | collective-permute-start | bytes 1179656 | tf_op jit(solution)/shard_map/ppermute | solution.py:252
  238.5 7.8 %collective-permute-start.30 = (f32[192,512]{1,0:T(8,128)S(1)}, f32[192,512]{1,0:T(8,128)S(1)}, u32[]{:S(2)}, u32[]{:S(2)}) collective-permute-start(f32[192,512]{1,0:T(8,128)S(1)} %maximum_select_fusion.6), channel_id=1, source_target_pairs={{0,8},{8,0},{16,24},{24,16},{1,9},{9,1},{17,25},{25,17},{2,10},{10... | collective-permute-start | bytes 1179656 | tf_op jit(solution)/shard_map/ppermute | solution.py:252
  238.7 9.2 %collective-permute-start.14 = (f32[256,512]{1,0:T(8,128)S(1)}, f32[256,512]{1,0:T(8,128)S(1)}, u32[]{:S(2)}, u32[]{:S(2)}) collective-permute-start(f32[256,512]{1,0:T(8,128)S(1)} %maximum_select_fusion.4), channel_id=1, source_target_pairs={{0,2},{1,3},{2,0},{3,1},{4,6},{5,7},{6,4},{7,5},{8,10},{9,11},{10,... | collective-permute-start | bytes 1572872 | tf_op jit(solution)/shard_map/ppermute | solution.py:252
  249.8 5.3 %collective-permute-start.31 = (f32[1280,512]{1,0:T(8,128)}, f32[1280,512]{1,0:T(8,128)}, u32[]{:S(2)}, u32[]{:S(2)}) collective-permute-start(f32[1280,512]{1,0:T(8,128)} %pad_maximum_fusion), channel_id=1, source_target_pairs={{0,1},{1,0},{2,3},{3,2},{4,5},{5,4},{6,7},{7,6},{8,9},{9,8},{10,11... | collective-permute-start | bytes 7864328 | tf_op jit(solution)/shard_map/ppermute | solution.py:252
  (10 other events, 78.4 us)
where the time goes:
time: 260 us
  Pallas kernels  132 us (51%)
  waiting for transfers between devices  65 us (25%)
  starting transfers between devices  39.6 us (15%)
  other arithmetic  11.4 us (4%)
  local copies, waits for them, and re-layouts  11 us (4%)
    pallas_call x1, Pallas kernels, gather_sends(): pl.pallas_call(gather_kernel, out_shape=[shape] * sides, grid_spec=pltpu....  65.5 us
    ppermute x26, waiting for transfers between devices, flip(): return lax.ppermute(value, axis, [(i, i ^ mask) for i in range(count)])  58.7 us
    pallas_call x1, Pallas kernels, project_terms(): pl.pallas_call(kernel, out_shape=jax.ShapeDtypeStruct((number, width, wid...  51.1 us
    ppermute x26, starting transfers between devices, flip(): return lax.ppermute(value, axis, [(i, i ^ mask) for i in range(count)])  29.2 us
    ppermute x4, starting transfers between devices, passed_along(): return lax.ppermute(value, axis, pairs)  7.84 us
    pallas_call x1, Pallas kernels, split_own(): pl.pallas_call(own_kernel, out_shape=[table, table, jax.ShapeDtypeStruct(...  7.51 us
    ppermute x2, waiting for transfers between devices, from_behind(): lax.ppermute(value, axis, [(source, source + steps) for source in range(l...  6.29 us
  transfers between devices with their start and end apart: 32, of which 20 were waited for; matrix products, arithmetic and copies ran while one was open for 3% of the time, Pallas kernels for 5%

commit v1 on v0

--- a/solution.py
+++ b/solution.py
@@ -57,7 +57,7 @@
             num_scalar_prefetch=1,
             grid=(),
             in_specs=[pl.BlockSpec(memory_space=pl.ANY)],
-            out_specs=[pl.BlockSpec(memory_space=pl.ANY)] * sides,
+            out_specs=[pl.BlockSpec(memory_space=pltpu.VMEM)] * sides,
             scratch_shapes=[pltpu.SemaphoreType.DMA((sides, cap))],
         ),
         name="gather_sends",
@@ -122,51 +122,84 @@
     )(*ghosts, high, low)
 
 
-def die_kernel(basis, next_row, next_col, fields, turned):
-    nx, ny, width = basis.shape
-    value = basis[...]
-    below = jnp.concatenate([value[1:], next_row[...]], axis=0)
-    right = jnp.concatenate([value[:, 1:], next_col[...]], axis=1)
-    for k, field in enumerate((value, value - below, value - right)):
-        flat = field.reshape(nx * ny, width)
-        fields[k] = flat
-        t_high, t_low = split(flat.T)
-        turned[k, :, : nx * ny] = t_high
-        turned[k, :, nx * ny :] = t_low
-
-
-def split_die(basis, next_row, next_col):
+DIE_FIELDS = ((0,), (1,), (2,), (0,), (1, 2))
+
+
+def die_kernel(basis, next_row, next_col, weights, out, fields, turned):
     nx, ny, width = basis.shape
     cells = nx * ny
+    term = pl.program_id(0)
+
+    @pl.when(term == 0)
+    def _():
+        value = basis[...]
+        below = jnp.concatenate([value[1:], next_row[...]], axis=0)
+        right = jnp.concatenate([value[:, 1:], next_col[...]], axis=1)
+        for k, field in enumerate((value, value - below, value - right)):
+            flat = field.reshape(cells, width)
+            fields[k] = flat
+            t_high, t_low = split(flat.T)
+            turned[k, :, :cells] = t_high
+            turned[k, :, cells:] = t_low
+
+    def gram(k):
+        w_high, w_low = split(weights[0] * fields[k])
+        pair = turned[k]
+        left = jnp.concatenate([pair, pair[:, :cells]], axis=1)
+        return mm(left, jnp.concatenate([w_high, w_high, w_low], axis=0))
+
+    for q, picks in enumerate(DIE_FIELDS):
+        @pl.when(term == q)
+        def _():
+            total = gram(picks[0])
+            for k in picks[1:]:
+                total += gram(k)
+            out[0] = total
+
+
+def die_parts(basis, next_row, next_col, weights):
+    nx, ny, width = basis.shape
+    cells = nx * ny
+    terms = weights.shape[0]
+
+    def whole(array):
+        return pl.BlockSpec(array.shape, lambda i: (0,) * array.ndim)
+
     return pl.pallas_call(
         die_kernel,
-        out_shape=[
-            jax.ShapeDtypeStruct((3, cells, width), F32),
-            jax.ShapeDtypeStruct((3, width, 2 * cells), BF16),
+        out_shape=jax.ShapeDtypeStruct((terms, width, width), F32),
+        grid=(terms,),
+        in_specs=[
+            whole(basis),
+            whole(next_row),
+            whole(next_col),
+            pl.BlockSpec((1, cells, 1), lambda i: (i, 0, 0)),
         ],
-        name="split_die",
-    )(basis, next_row, next_col)
-
-
-def gram(turned, weights, field):
-    cells = field.shape[0]
-    w_high, w_low = split(weights * field)
-    t_high, t_low = turned[:, :cells], turned[:, cells:]
-    return mm(t_high, w_high) + mm(t_low, w_high) + mm(t_high, w_low)
+        out_specs=pl.BlockSpec((1, width, width), lambda i: (i, 0, 0)),
+        scratch_shapes=[
+            pltpu.VMEM((3, cells, width), F32),
+            pltpu.VMEM((3, width, 2 * cells), BF16),
+        ],
+        cost_estimate=pl.CostEstimate(
+            flops=36 * cells * width * width, transcendentals=0, bytes_accessed=8 * terms * width * width
+        ),
+        name="die_parts",
+    )(basis, next_row, next_col, weights)
 
 
 def term_kernel(
-    columns, counts, fields, die_turned, weights, turned, high, low, blocks, out,
-    image_high, image_low, *, first, picks,
+    columns, counts, core, die, turned, high, low, blocks, keep, send,
+    total, image_high, image_low, *, first,
 ):
     term = first + pl.program_id(0)
+    mine = core[0]
     count = blocks.shape[1]
     block, wide = blocks.shape[2:]
     entries = wide // block
     groups = turned.shape[0]
     per = count // groups
     depth = per * block
-    width = out.shape[2]
+    half = keep.shape[1]
     lane = lax.broadcasted_iota(jnp.int32, (block, wide), 1)
 
     def image_rows(group, slot):
@@ -189,62 +222,97 @@
         pair = turned[group]
         left = jnp.concatenate([pair, pair[:, :depth]], axis=1)
         right = jnp.concatenate([top, top, rest], axis=0)
-        out[0] += mm(left, right)
+        return mm(left, right).reshape(total.shape)
 
     image_rows(0, 0)
-    for which, (q, die) in enumerate(picks):
-        @pl.when(term == q)
-        def _():
-            total = gram(die_turned[die[0]], weights[0], fields[die[0]])
-            for k in die[1:]:
-                total += gram(die_turned[k], weights[0], fields[k])
-            out[0] = total
+    total[...] = die[0].reshape(total.shape)
 
     def step(group, carry):
-        project(group - 1, (group - 1) % 2)
+        total[...] += project(group - 1, (group - 1) % 2)
         image_rows(group, group % 2)
         return carry
 
     lax.fori_loop(1, groups, step, 0)
-    project(groups - 1, (groups - 1) % 2)
-
-
-DIE_FIELDS = ((0,), (1,), (2,), (0,), (1, 2))
-
-
-def project_terms(first, number, columns, counts, fields, die_turned, weights, turned, high, low, blocks):
+    total[...] += project(groups - 1, (groups - 1) % 2)
+    keep[0] = total[mine]
+    send[0] = total[1 - mine]
+
+
+def project_terms(first, number, columns, counts, core, die, turned, high, low, blocks):
     terms, count, block, wide = blocks.shape
     width = high.shape[2]
     depth = turned.shape[2] // 2
-    picks = tuple((q, DIE_FIELDS[q]) for q in range(first, first + number))
+    half = width // 2
 
     def whole(array):
         return pl.BlockSpec(array.shape, lambda i, *_: (0,) * array.ndim, pipeline_mode=pl.Buffered(1))
 
     def kernel(*refs):
-        term_kernel(*refs, first=first, picks=picks)
-
+        term_kernel(*refs, first=first)
+
+    out = jax.ShapeDtypeStruct((number, half, width), F32)
+    out_spec = pl.BlockSpec((1, half, width), lambda i, *_: (i, 0, 0))
     return pl.pallas_call(
         kernel,
-        out_shape=jax.ShapeDtypeStruct((number, width, width), F32),
+        out_shape=[out, out],
         grid_spec=pltpu.PrefetchScalarGridSpec(
-            num_scalar_prefetch=2,
+            num_scalar_prefetch=3,
             grid=(number,),
             in_specs=[
-                whole(fields),
-                whole(die_turned),
-                pl.BlockSpec((1,) + weights.shape[1:], lambda i, *_: (first + i, 0, 0)),
+                pl.BlockSpec((1, width, width), lambda i, *_: (first + i, 0, 0)),
                 whole(turned),
                 whole(high),
                 whole(low),
                 pl.BlockSpec((1, count, block, wide), lambda i, *_: (first + i, 0, 0, 0)),
             ],
-            out_specs=pl.BlockSpec((1, width, width), lambda i, *_: (i, 0, 0)),
-            scratch_shapes=[pltpu.VMEM((2, depth, width), BF16)] * 2,
+            out_specs=[out_spec, out_spec],
+            scratch_shapes=[
+                pltpu.VMEM((2, half, width), F32),
+                pltpu.VMEM((2, depth, width), BF16),
+                pltpu.VMEM((2, depth, width), BF16),
+            ],
         ),
-        compiler_params=pltpu.CompilerParams(vmem_limit_bytes=60 << 20),
+        compiler_params=pltpu.CompilerParams(vmem_limit_bytes=40 << 20),
+        cost_estimate=pl.CostEstimate(
+            flops=8 * number * count * block * width * (wide + width),
+            transcendentals=0,
+            bytes_accessed=4 * number * (count * block * wide + 2 * width * width),
+        ),
         name=f"terms_{first}_{number}",
-    )(columns, counts, fields, die_turned, weights, turned, high, low, blocks)
+    )(columns, counts, core, die, turned, high, low, blocks)
+
+
+def place_kernel(core, mine, other, *refs):
+    out = refs[-1]
+    half = mine.shape[1]
+
+    @pl.when(core[0] == 0)
+    def _():
+        out[0, :half] = mine[0]
+        out[0, half:] = other[0]
+
+    @pl.when(core[0] == 1)
+    def _():
+        out[0, :half] = other[0]
+        out[0, half:] = mine[0]
+
+
+def place(core, mine, other, first, terms, filled):
+    number, half, width = mine.shape
+    spec = pl.BlockSpec((1, half, width), lambda i, *_: (i, 0, 0))
+    extra = [] if filled is None else [filled]
+    return pl.pallas_call(
+        place_kernel,
+        out_shape=jax.ShapeDtypeStruct((terms, 2 * half, width), F32),
+        grid_spec=pltpu.PrefetchScalarGridSpec(
+            num_scalar_prefetch=1,
+            grid=(number,),
+            in_specs=[spec, spec] + [pl.BlockSpec(memory_space=pl.ANY)] * len(extra),
+            out_specs=pl.BlockSpec((1, 2 * half, width), lambda i, *_: (first + i, 0, 0)),
+        ),
+        input_output_aliases={3: 0} if extra else {},
+        name=f"place_{first}",
+    )(core, mine, other, *extra)
 
 
 def flip(value, axis, mask):
@@ -256,13 +324,20 @@
     return (lax.axis_index(axis) // mask) % 2
 
 
-def halve(value, dim):
+def halve(pair, dim):
     axis, mask = dim
     mine = side(axis, mask)
-    halves = value.reshape((2, value.shape[0] // 2) + value.shape[1:])
-    send = lax.dynamic_index_in_dim(halves, 1 - mine, 0, keepdims=False)
-    keep = lax.dynamic_index_in_dim(halves, mine, 0, keepdims=False)
-    return keep + flip(send, axis, mask)
+
+    def half_of(which):
+        picked = [
+            lax.dynamic_index_in_dim(
+                part.reshape((2, part.shape[0] // 2) + part.shape[1:]), which, 0, keepdims=False
+            )
+            for part in pair
+        ]
+        return picked[0] + picked[1]
+
+    return half_of(mine), flip(half_of(1 - mine), axis, mask)
 
 
 def double(value, dim):
@@ -278,27 +353,20 @@
     return [(axis, 1 << k) for k in range(count.bit_length() - 1)]
 
 
-def total_of(terms):
-    flat = terms.reshape(-1, terms.shape[-1])
-    core, *plane = masks("gy")
-    line = masks("gx")
-    orders = [plane + line, plane[1:] + line + plane[:1], line + plane]
-    flat = halve(flat, core)
-    rows = flat.shape[0]
-    unit = 8 << len(plane + line)
-    if rows % unit or rows // unit < 3:
-        orders, sizes = orders[:1], [rows]
-    else:
-        each = rows // unit // 3
-        sizes = [rows - 2 * each * unit, each * unit, each * unit]
-    starts = [sum(sizes[:k]) for k in range(len(sizes))]
-    parts = [lax.slice_in_dim(flat, a, a + n) for a, n in zip(starts, sizes)]
-    stages = len(plane + line)
-    for k in range(stages):
-        parts = [halve(p, o[k]) for p, o in zip(parts, orders)]
-    for k in reversed(range(stages)):
-        parts = [double(p, o[k]) for p, o in zip(parts, orders)]
-    return double(jnp.concatenate(parts, axis=0), core).reshape(terms.shape)
+def chunk_sizes(terms):
+    base, extra = divmod(terms, 3)
+    return [n for n in (base + (k < extra) for k in range(3)) if n]
+
+
+def summed(keep, received, order):
+    shape = keep.shape
+    pair = (keep.reshape(-1, shape[-1]), received.reshape(-1, shape[-1]))
+    for dim in order:
+        pair = halve(pair, dim)
+    value = pair[0] + pair[1]
+    for dim in reversed(order):
+        value = double(value, dim)
+    return value.reshape(shape)
 
 
 def body(die_basis, die_coeff, pkg_basis, send_blocks, columns, counts, pkg_blocks):
@@ -315,14 +383,25 @@
     count = pkg_basis.shape[0]
     terms = columns.shape[0]
     high, low, turned = split_own(pkg_basis, count + lists.shape[0] * lists.shape[1])
-    fields, die_turned = split_die(die_basis, next_x_row, next_y_col)
+    weights = die_coeff.reshape(terms, -1, 1)
+    die = die_parts(die_basis, next_x_row, next_y_col, weights)
     high, low = split_ghosts(ghosts, high, low, count)
-    weights = die_coeff.reshape(terms, -1, 1)
     columns = columns.reshape(terms, -1)
-    parts = project_terms(
-        0, terms, columns, counts, fields, die_turned, weights, turned, high, low, pkg_blocks
-    )
-    return total_of(parts)
+    (axis, mask), *plane = masks("gy")
+    line = masks("gx")
+    core = side(axis, mask).astype(jnp.int32).reshape(1)
+    orders = [plane + line, plane[1:] + line + plane[:1], line + plane]
+    reduced = None
+    first = 0
+    for number, order in zip(chunk_sizes(terms), orders):
+        keep, send = project_terms(
+            first, number, columns, counts, core, die, turned, high, low, pkg_blocks
+        )
+        mine = summed(keep, flip(send, axis, mask), order)
+        other = flip(mine, axis, mask)
+        reduced = place(core, mine, other, first, terms, reduced)
+        first += number
+    return reduced
 
 
 def solution(mesh):

time: 260 us -> 206 us (0.79)
  Pallas kernels: 132 us -> 78.9 us
  starting transfers between devices: 39.6 us -> 31.9 us
  local copies, waits for them, and re-layouts: 11 us -> 18.2 us
  other arithmetic: 11.4 us -> 4.57 us
  waiting for transfers between devices: 65 us -> 71.1 us
    pallas_call x1, Pallas kernels: 65.5 us -> 3.92 us  [gather_sends(): pl.pallas_call(gather_kernel, out_shape=[shape] * sides, grid_spec=pltpu....]
    unnamed x21 -> x47, local copies, waits for them, and re-layouts: 2.89 us -> 13.8 us
    pallas_call x2 -> x7, Pallas kernels: 55.9 us -> 64 us  [the longest x3 47.4 us: project_terms(): pl.pallas_call(kernel, out_shape=[out, out], grid_spec=pltpu.PrefetchScal...]
    ppermute x26 -> x30, starting transfers between devices: 29.2 us -> 21.3 us  [flip(): return lax.ppermute(value, axis, [(i, i ^ mask) for i in range(count)])]
    select_n x13 -> x12, other arithmetic: 5.15 us -> 0.43 us  [double(): return jnp.where(side(axis, mask) == 0, low, high)]
    ppermute x2, waiting for transfers between devices: 6.29 us -> 10.2 us  [from_behind(): lax.ppermute(value, axis, [(source, source + steps) for source in range(l...]
    squeeze x13 -> x0, local copies, waits for them, and re-layouts: 2.99 us -> none  [halve(): send = lax.dynamic_index_in_dim(halves, 1 - mine, 0, keepdims=False)]
    ppermute x26 -> x30, waiting for transfers between devices: 58.7 us -> 60.9 us  [flip(): return lax.ppermute(value, axis, [(i, i ^ mask) for i in range(count)])]
  transfers between devices with their start and end apart: 32 -> 36, of which waited for: 20 -> 18; matrix products, arithmetic and copies ran while one was open for 3% -> 4% of each run, Pallas kernels for 5% -> 27%
where the time goes in v1:
time: 206 us; the launch traced here: 205 us
  Pallas kernels  78.9 us (38%)
  waiting for transfers between devices  71.1 us (35%)
  starting transfers between devices  31.9 us (15%)
  local copies, waits for them, and re-layouts  18.2 us (9%)
  other arithmetic  4.57 us (2%)
    ppermute x30, waiting for transfers between devices, flip(): return lax.ppermute(value, axis, [(i, i ^ mask) for i in range(count)])  60.9 us
    pallas_call x3, Pallas kernels, project_terms(): pl.pallas_call(kernel, out_shape=[out, out], grid_spec=pltpu.PrefetchScal...  47.4 us
    ppermute x30, starting transfers between devices, flip(): return lax.ppermute(value, axis, [(i, i ^ mask) for i in range(count)])  21.3 us
    unnamed x47, local copies, waits for them, and re-layouts  13.8 us
    ppermute x2, waiting for transfers between devices, from_behind(): lax.ppermute(value, axis, [(source, source + steps) for source in range(l...  10.2 us
    pallas_call x1, Pallas kernels, die_parts(): pl.pallas_call(die_kernel, out_shape=jax.ShapeDtypeStruct((terms, width,...  9 us
    ppermute x4, starting transfers between devices, passed_along(): return lax.ppermute(value, axis, pairs)  8.09 us
    pallas_call x3, Pallas kernels, place(): pl.pallas_call(place_kernel, out_shape=jax.ShapeDtypeStruct((terms, 2 * h...  7.53 us
  transfers between devices with their start and end apart: 36, of which 18 were waited for; matrix products, arithmetic and copies ran while one was open for 4% of the time, Pallas kernels for 27%

profile of v1, /device:TPU:0, one launch (start us, length us, event | category | flops | bytes accessed | tf_op | source)
XLA Modules:
  0.0 205.1 jit_solution(1097836754360953789)
XLA Ops:
  2.3 3.9 %gather_sends.1 = (f32[4,64,512]{2,1,0:T(8,128)}, f32[4,64,512]{2,1,0:T(8,128)}, f32[4,64,512]{2,1,0:T(8,128)}, f32[4,64,512]{2,1,0:T(8,128)}) custom-call(s32[4,4]{1,0:T(4,128)} %bitcast.88, f32[32,64,512]{2,1,0:T(8,128)} %table.1), custom_call_target="tpu_custom_call" | custom-call | tf_op jit(solution)/shard_map/gather_sends/pallas_call | solution.py:53
  6.2 3.1 %collective-permute-start.2 = (f32[4,64,512]{2,1,0:T(8,128)}, f32[4,64,512]{2,1,0:T(8,128)S(1)}, u32[]{:S(2)}, u32[]{:S(2)}) collective-permute-start(f32[4,64,512]{2,1,0:T(8,128)} %get-tuple-element.21), channel_id=1, source_target_pairs={{0,8},{8,16},{16,24},{24,0},{1,9},{9,17},{17,25},{25,1},{2,10},{10... | collective-permute-start | bytes 1572872 | tf_op jit(solution)/shard_map/ppermute | solution.py:22
  9.3 2.1 %collective-permute-start.3 = (f32[4,64,512]{2,1,0:T(8,128)}, f32[4,64,512]{2,1,0:T(8,128)S(1)}, u32[]{:S(2)}, u32[]{:S(2)}) collective-permute-start(f32[4,64,512]{2,1,0:T(8,128)} %get-tuple-element.22), channel_id=1, source_target_pairs={{0,24},{8,0},{16,8},{24,16},{1,25},{9,1},{17,9},{25,17},{2,26},{10... | collective-permute-start | bytes 1572872 | tf_op jit(solution)/shard_map/ppermute | solution.py:22
  12.3 2.1 %collective-permute-start.5 = (f32[4,64,512]{2,1,0:T(8,128)}, f32[4,64,512]{2,1,0:T(8,128)S(1)}, u32[]{:S(2)}, u32[]{:S(2)}) collective-permute-start(f32[4,64,512]{2,1,0:T(8,128)} %get-tuple-element.24), channel_id=1, source_target_pairs={{0,7},{1,0},{2,1},{3,2},{4,3},{5,4},{6,5},{7,6},{8,15},{9,8},{10,9... | collective-permute-start | bytes 1572872 | tf_op jit(solution)/shard_map/ppermute | solution.py:22
  16.5 7.5 %split_own.1 = (bf16[48,64,512]{2,1,0:T(8,128)(2,1)}, bf16[48,64,512]{2,1,0:T(8,128)(2,1)}, bf16[8,512,512]{2,1,0:T(8,128)(2,1)}) custom-call(f32[32,64,512]{2,1,0:T(8,128)} %table.1), custom_call_target="tpu_custom_call" | custom-call | tf_op jit(solution)/shard_map/split_own/pallas_call | solution.py:85
  24.2 2.4 %reshape.231.weights = f32[5,512,1]{2,1,0:T(8,128)} reshape(f32[5,16,32]{2,1,0:T(8,128)S(1)} %copy-done.19) | data formatting | bytes 20480 | tf_op jit(solution)/shard_map/reshape | solution.py:386
  26.7 10.2 %collective-permute-done.next_row = f32[1,32,512]{2,1,0:T(8,128)S(1)} collective-permute-done((f32[1,32,512]{2,1,0:T(8,128)S(1)}, f32[1,32,512]{2,1,0:T(8,128)S(1)}, u32[]{:S(2)}, u32[]{:S(2)}) %collective-permute-start) | collective-permute-done | bytes 65568 | tf_op jit(solution)/shard_map/ppermute | solution.py:16
  37.5 9.0 %die_parts.1.refs_3_ = f32[5,512,512]{2,1,0:T(8,128)} custom-call(f32[16,32,512]{2,1,0:T(8,128)} %basis.1, f32[1,32,512]{2,1,0:T(8,128)} %copy-done.21, f32[16,1,512]{2,1,0:T(1,128)} %copy-done.22, f32[5,512,1]{2,1,0:T(8,128)} %reshape.231.weights), custom_call_target="tpu_custom_call" | custom-call | flops 4831838208 | bytes 10485760 | tf_op jit(solution)/shard_map/die_parts/pallas_call | solution.py:168
  47.9 3.5 %split_ghosts.1 = (bf16[48,64,512]{2,1,0:T(8,128)(2,1)}, bf16[48,64,512]{2,1,0:T(8,128)(2,1)}) custom-call(f32[4,64,512]{2,1,0:T(8,128)} %copy-done.14, f32[4,64,512]{2,1,0:T(8,128)} %copy-done.15, f32[4,64,512]{2,1,0:T(8,128)} %copy-done.16, f32[4,64,512]{2,1,0:T(8,128)} %copy-done.17, ...), custom_call_target="tpu_custom_call", output_to_operand_aliasing={{0}: (4, {}), {1}: (5, {})} | custom-call | tf_op jit(solution)/shard_map/split_ghosts/pallas_call | solution.py:114
  55.2 2.2 %copy-done.4 = bf16[8,512,512]{2,1,0:T(8,128)(2,1)S(1)} copy-done((bf16[8,512,512]{2,1,0:T(8,128)(2,1)S(1)}, bf16[8,512,512]{2,1,0:T(8,128)(2,1)}, u32[]{:S(2)}) %copy-start.4) | copy-done | bytes 4194328
  57.3 18.2 %terms_2_2.1 = (f32[2,256,512]{2,1,0:T(8,128)S(1)}, f32[2,256,512]{2,1,0:T(8,128)}) custom-call(s32[5,128]{1,0:T(8,128)S(1)} %reshape.220.refs_0_, s32[5,32]{1,0:T(8,128)S(1)} %copy-done.10, s32[1]{0:T(128)} %bitcast.refs_2_.core, f32[5,512,512]{2,1,0:T(8,128)} %die_parts.1.refs_3_, bf16[8,512,512]{2,1,0:T(8,128)(2,1)S(1)} %copy-done.4, ...), custom_call_target="tpu_custom_call" | custom-call | flops 12884901888 | bytes 8388608 | tf_op jit(solution)/shard_map/terms_2_2/pallas_call | solution.py:255
  76.6 18.2 %terms_0_2.1 = (f32[2,256,512]{2,1,0:T(8,128)S(1)}, f32[2,256,512]{2,1,0:T(8,128)}) custom-call(s32[5,128]{1,0:T(8,128)S(1)} %reshape.220.refs_0_, s32[5,32]{1,0:T(8,128)S(1)} %copy-done.10, s32[1]{0:T(128)} %bitcast.refs_2_.core, f32[5,512,512]{2,1,0:T(8,128)} %die_parts.1.refs_3_, bf16[8,512,512]{2,1,0:T(8,128)(2,1)S(1)} %copy-done.4, ...), custom_call_target="tpu_custom_call" | custom-call | flops 12884901888 | bytes 8388608 | tf_op jit(solution)/shard_map/terms_0_2/pallas_call | solution.py:255
  96.3 2.0 dynamic-slice_add_fusion.1
  103.1 2.2 %copy-done.5 = bf16[8,512,512]{2,1,0:T(8,128)(2,1)S(1)} copy-done((bf16[8,512,512]{2,1,0:T(8,128)(2,1)S(1)}, bf16[8,512,512]{2,1,0:T(8,128)(2,1)}, u32[]{:S(2)}) %copy-start.5) | copy-done | bytes 4194328
  105.3 11.0 %terms_4_1.1 = (f32[1,256,512]{2,1,0:T(8,128)S(1)}, f32[1,256,512]{2,1,0:T(8,128)}) custom-call(s32[5,128]{1,0:T(8,128)S(1)} %reshape.220.refs_0_, s32[5,32]{1,0:T(8,128)S(1)} %copy-done.10, s32[1]{0:T(128)} %bitcast.refs_2_.core, f32[5,512,512]{2,1,0:T(8,128)} %die_parts.1.refs_3_, bf16[8,512,512]{2,1,0:T(8,128)(2,1)S(1)} %copy-done.5, ...), custom_call_target="tpu_custom_call" | custom-call | flops 6442450944 | bytes 4194304 | tf_op jit(solution)/shard_map/terms_4_1/pallas_call | solution.py:255
  119.2 6.8 %collective-permute-done.18 = f32[128,512]{1,0:T(8,128)S(1)} collective-permute-done((f32[128,512]{1,0:T(8,128)S(1)}, f32[128,512]{1,0:T(8,128)S(1)}, u32[]{:S(2)}, u32[]{:S(2)}) %collective-permute-start.18) | collective-permute-done | bytes 262176 | tf_op jit(solution)/shard_map/ppermute | solution.py:320
  129.5 5.4 %collective-permute-done.19 = f32[64,512]{1,0:T(8,128)S(1)} collective-permute-done((f32[64,512]{1,0:T(8,128)S(1)}, f32[64,512]{1,0:T(8,128)S(1)}, u32[]{:S(2)}, u32[]{:S(2)}) %collective-permute-start.19) | collective-permute-done | bytes 131104 | tf_op jit(solution)/shard_map/ppermute | solution.py:320
  137.3 1.9 collective-permute-done.20
  144.7 2.0 collective-permute-start.8
  146.7 5.5 %collective-permute-done.31 = f32[32,512]{1,0:T(8,128)S(1)} collective-permute-done((f32[32,512]{1,0:T(8,128)S(1)}, f32[32,512]{1,0:T(8,128)S(1)}, u32[]{:S(2)}, u32[]{:S(2)}) %collective-permute-start.31) | collective-permute-done | bytes 65568 | tf_op jit(solution)/shard_map/ppermute | solution.py:320
  152.3 3.6 %collective-permute-done.22 = f32[64,512]{1,0:T(8,128)S(1)} collective-permute-done((f32[64,512]{1,0:T(8,128)S(1)}, f32[64,512]{1,0:T(8,128)S(1)}, u32[]{:S(2)}, u32[]{:S(2)}) %collective-permute-start.22) | collective-permute-done | bytes 131104 | tf_op jit(solution)/shard_map/ppermute | solution.py:320
  156.0 2.0 collective-permute-done.8
  158.6 2.0 collective-permute-done.32
  162.8 2.1 %collective-permute-done.23 = f32[128,512]{1,0:T(8,128)S(1)} collective-permute-done((f32[128,512]{1,0:T(8,128)S(1)}, f32[128,512]{1,0:T(8,128)S(1)}, u32[]{:S(2)}, u32[]{:S(2)}) %collective-permute-start.23) | collective-permute-done | bytes 262176 | tf_op jit(solution)/shard_map/ppermute | solution.py:320
  165.5 2.2 %collective-permute-done.33 = f32[128,512]{1,0:T(8,128)S(1)} collective-permute-done((f32[128,512]{1,0:T(8,128)S(1)}, f32[128,512]{1,0:T(8,128)S(1)}, u32[]{:S(2)}, u32[]{:S(2)}) %collective-permute-start.33) | collective-permute-done | bytes 262176 | tf_op jit(solution)/shard_map/ppermute | solution.py:320
  169.0 10.3 %collective-permute-done.11 = f32[16,512]{1,0:T(8,128)S(1)} collective-permute-done((f32[16,512]{1,0:T(8,128)S(1)}, f32[16,512]{1,0:T(8,128)S(1)}, u32[]{:S(2)}, u32[]{:S(2)}) %collective-permute-start.11) | collective-permute-done | bytes 32800 | tf_op jit(solution)/shard_map/ppermute | solution.py:320
  180.1 3.6 %collective-permute-done.12 = f32[32,512]{1,0:T(8,128)S(1)} collective-permute-done((f32[32,512]{1,0:T(8,128)S(1)}, f32[32,512]{1,0:T(8,128)S(1)}, u32[]{:S(2)}, u32[]{:S(2)}) %collective-permute-start.12) | collective-permute-done | bytes 65568 | tf_op jit(solution)/shard_map/ppermute | solution.py:320
  184.7 5.4 %collective-permute-done.13 = f32[64,512]{1,0:T(8,128)S(1)} collective-permute-done((f32[64,512]{1,0:T(8,128)S(1)}, f32[64,512]{1,0:T(8,128)S(1)}, u32[]{:S(2)}, u32[]{:S(2)}) %collective-permute-start.13) | collective-permute-done | bytes 131104 | tf_op jit(solution)/shard_map/ppermute | solution.py:320
  190.2 6.4 %collective-permute-done.14 = f32[128,512]{1,0:T(8,128)S(1)} collective-permute-done((f32[128,512]{1,0:T(8,128)S(1)}, f32[128,512]{1,0:T(8,128)S(1)}, u32[]{:S(2)}, u32[]{:S(2)}) %collective-permute-start.14) | collective-permute-done | bytes 262176 | tf_op jit(solution)/shard_map/ppermute | solution.py:320
  196.7 2.7 %place_0.1.refs_0_ = f32[5,512,512]{2,1,0:T(8,128)} custom-call(s32[1]{0:T(128)} %bitcast.refs_2_.core, f32[2,256,512]{2,1,0:T(8,128)} %bitcast.60, f32[2,256,512]{2,1,0:T(8,128)} %collective-permute-done.35.other), custom_call_target="tpu_custom_call" | custom-call | tf_op jit(solution)/shard_map/place_0/pallas_call | solution.py:304
  199.4 2.6 %place_2.1.refs_0_ = f32[5,512,512]{2,1,0:T(8,128)} custom-call(s32[1]{0:T(128)} %bitcast.refs_2_.core, f32[2,256,512]{2,1,0:T(8,128)} %bitcast.58, f32[2,256,512]{2,1,0:T(8,128)} %collective-permute-done.25.other, f32[5,512,512]{2,1,0:T(8,128)} %place_0.1.refs_0_), custom_call_target="tpu_custom_call", output_to_operand_aliasing={{}: (3, {})} | custom-call | tf_op jit(solution)/shard_map/place_2/pallas_call | solution.py:304
  202.8 2.2 %place_4.1 = f32[5,512,512]{2,1,0:T(8,128)} custom-call(s32[1]{0:T(128)} %bitcast.refs_2_.core, f32[1,256,512]{2,1,0:T(8,128)} %copy-done.13, f32[1,256,512]{2,1,0:T(8,128)} %copy-done.18, f32[5,512,512]{2,1,0:T(8,128)} %place_2.1.refs_0_), custom_call_target="tpu_custom_call", output_to_operand_aliasing={{}: (3, {})} | custom-call | tf_op jit(solution)/shard_map/place_4/pallas_call | solution.py:304
  (128 shorter events, 40.5 us)
Async XLA Ops:
  1.0 14.2 %collective-permute-start.1 = (f32[16,1,512]{2,1,0:T(1,128)S(1)}, f32[16,1,512]{2,1,0:T(1,128)S(1)}, u32[]{:S(2)}, u32[]{:S(2)}) collective-permute-start(f32[16,1,512]{2,1,0:T(1,128)S(1)} %slice.7), channel_id=1, source_target_pairs={{1,0},{2,1},{3,2},{4,3},{5,4},{6,5},{7,6},{9,8},{10,9},{11,10},{12... | collective-permute-start | bytes 98312 | tf_op jit(solution)/shard_map/ppermute | solution.py:16
  6.2 40.3 %collective-permute-start.2 = (f32[4,64,512]{2,1,0:T(8,128)}, f32[4,64,512]{2,1,0:T(8,128)S(1)}, u32[]{:S(2)}, u32[]{:S(2)}) collective-permute-start(f32[4,64,512]{2,1,0:T(8,128)} %get-tuple-element.21), channel_id=1, source_target_pairs={{0,8},{8,16},{16,24},{24,0},{1,9},{9,17},{17,25},{25,1},{2,10},{10... | collective-permute-start | bytes 1572872 | tf_op jit(solution)/shard_map/ppermute | solution.py:22
  9.3 37.2 %collective-permute-start.3 = (f32[4,64,512]{2,1,0:T(8,128)}, f32[4,64,512]{2,1,0:T(8,128)S(1)}, u32[]{:S(2)}, u32[]{:S(2)}) collective-permute-start(f32[4,64,512]{2,1,0:T(8,128)} %get-tuple-element.22), channel_id=1, source_target_pairs={{0,24},{8,0},{16,8},{24,16},{1,25},{9,1},{17,9},{25,17},{2,26},{10... | collective-permute-start | bytes 1572872 | tf_op jit(solution)/shard_map/ppermute | solution.py:22
  11.4 35.1 %collective-permute-start.4 = (f32[4,64,512]{2,1,0:T(8,128)}, f32[4,64,512]{2,1,0:T(8,128)S(1)}, u32[]{:S(2)}, u32[]{:S(2)}) collective-permute-start(f32[4,64,512]{2,1,0:T(8,128)} %get-tuple-element.23), channel_id=1, source_target_pairs={{0,1},{1,2},{2,3},{3,4},{4,5},{5,6},{6,7},{7,0},{8,9},{9,10},{10,1... | collective-permute-start | bytes 1572872 | tf_op jit(solution)/shard_map/ppermute | solution.py:22
  12.3 34.3 %collective-permute-start.5 = (f32[4,64,512]{2,1,0:T(8,128)}, f32[4,64,512]{2,1,0:T(8,128)S(1)}, u32[]{:S(2)}, u32[]{:S(2)}) collective-permute-start(f32[4,64,512]{2,1,0:T(8,128)} %get-tuple-element.24), channel_id=1, source_target_pairs={{0,7},{1,0},{2,1},{3,2},{4,3},{5,4},{6,5},{7,6},{8,15},{9,8},{10,9... | collective-permute-start | bytes 1572872 | tf_op jit(solution)/shard_map/ppermute | solution.py:22
  15.2 21.7 %collective-permute-start = (f32[1,32,512]{2,1,0:T(8,128)S(1)}, f32[1,32,512]{2,1,0:T(8,128)S(1)}, u32[]{:S(2)}, u32[]{:S(2)}) collective-permute-start(f32[1,32,512]{2,1,0:T(8,128)S(1)} %slice.6), channel_id=1, source_target_pairs={{8,0},{16,8},{24,16},{9,1},{17,9},{25,17},{10,2},{18,10},{26,18},{... | collective-permute-start | bytes 196616 | tf_op jit(solution)/shard_map/ppermute | solution.py:16
  76.6 19.7 %collective-permute-start.16 = (f32[2,256,512]{2,1,0:T(8,128)}, f32[2,256,512]{2,1,0:T(8,128)}, u32[]{:S(2)}, u32[]{:S(2)}) collective-permute-start(f32[2,256,512]{2,1,0:T(8,128)} %get-tuple-element.32), channel_id=1, source_target_pairs={{0,1},{1,0},{2,3},{3,2},{4,5},{5,4},{6,7},{7,6},{8,9},{9,8},{10,11... | collective-permute-start | bytes 3145736 | tf_op jit(solution)/shard_map/ppermute | solution.py:320
  98.3 18.8 %collective-permute-start.17 = (f32[256,512]{1,0:T(8,128)S(1)}, f32[256,512]{1,0:T(8,128)S(1)}, u32[]{:S(2)}, u32[]{:S(2)}) collective-permute-start(f32[256,512]{1,0:T(8,128)S(1)} %get-tuple-element.38), channel_id=1, source_target_pairs={{0,4},{1,5},{2,6},{3,7},{4,0},{5,1},{6,2},{7,3},{8,12},{9,13},{10,... | collective-permute-start | bytes 1572872 | tf_op jit(solution)/shard_map/ppermute | solution.py:320
  101.6 16.8 %collective-permute-start.27 = (f32[256,512]{1,0:T(8,128)S(1)}, f32[256,512]{1,0:T(8,128)S(1)}, u32[]{:S(2)}, u32[]{:S(2)}) collective-permute-start(f32[256,512]{1,0:T(8,128)S(1)} %get-tuple-element.36), channel_id=1, source_target_pairs={{0,2},{1,3},{2,0},{3,1},{4,6},{5,7},{6,4},{7,5},{8,10},{9,11},{10,... | collective-permute-start | bytes 1572872 | tf_op jit(solution)/shard_map/ppermute | solution.py:320
  117.1 10.9 %collective-permute-start.6 = (f32[1,256,512]{2,1,0:T(8,128)}, f32[1,256,512]{2,1,0:T(8,128)S(1)}, u32[]{:S(2)}, u32[]{:S(2)}) collective-permute-start(f32[1,256,512]{2,1,0:T(8,128)} %get-tuple-element.30), channel_id=1, source_target_pairs={{0,1},{1,0},{2,3},{3,2},{4,5},{5,4},{6,7},{7,6},{8,9},{9,8},{10,11... | collective-permute-start | bytes 1572872 | tf_op jit(solution)/shard_map/ppermute | solution.py:320
  117.2 8.8 %collective-permute-start.18 = (f32[128,512]{1,0:T(8,128)S(1)}, f32[128,512]{1,0:T(8,128)S(1)}, u32[]{:S(2)}, u32[]{:S(2)}) collective-permute-start(f32[128,512]{1,0:T(8,128)S(1)} %get-tuple-element.42), channel_id=1, source_target_pairs={{0,8},{8,0},{16,24},{24,16},{1,9},{9,1},{17,25},{25,17},{2,10},{10... | collective-permute-start | bytes 786440 | tf_op jit(solution)/shard_map/ppermute | solution.py:320
  118.5 8.8 %collective-permute-start.28 = (f32[128,512]{1,0:T(8,128)S(1)}, f32[128,512]{1,0:T(8,128)S(1)}, u32[]{:S(2)}, u32[]{:S(2)}) collective-permute-start(f32[128,512]{1,0:T(8,128)S(1)} %get-tuple-element.40), channel_id=1, source_target_pairs={{0,4},{1,5},{2,6},{3,7},{4,0},{5,1},{6,2},{7,3},{8,12},{9,13},{10,... | collective-permute-start | bytes 786440 | tf_op jit(solution)/shard_map/ppermute | solution.py:320
  126.0 8.9 %collective-permute-start.19 = (f32[64,512]{1,0:T(8,128)S(1)}, f32[64,512]{1,0:T(8,128)S(1)}, u32[]{:S(2)}, u32[]{:S(2)}) collective-permute-start(f32[64,512]{1,0:T(8,128)S(1)} %get-tuple-element.48), channel_id=1, source_target_pairs={{0,16},{8,24},{16,0},{24,8},{1,17},{9,25},{17,1},{25,9},{2,18},{10... | collective-permute-start | bytes 393224 | tf_op jit(solution)/shard_map/ppermute | solution.py:320
  127.3 8.6 %collective-permute-start.29 = (f32[64,512]{1,0:T(8,128)S(1)}, f32[64,512]{1,0:T(8,128)S(1)}, u32[]{:S(2)}, u32[]{:S(2)}) collective-permute-start(f32[64,512]{1,0:T(8,128)S(1)} %get-tuple-element.46), channel_id=1, source_target_pairs={{0,8},{8,0},{16,24},{24,16},{1,9},{9,1},{17,25},{25,17},{2,10},{10... | collective-permute-start | bytes 393224 | tf_op jit(solution)/shard_map/ppermute | solution.py:320
  128.1 16.6 %collective-permute-start.7 = (f32[128,512]{1,0:T(8,128)S(1)}, f32[128,512]{1,0:T(8,128)S(1)}, u32[]{:S(2)}, u32[]{:S(2)}) collective-permute-start(f32[128,512]{1,0:T(8,128)S(1)} %get-tuple-element.44), channel_id=1, source_target_pairs={{0,8},{8,0},{16,24},{24,16},{1,9},{9,1},{17,25},{25,17},{2,10},{10... | collective-permute-start | bytes 786440 | tf_op jit(solution)/shard_map/ppermute | solution.py:320
  135.9 5.7 %collective-permute-start.30 = (f32[32,512]{1,0:T(8,128)S(1)}, f32[32,512]{1,0:T(8,128)S(1)}, u32[]{:S(2)}, u32[]{:S(2)}) collective-permute-start(f32[32,512]{1,0:T(8,128)S(1)} %add_bitcast_fusion.8), channel_id=1, source_target_pairs={{0,16},{8,24},{16,0},{24,8},{1,17},{9,25},{17,1},{25,9},{2,18},{10... | collective-permute-start | bytes 196616 | tf_op jit(solution)/shard_map/ppermute | solution.py:320
  139.3 4.3 %collective-permute-start.21 = (f32[32,512]{1,0:T(8,128)S(1)}, f32[32,512]{1,0:T(8,128)S(1)}, u32[]{:S(2)}, u32[]{:S(2)}) collective-permute-start(f32[32,512]{1,0:T(8,128)S(1)} %bitcast_add_fusion.1), channel_id=1, source_target_pairs={{0,2},{1,3},{2,0},{3,1},{4,6},{5,7},{6,4},{7,5},{8,10},{9,11},{10,... | collective-permute-start | bytes 196616 | tf_op jit(solution)/shard_map/ppermute | solution.py:320
  141.6 10.6 %collective-permute-start.31 = (f32[32,512]{1,0:T(8,128)S(1)}, f32[32,512]{1,0:T(8,128)S(1)}, u32[]{:S(2)}, u32[]{:S(2)}) collective-permute-start(f32[32,512]{1,0:T(8,128)S(1)} %bitcast_add_fusion), channel_id=1, source_target_pairs={{0,16},{8,24},{16,0},{24,8},{1,17},{9,25},{17,1},{25,9},{2,18},{10... | collective-permute-start | bytes 196616 | tf_op jit(solution)/shard_map/ppermute | solution.py:320
  143.6 12.2 %collective-permute-start.22 = (f32[64,512]{1,0:T(8,128)S(1)}, f32[64,512]{1,0:T(8,128)S(1)}, u32[]{:S(2)}, u32[]{:S(2)}) collective-permute-start(f32[64,512]{1,0:T(8,128)S(1)} %maximum_select_fusion.9), channel_id=1, source_target_pairs={{0,16},{8,24},{16,0},{24,8},{1,17},{9,25},{17,1},{25,9},{2,18},{10... | collective-permute-start | bytes 393224 | tf_op jit(solution)/shard_map/ppermute | solution.py:320
  144.7 13.3 %collective-permute-start.8 = (f32[64,512]{1,0:T(8,128)S(1)}, f32[64,512]{1,0:T(8,128)S(1)}, u32[]{:S(2)}, u32[]{:S(2)}) collective-permute-start(f32[64,512]{1,0:T(8,128)S(1)} %get-tuple-element.50), channel_id=1, source_target_pairs={{0,16},{8,24},{16,0},{24,8},{1,17},{9,25},{17,1},{25,9},{2,18},{10... | collective-permute-start | bytes 393224 | tf_op jit(solution)/shard_map/ppermute | solution.py:320
  152.2 8.4 %collective-permute-start.32 = (f32[64,512]{1,0:T(8,128)S(1)}, f32[64,512]{1,0:T(8,128)S(1)}, u32[]{:S(2)}, u32[]{:S(2)}) collective-permute-start(f32[64,512]{1,0:T(8,128)S(1)} %maximum_select_fusion.10), channel_id=1, source_target_pairs={{0,8},{8,0},{16,24},{24,16},{1,9},{9,1},{17,25},{25,17},{2,10},{10... | collective-permute-start | bytes 393224 | tf_op jit(solution)/shard_map/ppermute | solution.py:320
  155.9 9.0 %collective-permute-start.23 = (f32[128,512]{1,0:T(8,128)S(1)}, f32[128,512]{1,0:T(8,128)S(1)}, u32[]{:S(2)}, u32[]{:S(2)}) collective-permute-start(f32[128,512]{1,0:T(8,128)S(1)} %maximum_select_fusion.6), channel_id=1, source_target_pairs={{0,8},{8,0},{16,24},{24,16},{1,9},{9,1},{17,25},{25,17},{2,10},{10... | collective-permute-start | bytes 786440 | tf_op jit(solution)/shard_map/ppermute | solution.py:320
  160.6 7.1 %collective-permute-start.33 = (f32[128,512]{1,0:T(8,128)S(1)}, f32[128,512]{1,0:T(8,128)S(1)}, u32[]{:S(2)}, u32[]{:S(2)}) collective-permute-start(f32[128,512]{1,0:T(8,128)S(1)} %maximum_select_fusion.7), channel_id=1, source_target_pairs={{0,4},{1,5},{2,6},{3,7},{4,0},{5,1},{6,2},{7,3},{8,12},{9,13},{10,... | collective-permute-start | bytes 786440 | tf_op jit(solution)/shard_map/ppermute | solution.py:320
  162.3 6.2 %collective-permute-start.10 = (f32[16,512]{1,0:T(8,128)S(1)}, f32[16,512]{1,0:T(8,128)S(1)}, u32[]{:S(2)}, u32[]{:S(2)}) collective-permute-start(f32[16,512]{1,0:T(8,128)S(1)} %add_bitcast_fusion.11), channel_id=1, source_target_pairs={{0,4},{1,5},{2,6},{3,7},{4,0},{5,1},{6,2},{7,3},{8,12},{9,13},{10,... | collective-permute-start | bytes 98312 | tf_op jit(solution)/shard_map/ppermute | solution.py:320
  165.0 19.0 %collective-permute-start.24 = (f32[256,512]{1,0:T(8,128)S(1)}, f32[256,512]{1,0:T(8,128)S(1)}, u32[]{:S(2)}, u32[]{:S(2)}) collective-permute-start(f32[256,512]{1,0:T(8,128)S(1)} %maximum_select_fusion.3), channel_id=1, source_target_pairs={{0,4},{1,5},{2,6},{3,7},{4,0},{5,1},{6,2},{7,3},{8,12},{9,13},{10,... | collective-permute-start | bytes 1572872 | tf_op jit(solution)/shard_map/ppermute | solution.py:320
  167.7 16.0 %collective-permute-start.34 = (f32[256,512]{1,0:T(8,128)S(1)}, f32[256,512]{1,0:T(8,128)S(1)}, u32[]{:S(2)}, u32[]{:S(2)}) collective-permute-start(f32[256,512]{1,0:T(8,128)S(1)} %maximum_select_fusion.4), channel_id=1, source_target_pairs={{0,2},{1,3},{2,0},{3,1},{4,6},{5,7},{6,4},{7,5},{8,10},{9,11},{10,... | collective-permute-start | bytes 1572872 | tf_op jit(solution)/shard_map/ppermute | solution.py:320
  168.5 10.8 %collective-permute-start.11 = (f32[16,512]{1,0:T(8,128)S(1)}, f32[16,512]{1,0:T(8,128)S(1)}, u32[]{:S(2)}, u32[]{:S(2)}) collective-permute-start(f32[16,512]{1,0:T(8,128)S(1)} %bitcast_add_fusion.2), channel_id=1, source_target_pairs={{0,4},{1,5},{2,6},{3,7},{4,0},{5,1},{6,2},{7,3},{8,12},{9,13},{10,... | collective-permute-start | bytes 98312 | tf_op jit(solution)/shard_map/ppermute | solution.py:320
  183.7 6.4 %collective-permute-start.13 = (f32[64,512]{1,0:T(8,128)S(1)}, f32[64,512]{1,0:T(8,128)S(1)}, u32[]{:S(2)}, u32[]{:S(2)}) collective-permute-start(f32[64,512]{1,0:T(8,128)S(1)} %maximum_select_fusion.8), channel_id=1, source_target_pairs={{0,16},{8,24},{16,0},{24,8},{1,17},{9,25},{17,1},{25,9},{2,18},{10... | collective-permute-start | bytes 393224 | tf_op jit(solution)/shard_map/ppermute | solution.py:320
  183.9 12.8 %collective-permute-start.35 = (f32[2,256,512]{2,1,0:T(8,128)S(1)}, f32[2,256,512]{2,1,0:T(8,128)}, u32[]{:S(2)}, u32[]{:S(2)}) collective-permute-start(f32[2,256,512]{2,1,0:T(8,128)S(1)} %bitcast.59), channel_id=1, source_target_pairs={{0,1},{1,0},{2,3},{3,2},{4,5},{5,4},{6,7},{7,6},{8,9},{9,8},{10,11... | collective-permute-start | bytes 3145736 | tf_op jit(solution)/shard_map/ppermute | solution.py:320
  184.1 15.3 %collective-permute-start.25 = (f32[2,256,512]{2,1,0:T(8,128)S(1)}, f32[2,256,512]{2,1,0:T(8,128)}, u32[]{:S(2)}, u32[]{:S(2)}) collective-permute-start(f32[2,256,512]{2,1,0:T(8,128)S(1)} %bitcast.57), channel_id=1, source_target_pairs={{0,1},{1,0},{2,3},{3,2},{4,5},{5,4},{6,7},{7,6},{8,9},{9,8},{10,11... | collective-permute-start | bytes 3145736 | tf_op jit(solution)/shard_map/ppermute | solution.py:320
  190.1 6.4 %collective-permute-start.14 = (f32[128,512]{1,0:T(8,128)S(1)}, f32[128,512]{1,0:T(8,128)S(1)}, u32[]{:S(2)}, u32[]{:S(2)}) collective-permute-start(f32[128,512]{1,0:T(8,128)S(1)} %maximum_select_fusion.5), channel_id=1, source_target_pairs={{0,8},{8,0},{16,24},{24,16},{1,9},{9,1},{17,25},{25,17},{2,10},{10... | collective-permute-start | bytes 786440 | tf_op jit(solution)/shard_map/ppermute | solution.py:320
  196.6 5.4 %collective-permute-start.15 = (f32[1,256,512]{2,1,0:T(8,128)S(1)}, f32[1,256,512]{2,1,0:T(8,128)S(1)}, u32[]{:S(2)}, u32[]{:S(2)}) collective-permute-start(f32[1,256,512]{2,1,0:T(8,128)S(1)} %maximum_select_fusion.2.mine), channel_id=1, source_target_pairs={{0,1},{1,0},{2,3},{3,2},{4,5},{5,4},{6,7},{7,6},{8,9},{9,8},{10,11... | collective-permute-start | bytes 1572872 | tf_op jit(solution)/shard_map/ppermute | solution.py:320
  (27 other events, 161.2 us)

commit v2 on v1

--- a/solution.py
+++ b/solution.py
@@ -5,6 +5,7 @@
 from jax.experimental.pallas import tpu as pltpu
 from jax.sharding import PartitionSpec as P
 
+
 ROWS = 4
 BF16 = jnp.bfloat16
 F32 = jnp.float32
@@ -31,95 +32,115 @@
     return lax.dot_general(a, b, (((1,), (0,)), ((), ())), preferred_element_type=F32)
 
 
-def gather_kernel(lists, table, *rest):
-    outs, sem = rest[:-1], rest[-1]
-    copies = []
-    for side_index, out in enumerate(outs):
-        for k in range(out.shape[0]):
-            copies.append(
-                pltpu.make_async_copy(
-                    table.at[lists[side_index, k]], out.at[k], sem.at[side_index, k]
-                )
-            )
+def gather_kernel(lists, table, first_row, first_col, *refs):
+    sides, cap = lists.shape
+    outs, (row, col, sems) = refs[:sides], refs[sides:]
+    copies = [
+        pltpu.make_async_copy(table.at[lists[i, k]], outs[i].at[k], sems.at[i, k])
+        for i in range(sides)
+        for k in range(cap)
+    ]
     for copy in copies:
         copy.start()
+    row[...] = first_row[...]
+    col[...] = first_col[:, :1]
     for copy in copies:
         copy.wait()
 
 
-def gather_sends(table, lists):
+def gather_sends(table, basis, lists):
     sides, cap = lists.shape
+    nx, ny, width = basis.shape
     shape = jax.ShapeDtypeStruct((cap,) + table.shape[1:], table.dtype)
+    some = min(8, ny)
     return pl.pallas_call(
         gather_kernel,
-        out_shape=[shape] * sides,
+        out_shape=[shape] * sides
+        + [
+            jax.ShapeDtypeStruct((1, ny, width), F32),
+            jax.ShapeDtypeStruct((nx, 1, width), F32),
+        ],
         grid_spec=pltpu.PrefetchScalarGridSpec(
             num_scalar_prefetch=1,
-            grid=(),
-            in_specs=[pl.BlockSpec(memory_space=pl.ANY)],
-            out_specs=[pl.BlockSpec(memory_space=pltpu.VMEM)] * sides,
+            grid=(1,),
+            in_specs=[
+                pl.BlockSpec(memory_space=pltpu.HBM),
+                pl.BlockSpec((1, ny, width), lambda *_: (0, 0, 0)),
+                pl.BlockSpec((nx, some, width), lambda *_: (0, 0, 0)),
+            ],
+            out_specs=[pl.BlockSpec(shape.shape, lambda *_: (0, 0, 0))] * sides
+            + [
+                pl.BlockSpec((1, ny, width), lambda *_: (0, 0, 0)),
+                pl.BlockSpec((nx, 1, width), lambda *_: (0, 0, 0)),
+            ],
             scratch_shapes=[pltpu.SemaphoreType.DMA((sides, cap))],
         ),
         name="gather_sends",
-    )(lists, table)
+    )(lists, table, basis, basis)
+
+
+def in_vmem(value):
+    return pltpu.with_memory_space_constraint(value, pltpu.VMEM)
+
+
+def in_hbm(value):
+    return pltpu.with_memory_space_constraint(value, pltpu.HBM)
+
+
+VMEM_SPEC = pl.BlockSpec(memory_space=pltpu.VMEM)
 
 
 def own_kernel(owned, high, low, turned):
     group, block, width = owned.shape
+    at = pl.program_id(0)
+    rows = pl.ds(at * group, group)
     value = owned[...]
     top, rest = split(value)
-    high[...] = top
-    low[...] = rest
+    high[rows] = top
+    low[rows] = rest
     flat = value.reshape(group * block, width)
     t_high, t_low = split(flat.T)
-    turned[0, :, : group * block] = t_high
-    turned[0, :, group * block :] = t_low
+    turned[at, :, : group * block] = t_high
+    turned[at, :, group * block :] = t_low
 
 
 def split_own(owned, entries):
     count, block, width = owned.shape
     steps = count // ROWS
     depth = ROWS * block
-    table = jax.ShapeDtypeStruct((entries, block, width), BF16)
-    table_spec = pl.BlockSpec((ROWS, block, width), lambda i: (i, 0, 0))
+    table = pltpu.VMEM((entries, block, width), BF16)
     return pl.pallas_call(
         own_kernel,
-        out_shape=[table, table, jax.ShapeDtypeStruct((steps, width, 2 * depth), BF16)],
+        out_shape=[table, table, pltpu.VMEM((steps, width, 2 * depth), BF16)],
         grid=(steps,),
-        in_specs=[table_spec],
-        out_specs=[
-            table_spec,
-            table_spec,
-            pl.BlockSpec((1, width, 2 * depth), lambda i: (i, 0, 0)),
-        ],
+        in_specs=[pl.BlockSpec((ROWS, block, width), lambda i: (i, 0, 0))],
+        out_specs=[VMEM_SPEC] * 3,
+        compiler_params=pltpu.CompilerParams(vmem_limit_bytes=24 << 20),
         name="split_own",
     )(owned)
 
 
 def ghost_kernel(*refs):
     ghosts, high, low = refs[:-4], refs[-2], refs[-1]
+    cap = ghosts[0].shape[0]
+    count = high.shape[0] - len(ghosts) * cap
     for k, ghost in enumerate(ghosts):
-        @pl.when(pl.program_id(0) == k)
-        def _():
-            top, rest = split(ghost[...])
-            high[...] = top
-            low[...] = rest
-
-
-def split_ghosts(ghosts, high, low, count):
-    cap, block, width = ghosts[0].shape
-    whole = pl.BlockSpec(ghosts[0].shape, lambda i: (0, 0, 0))
-    out_spec = pl.BlockSpec(ghosts[0].shape, lambda i: (count // cap + i, 0, 0))
+        top, rest = split(ghost[...])
+        high[count + k * cap : count + (k + 1) * cap] = top
+        low[count + k * cap : count + (k + 1) * cap] = rest
+
+
+def add_ghosts(high, low, ghosts):
     n = len(ghosts)
     return pl.pallas_call(
         ghost_kernel,
-        out_shape=[jax.ShapeDtypeStruct(high.shape, BF16)] * 2,
-        grid=(n,),
-        in_specs=[whole] * n + [pl.BlockSpec(memory_space=pl.ANY)] * 2,
-        out_specs=[out_spec] * 2,
+        out_shape=[pltpu.VMEM(high.shape, BF16)] * 2,
+        in_specs=[VMEM_SPEC] * (n + 2),
+        out_specs=[VMEM_SPEC] * 2,
         input_output_aliases={n: 0, n + 1: 1},
-        name="split_ghosts",
-    )(*ghosts, high, low)
+        compiler_params=pltpu.CompilerParams(vmem_limit_bytes=24 << 20),
+        name="add_ghosts",
+    )(*[in_vmem(ghost) for ghost in ghosts], in_vmem(high), in_vmem(low))
 
 
 DIE_FIELDS = ((0,), (1,), (2,), (0,), (1, 2))
@@ -143,7 +164,7 @@
             turned[k, :, cells:] = t_low
 
     def gram(k):
-        w_high, w_low = split(weights[0] * fields[k])
+        w_high, w_low = split((weights[0][:, :, None] * fields[k].reshape(nx, ny, width)).reshape(cells, width))
         pair = turned[k]
         left = jnp.concatenate([pair, pair[:, :cells]], axis=1)
         return mm(left, jnp.concatenate([w_high, w_high, w_low], axis=0))
@@ -173,7 +194,7 @@
             whole(basis),
             whole(next_row),
             whole(next_col),
-            pl.BlockSpec((1, cells, 1), lambda i: (i, 0, 0)),
+            pl.BlockSpec((1, nx, ny), lambda i: (i, 0, 0)),
         ],
         out_specs=pl.BlockSpec((1, width, width), lambda i: (i, 0, 0)),
         scratch_shapes=[
@@ -183,23 +204,22 @@
         cost_estimate=pl.CostEstimate(
             flops=36 * cells * width * width, transcendentals=0, bytes_accessed=8 * terms * width * width
         ),
+        compiler_params=pltpu.CompilerParams(vmem_limit_bytes=24 << 20),
         name="die_parts",
     )(basis, next_row, next_col, weights)
 
 
 def term_kernel(
-    columns, counts, core, die, turned, high, low, blocks, keep, send,
+    columns, counts, core, die, blocks, high, low, turned, keep, send,
     total, image_high, image_low, *, first,
 ):
     term = first + pl.program_id(0)
     mine = core[0]
-    count = blocks.shape[1]
-    block, wide = blocks.shape[2:]
+    count, block, wide = blocks.shape[1:]
     entries = wide // block
     groups = turned.shape[0]
     per = count // groups
     depth = per * block
-    half = keep.shape[1]
     lane = lax.broadcasted_iota(jnp.int32, (block, wide), 1)
 
     def image_rows(group, slot):
@@ -238,14 +258,11 @@
     send[0] = total[1 - mine]
 
 
-def project_terms(first, number, columns, counts, core, die, turned, high, low, blocks):
-    terms, count, block, wide = blocks.shape
+def project_terms(first, number, columns, counts, core, die, blocks, high, low, turned):
+    _, count, block, wide = blocks.shape
     width = high.shape[2]
     depth = turned.shape[2] // 2
     half = width // 2
-
-    def whole(array):
-        return pl.BlockSpec(array.shape, lambda i, *_: (0,) * array.ndim, pipeline_mode=pl.Buffered(1))
 
     def kernel(*refs):
         term_kernel(*refs, first=first)
@@ -260,10 +277,10 @@
             grid=(number,),
             in_specs=[
                 pl.BlockSpec((1, width, width), lambda i, *_: (first + i, 0, 0)),
-                whole(turned),
-                whole(high),
-                whole(low),
                 pl.BlockSpec((1, count, block, wide), lambda i, *_: (first + i, 0, 0, 0)),
+                VMEM_SPEC,
+                VMEM_SPEC,
+                VMEM_SPEC,
             ],
             out_specs=[out_spec, out_spec],
             scratch_shapes=[
@@ -272,14 +289,16 @@
                 pltpu.VMEM((2, depth, width), BF16),
             ],
         ),
-        compiler_params=pltpu.CompilerParams(vmem_limit_bytes=40 << 20),
+        compiler_params=pltpu.CompilerParams(vmem_limit_bytes=24 << 20),
         cost_estimate=pl.CostEstimate(
             flops=8 * number * count * block * width * (wide + width),
             transcendentals=0,
             bytes_accessed=4 * number * (count * block * wide + 2 * width * width),
         ),
-        name=f"terms_{first}_{number}",
-    )(columns, counts, core, die, turned, high, low, blocks)
+    )(
+        columns, counts, core, in_hbm(die), in_hbm(blocks), in_vmem(high), in_vmem(low),
+        in_vmem(turned),
+    )
 
 
 def place_kernel(core, mine, other, *refs):
@@ -311,22 +330,36 @@
             out_specs=pl.BlockSpec((1, 2 * half, width), lambda i, *_: (first + i, 0, 0)),
         ),
         input_output_aliases={3: 0} if extra else {},
-        name=f"place_{first}",
     )(core, mine, other, *extra)
 
 
-def flip(value, axis, mask):
+def bits(axis):
     count = lax.axis_size(axis)
-    return lax.ppermute(value, axis, [(i, i ^ mask) for i in range(count)])
-
-
-def side(axis, mask):
+    return [(axis, 1 << k) for k in range(count.bit_length() - 1)]
+
+
+def side(dim):
+    axis, mask = dim
     return (lax.axis_index(axis) // mask) % 2
 
 
-def halve(pair, dim):
-    axis, mask = dim
-    mine = side(axis, mask)
+def flip(value, dims):
+    rows, cols = lax.axis_size("gx"), lax.axis_size("gy")
+    pairs = []
+    for a in range(rows):
+        for b in range(cols):
+            axis, mask = dims[b % 2]
+            there = (a ^ mask, b) if axis == "gx" else (a, b ^ mask)
+            pairs.append((a * cols + b, there[0] * cols + there[1]))
+    return lax.ppermute(value, ("gx", "gy"), pairs)
+
+
+def side_of(dims):
+    return jnp.where(lax.axis_index("gy") % 2 == 0, side(dims[0]), side(dims[1]))
+
+
+def halve(pair, dims):
+    mine = side_of(dims)
 
     def half_of(which):
         picked = [
@@ -337,25 +370,22 @@
         ]
         return picked[0] + picked[1]
 
-    return half_of(mine), flip(half_of(1 - mine), axis, mask)
-
-
-def double(value, dim):
-    axis, mask = dim
-    other = flip(value, axis, mask)
+    return half_of(mine), flip(half_of(1 - mine), dims)
+
+
+def double(value, dims):
+    other = flip(value, dims)
     low = jnp.concatenate([value, other], axis=0)
     high = jnp.concatenate([other, value], axis=0)
-    return jnp.where(side(axis, mask) == 0, low, high)
-
-
-def masks(axis):
-    count = lax.axis_size(axis)
-    return [(axis, 1 << k) for k in range(count.bit_length() - 1)]
+    return jnp.where(side_of(dims) == 0, low, high)
+
+
+CHUNKS = 3
 
 
 def chunk_sizes(terms):
-    base, extra = divmod(terms, 3)
-    return [n for n in (base + (k < extra) for k in range(3)) if n]
+    base, extra = divmod(terms, CHUNKS)
+    return [n for n in (base + (k < extra) for k in range(CHUNKS)) if n]
 
 
 def summed(keep, received, order):
@@ -370,35 +400,31 @@
 
 
 def body(die_basis, die_coeff, pkg_basis, send_blocks, columns, counts, pkg_blocks):
-    next_x_row = from_behind(die_basis[:1], "gx", -1)
-    next_y_col = from_behind(die_basis[:, :1], "gy", -1)
     lists = send_blocks[0]
-    sends = gather_sends(pkg_basis, lists)
-    ghosts = [
-        passed_along(sends[0], "gx", 1),
-        passed_along(sends[1], "gx", -1),
-        passed_along(sends[2], "gy", 1),
-        passed_along(sends[3], "gy", -1),
-    ]
-    count = pkg_basis.shape[0]
+    *sends, row, col = gather_sends(pkg_basis, die_basis, lists)
+    next_x_row = from_behind(row, "gx", -1)
+    next_y_col = from_behind(col, "gy", -1)
+    ghosts = []
+    for k, (axis, steps) in enumerate((("gx", 1), ("gx", -1), ("gy", 1), ("gy", -1))):
+        ghosts.append(passed_along(sends[k], axis, steps))
     terms = columns.shape[0]
-    high, low, turned = split_own(pkg_basis, count + lists.shape[0] * lists.shape[1])
-    weights = die_coeff.reshape(terms, -1, 1)
-    die = die_parts(die_basis, next_x_row, next_y_col, weights)
-    high, low = split_ghosts(ghosts, high, low, count)
+    entries = pkg_basis.shape[0] + lists.shape[0] * lists.shape[1]
+    high, low, turned = split_own(pkg_basis, entries)
+    die = die_parts(die_basis, next_x_row, next_y_col, die_coeff)
+    high, low = add_ghosts(high, low, ghosts)
     columns = columns.reshape(terms, -1)
-    (axis, mask), *plane = masks("gy")
-    line = masks("gx")
-    core = side(axis, mask).astype(jnp.int32).reshape(1)
-    orders = [plane + line, plane[1:] + line + plane[:1], line + plane]
+    pair, *plane = bits("gy")
+    line = bits("gx")
+    core = side(pair).astype(jnp.int32).reshape(1)
+    orders = list(zip(plane + line, plane[1:] + line + plane[:1]))
     reduced = None
     first = 0
-    for number, order in zip(chunk_sizes(terms), orders):
+    for number in chunk_sizes(terms):
         keep, send = project_terms(
-            first, number, columns, counts, core, die, turned, high, low, pkg_blocks
+            first, number, columns, counts, core, die, pkg_blocks, high, low, turned
         )
-        mine = summed(keep, flip(send, axis, mask), order)
-        other = flip(mine, axis, mask)
+        mine = summed(keep, flip(send, (pair, pair)), orders)
+        other = flip(mine, (pair, pair))
         reduced = place(core, mine, other, first, terms, reduced)
         first += number
     return reduced

time: 206 us -> 186 us (0.903)
  waiting for transfers between devices: 71.1 us -> 60 us
  Pallas kernels: 78.9 us -> 70.3 us
    ppermute x30, waiting for transfers between devices: 60.9 us -> 46.6 us  [flip(): return lax.ppermute(value, ('gx', 'gy'), pairs)]
    pallas_call x3, Pallas kernels: 14.9 us -> 8.68 us  [the longest x1 4.91 us: gather_sends(): pl.pallas_call(gather_kernel, out_shape=[shape] * sides + [jax.ShapeDtype...]
    ppermute x2, waiting for transfers between devices: 10.2 us -> 13.4 us  [from_behind(): lax.ppermute(value, axis, [(source, source + steps) for source in range(l...]
    reshape x1 -> x0, local copies, waits for them, and re-layouts: 2.45 us -> none  [body(): weights = die_coeff.reshape(terms, -1, 1)]
    pallas_call x1, Pallas kernels: 9 us -> 6.56 us  [die_parts(): pl.pallas_call(die_kernel, out_shape=jax.ShapeDtypeStruct((terms, width,...]
    unnamed x47 -> x43, local copies, waits for them, and re-layouts: 13.8 us -> 16.1 us
  transfers between devices with their start and end apart: 36 -> 36, of which waited for: 18 -> 17; matrix products, arithmetic and copies ran while one was open for 4% -> 3% of each run, Pallas kernels for 27% -> 23%
where the time goes in v2:
time: 186 us; the launch traced here: 185 us
  Pallas kernels  70.3 us (38%)
  waiting for transfers between devices  60 us (32%)
  starting transfers between devices  33.6 us (18%)
  local copies, waits for them, and re-layouts  16.2 us (9%)
  other arithmetic  4.53 us (2%)
    pallas_call x3, Pallas kernels, project_terms(): pl.pallas_call(kernel, out_shape=[out, out], grid_spec=pltpu.PrefetchScal...  47.5 us
    ppermute x30, waiting for transfers between devices, flip(): return lax.ppermute(value, ('gx', 'gy'), pairs)  46.6 us
    ppermute x30, starting transfers between devices, flip(): return lax.ppermute(value, ('gx', 'gy'), pairs)  22.9 us
    unnamed x43, local copies, waits for them, and re-layouts  16.1 us
    ppermute x2, waiting for transfers between devices, from_behind(): lax.ppermute(value, axis, [(source, source + steps) for source in range(l...  13.4 us
    ppermute x4, starting transfers between devices, passed_along(): return lax.ppermute(value, axis, pairs)  8.09 us
    pallas_call x3, Pallas kernels, place(): pl.pallas_call(place_kernel, out_shape=jax.ShapeDtypeStruct((terms, 2 * h...  7.53 us
    pallas_call x1, Pallas kernels, die_parts(): pl.pallas_call(die_kernel, out_shape=jax.ShapeDtypeStruct((terms, width,...  6.56 us
  transfers between devices with their start and end apart: 36, of which 17 were waited for; matrix products, arithmetic and copies ran while one was open for 3% of the time, Pallas kernels for 23%

profile of v2, /device:TPU:0, one launch (start us, length us, event | category | flops | bytes accessed | tf_op | source)
XLA Modules:
  0.0 185.0 jit_solution(6323637780812089020)
XLA Ops:
  0.0 4.9 %gather_sends.1 = (f32[4,64,512]{2,1,0:T(8,128)}, f32[4,64,512]{2,1,0:T(8,128)}, f32[4,64,512]{2,1,0:T(8,128)}, f32[4,64,512]{2,1,0:T(8,128)}, f32[1,32,512]{2,1,0:T(8,128)}, /*index=5*/f32[16,1,512]{2,1,0:T(1,128)}) custom-call(s32[4,4]{1,0:T(4,128)} %bitcast.88, f32[32,64,512]{2,1,0:T(8,128)} %owned.1, f32[16,32,512]{2,1,0:T(8,128)} %basis.1, ...), custom_call_target="tpu_custom_call" | custom-call | tf_op jit(solution)/shard_map/gather_sends/pallas_call | solution.py:56
  6.2 3.1 %collective-permute-start.2 = (f32[4,64,512]{2,1,0:T(8,128)}, f32[4,64,512]{2,1,0:T(8,128)}, u32[]{:S(2)}, u32[]{:S(2)}) collective-permute-start(f32[4,64,512]{2,1,0:T(8,128)} %get-tuple-element.24), channel_id=1, source_target_pairs={{0,8},{8,16},{16,24},{24,0},{1,9},{9,17},{17,25},{25,1},{2,10},{10... | collective-permute-start | bytes 1572872 | tf_op jit(solution)/shard_map/ppermute | solution.py:23
  9.3 2.1 %collective-permute-start.3 = (f32[4,64,512]{2,1,0:T(8,128)}, f32[4,64,512]{2,1,0:T(8,128)}, u32[]{:S(2)}, u32[]{:S(2)}) collective-permute-start(f32[4,64,512]{2,1,0:T(8,128)} %get-tuple-element.25), channel_id=1, source_target_pairs={{0,24},{8,0},{16,8},{24,16},{1,25},{9,1},{17,9},{25,17},{2,26},{10... | collective-permute-start | bytes 1572872 | tf_op jit(solution)/shard_map/ppermute | solution.py:23
  12.3 2.1 %collective-permute-start.5 = (f32[4,64,512]{2,1,0:T(8,128)}, f32[4,64,512]{2,1,0:T(8,128)}, u32[]{:S(2)}, u32[]{:S(2)}) collective-permute-start(f32[4,64,512]{2,1,0:T(8,128)} %get-tuple-element.27), channel_id=1, source_target_pairs={{0,7},{1,0},{2,1},{3,2},{4,3},{5,4},{6,5},{7,6},{8,15},{9,8},{10,9... | collective-permute-start | bytes 1572872 | tf_op jit(solution)/shard_map/ppermute | solution.py:23
  15.6 2.2 %copy-done = f32[32,64,512]{2,1,0:T(8,128)S(1)} copy-done((f32[32,64,512]{2,1,0:T(8,128)S(1)}, f32[32,64,512]{2,1,0:T(8,128)}, u32[]{:S(2)}) %copy-start) | copy-done | bytes 4194328
  17.8 1.7 split_own.1
  21.2 2.0 %copy-done.6 = bf16[8,512,512]{2,1,0:T(8,128)(2,1)} copy-done((bf16[8,512,512]{2,1,0:T(8,128)(2,1)}, bf16[8,512,512]{2,1,0:T(8,128)(2,1)S(1)}, u32[]{:S(2)}) %copy-start.6) | copy-done | bytes 4194328
  23.4 13.4 %collective-permute-done.next_row = f32[1,32,512]{2,1,0:T(8,128)S(1)} collective-permute-done((f32[1,32,512]{2,1,0:T(8,128)}, f32[1,32,512]{2,1,0:T(8,128)S(1)}, u32[]{:S(2)}, u32[]{:S(2)}) %collective-permute-start) | collective-permute-done | bytes 65568 | tf_op jit(solution)/shard_map/ppermute | solution.py:17
  38.1 6.6 %die_parts.1.refs_3_ = f32[5,512,512]{2,1,0:T(8,128)S(1)} custom-call(f32[16,32,512]{2,1,0:T(8,128)S(1)} %copy-done.9, f32[1,32,512]{2,1,0:T(8,128)S(1)} %collective-permute-done.next_row, f32[16,1,512]{2,1,0:T(1,128)S(1)} %collective-permute-done.1.next_col, f32[5,16,32]{2,1,0:T(8,128)S(1)} %copy-done.15), custom_call_target="tpu_custom_call" | custom-call | flops 4831838208 | bytes 10485760 | tf_op jit(solution)/shard_map/die_parts/pallas_call | solution.py:189
  44.7 2.3 %copy-done.5 = f32[5,512,512]{2,1,0:T(8,128)} copy-done((f32[5,512,512]{2,1,0:T(8,128)}, f32[5,512,512]{2,1,0:T(8,128)S(1)}, u32[]{:S(2)}) %copy-start.5) | copy-done | bytes 5242904
  47.1 2.0 %add_ghosts.1 = (bf16[48,64,512]{2,1,0:T(8,128)(2,1)S(1)}, bf16[48,64,512]{2,1,0:T(8,128)(2,1)S(1)}) custom-call(f32[4,64,512]{2,1,0:T(8,128)} %collective-permute-done.2.refs_0_, f32[4,64,512]{2,1,0:T(8,128)} %collective-permute-done.3.refs_1_, f32[4,64,512]{2,1,0:T(8,128)} %collective-permute-done.4.refs_2_, ...), custom_call_target="tpu_custom_call", output_to_operand_aliasing={{0}: (4, {}), {1}: (5, {})} | custom-call | tf_op jit(solution)/shard_map/add_ghosts/pallas_call | solution.py:135
  49.9 18.3 %shard_map.74 = (f32[2,256,512]{2,1,0:T(8,128)S(1)}, f32[2,256,512]{2,1,0:T(8,128)}) custom-call(s32[5,128]{1,0:T(8,128)S(1)} %reshape.217.refs_0_, s32[5,32]{1,0:T(8,128)S(1)} %copy-done.14, s32[1]{0:T(128)} %bitcast.refs_2_.core, f32[5,512,512]{2,1,0:T(8,128)} %copy-done.5, f32[5,32,64,256]{3,2,1,0:T(8,128)} %refs_4_.5, ...), custom_call_target="tpu_custom_call" | custom-call | flops 12884901888 | bytes 8388608 | tf_op jit(solution)/shard_map/pallas_call | solution.py:272
  69.1 18.2 %shard_map.75 = (f32[2,256,512]{2,1,0:T(8,128)S(1)}, f32[2,256,512]{2,1,0:T(8,128)}) custom-call(s32[5,128]{1,0:T(8,128)S(1)} %reshape.217.refs_0_, s32[5,32]{1,0:T(8,128)S(1)} %copy-done.14, s32[1]{0:T(128)} %bitcast.refs_2_.core, f32[5,512,512]{2,1,0:T(8,128)} %copy-done.5, f32[5,32,64,256]{3,2,1,0:T(8,128)} %refs_4_.5, ...), custom_call_target="tpu_custom_call" | custom-call | flops 12884901888 | bytes 8388608 | tf_op jit(solution)/shard_map/pallas_call | solution.py:272
  88.9 1.9 %dynamic-slice_add_fusion.1 = (f32[1,256,512]{2,1,0:T(8,128)S(1)}, f32[256,512]{1,0:T(8,128)S(1)}) fusion(f32[2,256,512]{2,1,0:T(8,128)} %collective-permute-done.16, s32[]{:T(128)S(6)} %select_n.430, f32[2,256,512]{2,1,0:T(8,128)} %copy-done.11, s32[]{:T(128)S(6)} %select_n.432), kind=kLoop, calls=%fused_computation.8 | loop fusion | flops 262144 | bytes 3145736 | tf_op jit(solution)/shard_map/add | solution.py:371
  94.8 2.2 %copy-done.8 = bf16[8,512,512]{2,1,0:T(8,128)(2,1)S(1)} copy-done((bf16[8,512,512]{2,1,0:T(8,128)(2,1)S(1)}, bf16[8,512,512]{2,1,0:T(8,128)(2,1)}, u32[]{:S(2)}) %copy-start.8) | copy-done | bytes 4194328
  97.0 11.0 %shard_map.73 = (f32[1,256,512]{2,1,0:T(8,128)S(1)}, f32[1,256,512]{2,1,0:T(8,128)}) custom-call(s32[5,128]{1,0:T(8,128)S(1)} %reshape.217.refs_0_, s32[5,32]{1,0:T(8,128)S(1)} %copy-done.14, s32[1]{0:T(128)} %bitcast.refs_2_.core, f32[5,512,512]{2,1,0:T(8,128)} %copy-done.5, f32[5,32,64,256]{3,2,1,0:T(8,128)} %refs_4_.5, ...), custom_call_target="tpu_custom_call" | custom-call | flops 6442450944 | bytes 4194304 | tf_op jit(solution)/shard_map/pallas_call | solution.py:272
  111.2 4.2 %collective-permute-done.18 = f32[128,512]{1,0:T(8,128)S(1)} collective-permute-done((f32[128,512]{1,0:T(8,128)S(1)}, f32[128,512]{1,0:T(8,128)S(1)}, u32[]{:S(2)}, u32[]{:S(2)}) %collective-permute-start.18) | collective-permute-done | bytes 262176 | tf_op jit(solution)/shard_map/ppermute | solution.py:354
  125.3 1.9 %collective-permute-done.20 = f32[32,512]{1,0:T(8,128)S(1)} collective-permute-done((f32[32,512]{1,0:T(8,128)S(1)}, f32[32,512]{1,0:T(8,128)S(1)}, u32[]{:S(2)}, u32[]{:S(2)}) %collective-permute-start.20) | collective-permute-done | bytes 65568 | tf_op jit(solution)/shard_map/ppermute | solution.py:354
  127.8 2.1 %collective-permute-done.30 = f32[32,512]{1,0:T(8,128)S(1)} collective-permute-done((f32[32,512]{1,0:T(8,128)S(1)}, f32[32,512]{1,0:T(8,128)S(1)}, u32[]{:S(2)}, u32[]{:S(2)}) %collective-permute-start.30) | collective-permute-done | bytes 65568 | tf_op jit(solution)/shard_map/ppermute | solution.py:354
  130.6 4.8 %collective-permute-done.21 = f32[32,512]{1,0:T(8,128)S(1)} collective-permute-done((f32[32,512]{1,0:T(8,128)S(1)}, f32[32,512]{1,0:T(8,128)S(1)}, u32[]{:S(2)}, u32[]{:S(2)}) %collective-permute-start.21) | collective-permute-done | bytes 65568 | tf_op jit(solution)/shard_map/ppermute | solution.py:354
  136.5 1.8 collective-permute-done.31
  138.5 2.7 %collective-permute-done.22 = f32[64,512]{1,0:T(8,128)S(1)} collective-permute-done((f32[64,512]{1,0:T(8,128)S(1)}, f32[64,512]{1,0:T(8,128)S(1)}, u32[]{:S(2)}, u32[]{:S(2)}) %collective-permute-start.22) | collective-permute-done | bytes 131104 | tf_op jit(solution)/shard_map/ppermute | solution.py:354
  143.0 2.4 %collective-permute-done.32 = f32[64,512]{1,0:T(8,128)S(1)} collective-permute-done((f32[64,512]{1,0:T(8,128)S(1)}, f32[64,512]{1,0:T(8,128)S(1)}, u32[]{:S(2)}, u32[]{:S(2)}) %collective-permute-start.32) | collective-permute-done | bytes 131104 | tf_op jit(solution)/shard_map/ppermute | solution.py:354
  149.4 5.2 %collective-permute-done.33 = f32[128,512]{1,0:T(8,128)S(1)} collective-permute-done((f32[128,512]{1,0:T(8,128)S(1)}, f32[128,512]{1,0:T(8,128)S(1)}, u32[]{:S(2)}, u32[]{:S(2)}) %collective-permute-start.33) | collective-permute-done | bytes 262176 | tf_op jit(solution)/shard_map/ppermute | solution.py:354
  155.7 4.8 %collective-permute-done.11 = f32[16,512]{1,0:T(8,128)S(1)} collective-permute-done((f32[16,512]{1,0:T(8,128)S(1)}, f32[16,512]{1,0:T(8,128)S(1)}, u32[]{:S(2)}, u32[]{:S(2)}) %collective-permute-start.11) | collective-permute-done | bytes 32800 | tf_op jit(solution)/shard_map/ppermute | solution.py:354
  160.6 4.2 %collective-permute-done.12 = f32[32,512]{1,0:T(8,128)S(1)} collective-permute-done((f32[32,512]{1,0:T(8,128)S(1)}, f32[32,512]{1,0:T(8,128)S(1)}, u32[]{:S(2)}, u32[]{:S(2)}) %collective-permute-start.12) | collective-permute-done | bytes 65568 | tf_op jit(solution)/shard_map/ppermute | solution.py:354
  167.0 3.0 %collective-permute-done.13 = f32[64,512]{1,0:T(8,128)S(1)} collective-permute-done((f32[64,512]{1,0:T(8,128)S(1)}, f32[64,512]{1,0:T(8,128)S(1)}, u32[]{:S(2)}, u32[]{:S(2)}) %collective-permute-start.13) | collective-permute-done | bytes 131104 | tf_op jit(solution)/shard_map/ppermute | solution.py:354
  170.0 2.0 %collective-permute-start.14 = (f32[128,512]{1,0:T(8,128)S(1)}, f32[128,512]{1,0:T(8,128)S(1)}, u32[]{:S(2)}, u32[]{:S(2)}) collective-permute-start(f32[128,512]{1,0:T(8,128)S(1)} %maximum_select_fusion.5), channel_id=1, source_target_pairs={{0,2},{1,5},{2,0},{3,7},{4,6},{5,1},{6,4},{7,3},{8,10},{9,13},{10,... | collective-permute-start | bytes 786440 | tf_op jit(solution)/shard_map/ppermute | solution.py:354
  172.0 4.5 %collective-permute-done.14 = f32[128,512]{1,0:T(8,128)S(1)} collective-permute-done((f32[128,512]{1,0:T(8,128)S(1)}, f32[128,512]{1,0:T(8,128)S(1)}, u32[]{:S(2)}, u32[]{:S(2)}) %collective-permute-start.14) | collective-permute-done | bytes 262176 | tf_op jit(solution)/shard_map/ppermute | solution.py:354
  176.6 2.7 %shard_map.76.refs_0_ = f32[5,512,512]{2,1,0:T(8,128)} custom-call(s32[1]{0:T(128)} %bitcast.refs_2_.core, f32[2,256,512]{2,1,0:T(8,128)} %bitcast.60, f32[2,256,512]{2,1,0:T(8,128)} %collective-permute-done.35.other), custom_call_target="tpu_custom_call" | custom-call | tf_op jit(solution)/shard_map/pallas_call | solution.py:323
  179.3 2.6 %shard_map.77.refs_0_ = f32[5,512,512]{2,1,0:T(8,128)} custom-call(s32[1]{0:T(128)} %bitcast.refs_2_.core, f32[2,256,512]{2,1,0:T(8,128)} %bitcast.58, f32[2,256,512]{2,1,0:T(8,128)} %collective-permute-done.25.other, f32[5,512,512]{2,1,0:T(8,128)} %shard_map.76.refs_0_), custom_call_target="tpu_custom_call", output_to_operand_aliasing={{}: (3, {})} | custom-call | tf_op jit(solution)/shard_map/pallas_call | solution.py:323
  182.8 2.2 %shard_map.78 = f32[5,512,512]{2,1,0:T(8,128)} custom-call(s32[1]{0:T(128)} %bitcast.refs_2_.core, f32[1,256,512]{2,1,0:T(8,128)} %copy-done.18, f32[1,256,512]{2,1,0:T(8,128)} %copy-done.19, f32[5,512,512]{2,1,0:T(8,128)} %shard_map.77.refs_0_), custom_call_target="tpu_custom_call", output_to_operand_aliasing={{}: (3, {})} | custom-call | tf_op jit(solution)/shard_map/pallas_call | solution.py:323
  (121 shorter events, 39.4 us)
Async XLA Ops:
  4.9 9.4 %collective-permute-start.1 = (f32[16,1,512]{2,1,0:T(1,128)}, f32[16,1,512]{2,1,0:T(1,128)S(1)}, u32[]{:S(2)}, u32[]{:S(2)}) collective-permute-start(f32[16,1,512]{2,1,0:T(1,128)} %get-tuple-element.23), channel_id=1, source_target_pairs={{1,0},{2,1},{3,2},{4,3},{5,4},{6,5},{7,6},{9,8},{10,9},{11,10},{12... | collective-permute-start | bytes 98312 | tf_op jit(solution)/shard_map/ppermute | solution.py:17
  6.2 40.8 %collective-permute-start.2 = (f32[4,64,512]{2,1,0:T(8,128)}, f32[4,64,512]{2,1,0:T(8,128)}, u32[]{:S(2)}, u32[]{:S(2)}) collective-permute-start(f32[4,64,512]{2,1,0:T(8,128)} %get-tuple-element.24), channel_id=1, source_target_pairs={{0,8},{8,16},{16,24},{24,0},{1,9},{9,17},{17,25},{25,1},{2,10},{10... | collective-permute-start | bytes 1572872 | tf_op jit(solution)/shard_map/ppermute | solution.py:23
  9.3 37.7 %collective-permute-start.3 = (f32[4,64,512]{2,1,0:T(8,128)}, f32[4,64,512]{2,1,0:T(8,128)}, u32[]{:S(2)}, u32[]{:S(2)}) collective-permute-start(f32[4,64,512]{2,1,0:T(8,128)} %get-tuple-element.25), channel_id=1, source_target_pairs={{0,24},{8,0},{16,8},{24,16},{1,25},{9,1},{17,9},{25,17},{2,26},{10... | collective-permute-start | bytes 1572872 | tf_op jit(solution)/shard_map/ppermute | solution.py:23
  11.4 35.6 %collective-permute-start.4 = (f32[4,64,512]{2,1,0:T(8,128)}, f32[4,64,512]{2,1,0:T(8,128)}, u32[]{:S(2)}, u32[]{:S(2)}) collective-permute-start(f32[4,64,512]{2,1,0:T(8,128)} %get-tuple-element.26), channel_id=1, source_target_pairs={{0,1},{1,2},{2,3},{3,4},{4,5},{5,6},{6,7},{7,0},{8,9},{9,10},{10,1... | collective-permute-start | bytes 1572872 | tf_op jit(solution)/shard_map/ppermute | solution.py:23
  12.3 34.8 %collective-permute-start.5 = (f32[4,64,512]{2,1,0:T(8,128)}, f32[4,64,512]{2,1,0:T(8,128)}, u32[]{:S(2)}, u32[]{:S(2)}) collective-permute-start(f32[4,64,512]{2,1,0:T(8,128)} %get-tuple-element.27), channel_id=1, source_target_pairs={{0,7},{1,0},{2,1},{3,2},{4,3},{5,4},{6,5},{7,6},{8,15},{9,8},{10,9... | collective-permute-start | bytes 1572872 | tf_op jit(solution)/shard_map/ppermute | solution.py:23
  14.3 22.5 %collective-permute-start = (f32[1,32,512]{2,1,0:T(8,128)}, f32[1,32,512]{2,1,0:T(8,128)S(1)}, u32[]{:S(2)}, u32[]{:S(2)}) collective-permute-start(f32[1,32,512]{2,1,0:T(8,128)} %get-tuple-element.22), channel_id=1, source_target_pairs={{8,0},{16,8},{24,16},{9,1},{17,9},{25,17},{10,2},{18,10},{26,18},{... | collective-permute-start | bytes 196616 | tf_op jit(solution)/shard_map/ppermute | solution.py:17
  69.1 19.7 %collective-permute-start.16 = (f32[2,256,512]{2,1,0:T(8,128)}, f32[2,256,512]{2,1,0:T(8,128)}, u32[]{:S(2)}, u32[]{:S(2)}) collective-permute-start(f32[2,256,512]{2,1,0:T(8,128)} %get-tuple-element.36), channel_id=1, source_target_pairs={{0,1},{1,0},{2,3},{3,2},{4,5},{5,4},{6,7},{7,6},{8,9},{9,8},{10,11... | collective-permute-start | bytes 3145736 | tf_op jit(solution)/shard_map/ppermute | solution.py:354
  90.7 18.1 %collective-permute-start.17 = (f32[256,512]{1,0:T(8,128)S(1)}, f32[256,512]{1,0:T(8,128)S(1)}, u32[]{:S(2)}, u32[]{:S(2)}) collective-permute-start(f32[256,512]{1,0:T(8,128)S(1)} %get-tuple-element.42), channel_id=1, source_target_pairs={{0,2},{1,5},{2,0},{3,7},{4,6},{5,1},{6,4},{7,3},{8,10},{9,13},{10,... | collective-permute-start | bytes 1572872 | tf_op jit(solution)/shard_map/ppermute | solution.py:354
  94.0 16.4 %collective-permute-start.27 = (f32[256,512]{1,0:T(8,128)S(1)}, f32[256,512]{1,0:T(8,128)S(1)}, u32[]{:S(2)}, u32[]{:S(2)}) collective-permute-start(f32[256,512]{1,0:T(8,128)S(1)} %get-tuple-element.40), channel_id=1, source_target_pairs={{0,2},{1,5},{2,0},{3,7},{4,6},{5,1},{6,4},{7,3},{8,10},{9,13},{10,... | collective-permute-start | bytes 1572872 | tf_op jit(solution)/shard_map/ppermute | solution.py:354
  108.7 10.7 %collective-permute-start.6 = (f32[1,256,512]{2,1,0:T(8,128)}, f32[1,256,512]{2,1,0:T(8,128)S(1)}, u32[]{:S(2)}, u32[]{:S(2)}) collective-permute-start(f32[1,256,512]{2,1,0:T(8,128)} %get-tuple-element.34), channel_id=1, source_target_pairs={{0,1},{1,0},{2,3},{3,2},{4,5},{5,4},{6,7},{7,6},{8,9},{9,8},{10,11... | collective-permute-start | bytes 1572872 | tf_op jit(solution)/shard_map/ppermute | solution.py:354
  108.9 6.4 %collective-permute-start.18 = (f32[128,512]{1,0:T(8,128)S(1)}, f32[128,512]{1,0:T(8,128)S(1)}, u32[]{:S(2)}, u32[]{:S(2)}) collective-permute-start(f32[128,512]{1,0:T(8,128)S(1)} %get-tuple-element.46), channel_id=1, source_target_pairs={{0,4},{1,9},{2,6},{3,11},{4,0},{5,13},{6,2},{7,15},{8,12},{9,1},{1... | collective-permute-start | bytes 786440 | tf_op jit(solution)/shard_map/ppermute | solution.py:354
  110.5 7.7 %collective-permute-start.28 = (f32[128,512]{1,0:T(8,128)S(1)}, f32[128,512]{1,0:T(8,128)S(1)}, u32[]{:S(2)}, u32[]{:S(2)}) collective-permute-start(f32[128,512]{1,0:T(8,128)S(1)} %get-tuple-element.44), channel_id=1, source_target_pairs={{0,4},{1,9},{2,6},{3,11},{4,0},{5,13},{6,2},{7,15},{8,12},{9,1},{1... | collective-permute-start | bytes 786440 | tf_op jit(solution)/shard_map/ppermute | solution.py:354
  115.4 5.9 %collective-permute-start.19 = (f32[64,512]{1,0:T(8,128)S(1)}, f32[64,512]{1,0:T(8,128)S(1)}, u32[]{:S(2)}, u32[]{:S(2)}) collective-permute-start(f32[64,512]{1,0:T(8,128)S(1)} %get-tuple-element.52), channel_id=1, source_target_pairs={{0,8},{1,17},{2,10},{3,19},{4,12},{5,21},{6,14},{7,23},{8,0},{9,25... | collective-permute-start | bytes 393224 | tf_op jit(solution)/shard_map/ppermute | solution.py:354
  118.2 5.9 %collective-permute-start.29 = (f32[64,512]{1,0:T(8,128)S(1)}, f32[64,512]{1,0:T(8,128)S(1)}, u32[]{:S(2)}, u32[]{:S(2)}) collective-permute-start(f32[64,512]{1,0:T(8,128)S(1)} %get-tuple-element.50), channel_id=1, source_target_pairs={{0,8},{1,17},{2,10},{3,19},{4,12},{5,21},{6,14},{7,23},{8,0},{9,25... | collective-permute-start | bytes 393224 | tf_op jit(solution)/shard_map/ppermute | solution.py:354
  119.5 16.0 %collective-permute-start.7 = (f32[128,512]{1,0:T(8,128)S(1)}, f32[128,512]{1,0:T(8,128)S(1)}, u32[]{:S(2)}, u32[]{:S(2)}) collective-permute-start(f32[128,512]{1,0:T(8,128)S(1)} %get-tuple-element.48), channel_id=1, source_target_pairs={{0,2},{1,5},{2,0},{3,7},{4,6},{5,1},{6,4},{7,3},{8,10},{9,13},{10,... | collective-permute-start | bytes 786440 | tf_op jit(solution)/shard_map/ppermute | solution.py:354
  121.3 5.9 %collective-permute-start.20 = (f32[32,512]{1,0:T(8,128)S(1)}, f32[32,512]{1,0:T(8,128)S(1)}, u32[]{:S(2)}, u32[]{:S(2)}) collective-permute-start(f32[32,512]{1,0:T(8,128)S(1)} %add_bitcast_fusion.9), channel_id=1, source_target_pairs={{0,16},{1,3},{2,18},{3,1},{4,20},{5,7},{6,22},{7,5},{8,24},{9,11},... | collective-permute-start | bytes 196616 | tf_op jit(solution)/shard_map/ppermute | solution.py:354
  124.1 5.7 %collective-permute-start.30 = (f32[32,512]{1,0:T(8,128)S(1)}, f32[32,512]{1,0:T(8,128)S(1)}, u32[]{:S(2)}, u32[]{:S(2)}) collective-permute-start(f32[32,512]{1,0:T(8,128)S(1)} %add_bitcast_fusion.8), channel_id=1, source_target_pairs={{0,16},{1,3},{2,18},{3,1},{4,20},{5,7},{6,22},{7,5},{8,24},{9,11},... | collective-permute-start | bytes 196616 | tf_op jit(solution)/shard_map/ppermute | solution.py:354
  127.3 8.1 %collective-permute-start.21 = (f32[32,512]{1,0:T(8,128)S(1)}, f32[32,512]{1,0:T(8,128)S(1)}, u32[]{:S(2)}, u32[]{:S(2)}) collective-permute-start(f32[32,512]{1,0:T(8,128)S(1)} %bitcast_add_fusion.1), channel_id=1, source_target_pairs={{0,16},{1,3},{2,18},{3,1},{4,20},{5,7},{6,22},{7,5},{8,24},{9,11},... | collective-permute-start | bytes 196616 | tf_op jit(solution)/shard_map/ppermute | solution.py:354
  129.9 8.3 %collective-permute-start.31 = (f32[32,512]{1,0:T(8,128)S(1)}, f32[32,512]{1,0:T(8,128)S(1)}, u32[]{:S(2)}, u32[]{:S(2)}) collective-permute-start(f32[32,512]{1,0:T(8,128)S(1)} %bitcast_add_fusion), channel_id=1, source_target_pairs={{0,16},{1,3},{2,18},{3,1},{4,20},{5,7},{6,22},{7,5},{8,24},{9,11},... | collective-permute-start | bytes 196616 | tf_op jit(solution)/shard_map/ppermute | solution.py:354
  135.4 5.8 %collective-permute-start.22 = (f32[64,512]{1,0:T(8,128)S(1)}, f32[64,512]{1,0:T(8,128)S(1)}, u32[]{:S(2)}, u32[]{:S(2)}) collective-permute-start(f32[64,512]{1,0:T(8,128)S(1)} %maximum_select_fusion.9), channel_id=1, source_target_pairs={{0,8},{1,17},{2,10},{3,19},{4,12},{5,21},{6,14},{7,23},{8,0},{9,25... | collective-permute-start | bytes 393224 | tf_op jit(solution)/shard_map/ppermute | solution.py:354
  135.6 7.3 %collective-permute-start.8 = (f32[64,512]{1,0:T(8,128)S(1)}, f32[64,512]{1,0:T(8,128)S(1)}, u32[]{:S(2)}, u32[]{:S(2)}) collective-permute-start(f32[64,512]{1,0:T(8,128)S(1)} %get-tuple-element.54), channel_id=1, source_target_pairs={{0,4},{1,9},{2,6},{3,11},{4,0},{5,13},{6,2},{7,15},{8,12},{9,1},{1... | collective-permute-start | bytes 393224 | tf_op jit(solution)/shard_map/ppermute | solution.py:354
  138.2 7.1 %collective-permute-start.32 = (f32[64,512]{1,0:T(8,128)S(1)}, f32[64,512]{1,0:T(8,128)S(1)}, u32[]{:S(2)}, u32[]{:S(2)}) collective-permute-start(f32[64,512]{1,0:T(8,128)S(1)} %maximum_select_fusion.10), channel_id=1, source_target_pairs={{0,8},{1,17},{2,10},{3,19},{4,12},{5,21},{6,14},{7,23},{8,0},{9,25... | collective-permute-start | bytes 393224 | tf_op jit(solution)/shard_map/ppermute | solution.py:354
  141.3 6.7 %collective-permute-start.23 = (f32[128,512]{1,0:T(8,128)S(1)}, f32[128,512]{1,0:T(8,128)S(1)}, u32[]{:S(2)}, u32[]{:S(2)}) collective-permute-start(f32[128,512]{1,0:T(8,128)S(1)} %maximum_select_fusion.6), channel_id=1, source_target_pairs={{0,4},{1,9},{2,6},{3,11},{4,0},{5,13},{6,2},{7,15},{8,12},{9,1},{1... | collective-permute-start | bytes 786440 | tf_op jit(solution)/shard_map/ppermute | solution.py:354
  145.4 9.2 %collective-permute-start.33 = (f32[128,512]{1,0:T(8,128)S(1)}, f32[128,512]{1,0:T(8,128)S(1)}, u32[]{:S(2)}, u32[]{:S(2)}) collective-permute-start(f32[128,512]{1,0:T(8,128)S(1)} %maximum_select_fusion.7), channel_id=1, source_target_pairs={{0,4},{1,9},{2,6},{3,11},{4,0},{5,13},{6,2},{7,15},{8,12},{9,1},{1... | collective-permute-start | bytes 786440 | tf_op jit(solution)/shard_map/ppermute | solution.py:354
  147.9 7.7 %collective-permute-start.10 = (f32[16,512]{1,0:T(8,128)S(1)}, f32[16,512]{1,0:T(8,128)S(1)}, u32[]{:S(2)}, u32[]{:S(2)}) collective-permute-start(f32[16,512]{1,0:T(8,128)S(1)} %add_bitcast_fusion.11), channel_id=1, source_target_pairs={{0,16},{1,3},{2,18},{3,1},{4,20},{5,7},{6,22},{7,5},{8,24},{9,11},... | collective-permute-start | bytes 98312 | tf_op jit(solution)/shard_map/ppermute | solution.py:354
  148.0 18.3 %collective-permute-start.24 = (f32[256,512]{1,0:T(8,128)S(1)}, f32[256,512]{1,0:T(8,128)S(1)}, u32[]{:S(2)}, u32[]{:S(2)}) collective-permute-start(f32[256,512]{1,0:T(8,128)S(1)} %maximum_select_fusion.3), channel_id=1, source_target_pairs={{0,2},{1,5},{2,0},{3,7},{4,6},{5,1},{6,4},{7,3},{8,10},{9,13},{10,... | collective-permute-start | bytes 1572872 | tf_op jit(solution)/shard_map/ppermute | solution.py:354
  154.7 11.4 %collective-permute-start.34 = (f32[256,512]{1,0:T(8,128)S(1)}, f32[256,512]{1,0:T(8,128)S(1)}, u32[]{:S(2)}, u32[]{:S(2)}) collective-permute-start(f32[256,512]{1,0:T(8,128)S(1)} %maximum_select_fusion.4), channel_id=1, source_target_pairs={{0,2},{1,5},{2,0},{3,7},{4,6},{5,1},{6,4},{7,3},{8,10},{9,13},{10,... | collective-permute-start | bytes 1572872 | tf_op jit(solution)/shard_map/ppermute | solution.py:354
  164.8 5.2 %collective-permute-start.13 = (f32[64,512]{1,0:T(8,128)S(1)}, f32[64,512]{1,0:T(8,128)S(1)}, u32[]{:S(2)}, u32[]{:S(2)}) collective-permute-start(f32[64,512]{1,0:T(8,128)S(1)} %maximum_select_fusion.8), channel_id=1, source_target_pairs={{0,4},{1,9},{2,6},{3,11},{4,0},{5,13},{6,2},{7,15},{8,12},{9,1},{1... | collective-permute-start | bytes 393224 | tf_op jit(solution)/shard_map/ppermute | solution.py:354
  166.2 10.4 %collective-permute-start.35 = (f32[2,256,512]{2,1,0:T(8,128)S(1)}, f32[2,256,512]{2,1,0:T(8,128)}, u32[]{:S(2)}, u32[]{:S(2)}) collective-permute-start(f32[2,256,512]{2,1,0:T(8,128)S(1)} %bitcast.59), channel_id=1, source_target_pairs={{0,1},{1,0},{2,3},{3,2},{4,5},{5,4},{6,7},{7,6},{8,9},{9,8},{10,11... | collective-permute-start | bytes 3145736 | tf_op jit(solution)/shard_map/ppermute | solution.py:354
  166.4 12.9 %collective-permute-start.25 = (f32[2,256,512]{2,1,0:T(8,128)S(1)}, f32[2,256,512]{2,1,0:T(8,128)}, u32[]{:S(2)}, u32[]{:S(2)}) collective-permute-start(f32[2,256,512]{2,1,0:T(8,128)S(1)} %bitcast.57), channel_id=1, source_target_pairs={{0,1},{1,0},{2,3},{3,2},{4,5},{5,4},{6,7},{7,6},{8,9},{9,8},{10,11... | collective-permute-start | bytes 3145736 | tf_op jit(solution)/shard_map/ppermute | solution.py:354
  170.0 6.4 %collective-permute-start.14 = (f32[128,512]{1,0:T(8,128)S(1)}, f32[128,512]{1,0:T(8,128)S(1)}, u32[]{:S(2)}, u32[]{:S(2)}) collective-permute-start(f32[128,512]{1,0:T(8,128)S(1)} %maximum_select_fusion.5), channel_id=1, source_target_pairs={{0,2},{1,5},{2,0},{3,7},{4,6},{5,1},{6,4},{7,3},{8,10},{9,13},{10,... | collective-permute-start | bytes 786440 | tf_op jit(solution)/shard_map/ppermute | solution.py:354
  176.5 5.4 %collective-permute-start.15 = (f32[1,256,512]{2,1,0:T(8,128)S(1)}, f32[1,256,512]{2,1,0:T(8,128)S(1)}, u32[]{:S(2)}, u32[]{:S(2)}) collective-permute-start(f32[1,256,512]{2,1,0:T(8,128)S(1)} %maximum_select_fusion.2.mine), channel_id=1, source_target_pairs={{0,1},{1,0},{2,3},{3,2},{4,5},{5,4},{6,7},{7,6},{8,9},{9,8},{10,11... | collective-permute-start | bytes 1572872 | tf_op jit(solution)/shard_map/ppermute | solution.py:354
  (25 other events, 188.0 us)

commit v3 on v2

--- a/solution.py
+++ b/solution.py
@@ -32,51 +32,45 @@
     return lax.dot_general(a, b, (((1,), (0,)), ((), ())), preferred_element_type=F32)
 
 
-def gather_kernel(lists, table, first_row, first_col, *refs):
-    sides, cap = lists.shape
-    outs, (row, col, sems) = refs[:sides], refs[sides:]
+def gather_kernel(lists, table, edge, *refs, first):
+    outs, (halo, sems) = refs[:-2], refs[-2:]
     copies = [
-        pltpu.make_async_copy(table.at[lists[i, k]], outs[i].at[k], sems.at[i, k])
-        for i in range(sides)
-        for k in range(cap)
+        pltpu.make_async_copy(table.at[lists[first + i, k]], out.at[k], sems.at[i, k])
+        for i, out in enumerate(outs)
+        for k in range(out.shape[0])
     ]
     for copy in copies:
         copy.start()
-    row[...] = first_row[...]
-    col[...] = first_col[:, :1]
+    halo[...] = edge[:, : halo.shape[1]]
     for copy in copies:
         copy.wait()
 
 
-def gather_sends(table, basis, lists):
-    sides, cap = lists.shape
+def gather_sends(table, basis, lists, first, number, along):
+    cap = lists.shape[1]
     nx, ny, width = basis.shape
     shape = jax.ShapeDtypeStruct((cap,) + table.shape[1:], table.dtype)
-    some = min(8, ny)
-    return pl.pallas_call(
-        gather_kernel,
-        out_shape=[shape] * sides
-        + [
-            jax.ShapeDtypeStruct((1, ny, width), F32),
-            jax.ShapeDtypeStruct((nx, 1, width), F32),
-        ],
+    edge = (1, ny, width) if along == 0 else (nx, min(8, ny), width)
+    halo = (1, ny, width) if along == 0 else (nx, 1, width)
+
+    def kernel(*refs):
+        gather_kernel(*refs, first=first)
+
+    return pl.pallas_call(
+        kernel,
+        out_shape=[shape] * number + [jax.ShapeDtypeStruct(halo, F32)],
         grid_spec=pltpu.PrefetchScalarGridSpec(
             num_scalar_prefetch=1,
             grid=(1,),
             in_specs=[
                 pl.BlockSpec(memory_space=pltpu.HBM),
-                pl.BlockSpec((1, ny, width), lambda *_: (0, 0, 0)),
-                pl.BlockSpec((nx, some, width), lambda *_: (0, 0, 0)),
+                pl.BlockSpec(edge, lambda *_: (0, 0, 0)),
             ],
-            out_specs=[pl.BlockSpec(shape.shape, lambda *_: (0, 0, 0))] * sides
-            + [
-                pl.BlockSpec((1, ny, width), lambda *_: (0, 0, 0)),
-                pl.BlockSpec((nx, 1, width), lambda *_: (0, 0, 0)),
-            ],
-            scratch_shapes=[pltpu.SemaphoreType.DMA((sides, cap))],
+            out_specs=[pl.BlockSpec(shape.shape, lambda *_: (0, 0, 0))] * number
+            + [pl.BlockSpec(halo, lambda *_: (0, 0, 0))],
+            scratch_shapes=[pltpu.SemaphoreType.DMA((number, cap))],
         ),
-        name="gather_sends",
-    )(lists, table, basis, basis)
+    )(lists, table, basis)
 
 
 def in_vmem(value):
@@ -380,12 +374,12 @@
     return jnp.where(side_of(dims) == 0, low, high)
 
 
-CHUNKS = 3
+SHARES = (2, 2, 1)
 
 
 def chunk_sizes(terms):
-    base, extra = divmod(terms, CHUNKS)
-    return [n for n in (base + (k < extra) for k in range(CHUNKS)) if n]
+    ends = [terms * sum(SHARES[: k + 1]) // sum(SHARES) for k in range(len(SHARES))]
+    return [b - a for a, b in zip([0] + ends, ends)]
 
 
 def summed(keep, received, order):
@@ -401,7 +395,9 @@
 
 def body(die_basis, die_coeff, pkg_basis, send_blocks, columns, counts, pkg_blocks):
     lists = send_blocks[0]
-    *sends, row, col = gather_sends(pkg_basis, die_basis, lists)
+    *sends, row = gather_sends(pkg_basis, die_basis, lists, 0, 2, 0)
+    *more, col = gather_sends(pkg_basis, die_basis, lists, 2, 2, 1)
+    sends = sends + more
     next_x_row = from_behind(row, "gx", -1)
     next_y_col = from_behind(col, "gy", -1)
     ghosts = []
@@ -409,8 +405,9 @@
         ghosts.append(passed_along(sends[k], axis, steps))
     terms = columns.shape[0]
     entries = pkg_basis.shape[0] + lists.shape[0] * lists.shape[1]
-    high, low, turned = split_own(pkg_basis, entries)
     die = die_parts(die_basis, next_x_row, next_y_col, die_coeff)
+    owned, die = lax.optimization_barrier((pkg_basis, die))
+    high, low, turned = split_own(owned, entries)
     high, low = add_ghosts(high, low, ghosts)
     columns = columns.reshape(terms, -1)
     pair, *plane = bits("gy")

time: 186 us -> 190 us (1.022)
  local copies, waits for them, and re-layouts: 16.2 us -> 8.35 us
  waiting for transfers between devices: 60 us -> 67.8 us
  Pallas kernels: 70.3 us -> 75.1 us
    unnamed x43 -> x37, local copies, waits for them, and re-layouts: 16.1 us -> 8.25 us
    ppermute x2, waiting for transfers between devices: 13.4 us -> 21 us  [from_behind(): lax.ppermute(value, axis, [(source, source + steps) for source in range(l...]
    pallas_call x1 -> x2, Pallas kernels: 4.91 us -> 8.04 us  [gather_sends(): pl.pallas_call(kernel, out_shape=[shape] * number + [jax.ShapeDtypeStruct...]
  transfers between devices with their start and end apart: 36 -> 36, of which waited for: 17 -> 17; matrix products, arithmetic and copies ran while one was open for 3% -> 2% of each run, Pallas kernels for 23% -> 25%
where the time goes in v3:
time: 190 us
  Pallas kernels  75.1 us (40%)
  waiting for transfers between devices  67.8 us (36%)
  starting transfers between devices  33.4 us (18%)
  local copies, waits for them, and re-layouts  8.35 us (4%)
  other arithmetic  4.53 us (2%)
    pallas_call x3, Pallas kernels, project_terms(): pl.pallas_call(kernel, out_shape=[out, out], grid_spec=pltpu.PrefetchScal...  47.9 us
    ppermute x30, waiting for transfers between devices, flip(): return lax.ppermute(value, ('gx', 'gy'), pairs)  46.8 us
    ppermute x30, starting transfers between devices, flip(): return lax.ppermute(value, ('gx', 'gy'), pairs)  22.7 us
    ppermute x2, waiting for transfers between devices, from_behind(): lax.ppermute(value, axis, [(source, source + steps) for source in range(l...  21 us
    unnamed x37, local copies, waits for them, and re-layouts  8.25 us
    ppermute x4, starting transfers between devices, passed_along(): return lax.ppermute(value, axis, pairs)  8.1 us
    pallas_call x2, Pallas kernels, gather_sends(): pl.pallas_call(kernel, out_shape=[shape] * number + [jax.ShapeDtypeStruct...  8.04 us
    pallas_call x3, Pallas kernels, place(): pl.pallas_call(place_kernel, out_shape=jax.ShapeDtypeStruct((terms, 2 * h...  7.53 us
  transfers between devices with their start and end apart: 36, of which 17 were waited for; matrix products, arithmetic and copies ran while one was open for 2% of the time, Pallas kernels for 25%

profile of v3, /device:TPU:0, one launch (start us, length us, event | category | flops | bytes accessed | tf_op | source)
XLA Modules:
  0.0 189.7 jit_solution(9128656223463267004)
XLA Ops:
  0.0 4.1 %shard_map.74 = (f32[4,64,512]{2,1,0:T(8,128)}, f32[4,64,512]{2,1,0:T(8,128)}, f32[16,1,512]{2,1,0:T(1,128)}) custom-call(s32[4,4]{1,0:T(4,128)} %bitcast.88, f32[32,64,512]{2,1,0:T(8,128)} %owned, f32[16,32,512]{2,1,0:T(8,128)} %basis.1), custom_call_target="tpu_custom_call" | custom-call | tf_op jit(solution)/shard_map/pallas_call | solution.py:59
  5.4 3.9 %shard_map.73 = (f32[4,64,512]{2,1,0:T(8,128)}, f32[4,64,512]{2,1,0:T(8,128)}, f32[1,32,512]{2,1,0:T(8,128)}) custom-call(s32[4,4]{1,0:T(4,128)} %bitcast.89, f32[32,64,512]{2,1,0:T(8,128)} %owned, f32[16,32,512]{2,1,0:T(8,128)} %basis.1), custom_call_target="tpu_custom_call" | custom-call | tf_op jit(solution)/shard_map/pallas_call | solution.py:59
  9.4 3.1 %collective-permute-start.2 = (f32[4,64,512]{2,1,0:T(8,128)}, f32[4,64,512]{2,1,0:T(8,128)}, u32[]{:S(2)}, u32[]{:S(2)}) collective-permute-start(f32[4,64,512]{2,1,0:T(8,128)} %get-tuple-element.27), channel_id=1, source_target_pairs={{0,8},{8,16},{16,24},{24,0},{1,9},{9,17},{17,25},{25,1},{2,10},{10... | collective-permute-start | bytes 1572872 | tf_op jit(solution)/shard_map/ppermute | solution.py:23
  12.5 2.1 %collective-permute-start.3 = (f32[4,64,512]{2,1,0:T(8,128)}, f32[4,64,512]{2,1,0:T(8,128)}, u32[]{:S(2)}, u32[]{:S(2)}) collective-permute-start(f32[4,64,512]{2,1,0:T(8,128)} %get-tuple-element.28), channel_id=1, source_target_pairs={{0,24},{8,0},{16,8},{24,16},{1,25},{9,1},{17,9},{25,17},{2,26},{10... | collective-permute-start | bytes 1572872 | tf_op jit(solution)/shard_map/ppermute | solution.py:23
  15.4 2.1 %collective-permute-start.5 = (f32[4,64,512]{2,1,0:T(8,128)}, f32[4,64,512]{2,1,0:T(8,128)}, u32[]{:S(2)}, u32[]{:S(2)}) collective-permute-start(f32[4,64,512]{2,1,0:T(8,128)} %get-tuple-element.30), channel_id=1, source_target_pairs={{0,7},{1,0},{2,1},{3,2},{4,3},{5,4},{6,5},{7,6},{8,15},{9,8},{10,9... | collective-permute-start | bytes 1572872 | tf_op jit(solution)/shard_map/ppermute | solution.py:23
  19.0 21.0 %collective-permute-done.next_row = f32[1,32,512]{2,1,0:T(8,128)S(1)} collective-permute-done((f32[1,32,512]{2,1,0:T(8,128)}, f32[1,32,512]{2,1,0:T(8,128)S(1)}, u32[]{:S(2)}, u32[]{:S(2)}) %collective-permute-start) | collective-permute-done | bytes 65568 | tf_op jit(solution)/shard_map/ppermute | solution.py:17
  40.0 6.5 %die_parts.1.refs_3_ = f32[5,512,512]{2,1,0:T(8,128)S(1)} custom-call(f32[16,32,512]{2,1,0:T(8,128)S(1)} %copy-done.4, f32[1,32,512]{2,1,0:T(8,128)S(1)} %collective-permute-done.next_row, f32[16,1,512]{2,1,0:T(1,128)S(1)} %collective-permute-done.1.next_col, f32[5,16,32]{2,1,0:T(8,128)S(1)} %copy-done.12), custom_call_target="tpu_custom_call" | custom-call | flops 4831838208 | bytes 10485760 | tf_op jit(solution)/shard_map/die_parts/pallas_call | solution.py:183
  46.6 2.3 %copy-done.3 = f32[5,512,512]{2,1,0:T(8,128)} copy-done((f32[5,512,512]{2,1,0:T(8,128)}, f32[5,512,512]{2,1,0:T(8,128)S(1)}, u32[]{:S(2)}) %copy-start.3) | copy-done | bytes 5242904
  48.9 1.7 split_own.1
  50.7 3.4 %add_ghosts.1 = (bf16[48,64,512]{2,1,0:T(8,128)(2,1)S(1)}, bf16[48,64,512]{2,1,0:T(8,128)(2,1)S(1)}) custom-call(f32[4,64,512]{2,1,0:T(8,128)} %collective-permute-done.2.refs_0_, f32[4,64,512]{2,1,0:T(8,128)} %collective-permute-done.3.refs_1_, f32[4,64,512]{2,1,0:T(8,128)} %collective-permute-done.4.refs_2_, ...), custom_call_target="tpu_custom_call", output_to_operand_aliasing={{0}: (4, {}), {1}: (5, {})} | custom-call | tf_op jit(solution)/shard_map/add_ghosts/pallas_call | solution.py:129
  54.1 18.7 %shard_map.76 = (f32[2,256,512]{2,1,0:T(8,128)S(1)}, f32[2,256,512]{2,1,0:T(8,128)}) custom-call(s32[5,128]{1,0:T(8,128)S(1)} %reshape.217.refs_0_, s32[5,32]{1,0:T(8,128)S(1)} %copy-done.11, s32[1]{0:T(128)} %bitcast.refs_2_.core, f32[5,512,512]{2,1,0:T(8,128)} %copy-done.3, f32[5,32,64,256]{3,2,1,0:T(8,128)} %refs_4_.5, ...), custom_call_target="tpu_custom_call" | custom-call | flops 12884901888 | bytes 8388608 | tf_op jit(solution)/shard_map/pallas_call | solution.py:266
  73.8 18.2 %shard_map.77 = (f32[2,256,512]{2,1,0:T(8,128)S(1)}, f32[2,256,512]{2,1,0:T(8,128)}) custom-call(s32[5,128]{1,0:T(8,128)S(1)} %reshape.217.refs_0_, s32[5,32]{1,0:T(8,128)S(1)} %copy-done.11, s32[1]{0:T(128)} %bitcast.refs_2_.core, f32[5,512,512]{2,1,0:T(8,128)} %copy-done.3, f32[5,32,64,256]{3,2,1,0:T(8,128)} %refs_4_.5, ...), custom_call_target="tpu_custom_call" | custom-call | flops 12884901888 | bytes 8388608 | tf_op jit(solution)/shard_map/pallas_call | solution.py:266
  93.5 1.9 dynamic-slice_add_fusion.1
  96.9 1.7 dynamic-slice_add_fusion
  99.4 2.2 %copy-done.6 = bf16[8,512,512]{2,1,0:T(8,128)(2,1)S(1)} copy-done((bf16[8,512,512]{2,1,0:T(8,128)(2,1)S(1)}, bf16[8,512,512]{2,1,0:T(8,128)(2,1)}, u32[]{:S(2)}) %copy-start.6) | copy-done | bytes 4194328
  101.6 11.0 %shard_map.75 = (f32[1,256,512]{2,1,0:T(8,128)S(1)}, f32[1,256,512]{2,1,0:T(8,128)}) custom-call(s32[5,128]{1,0:T(8,128)S(1)} %reshape.217.refs_0_, s32[5,32]{1,0:T(8,128)S(1)} %copy-done.11, s32[1]{0:T(128)} %bitcast.refs_2_.core, f32[5,512,512]{2,1,0:T(8,128)} %copy-done.3, f32[5,32,64,256]{3,2,1,0:T(8,128)} %refs_4_.5, ...), custom_call_target="tpu_custom_call" | custom-call | flops 6442450944 | bytes 4194304 | tf_op jit(solution)/shard_map/pallas_call | solution.py:266
  115.8 4.2 %collective-permute-done.18 = f32[128,512]{1,0:T(8,128)S(1)} collective-permute-done((f32[128,512]{1,0:T(8,128)S(1)}, f32[128,512]{1,0:T(8,128)S(1)}, u32[]{:S(2)}, u32[]{:S(2)}) %collective-permute-start.18) | collective-permute-done | bytes 262176 | tf_op jit(solution)/shard_map/ppermute | solution.py:348
  129.9 1.9 %collective-permute-done.20 = f32[32,512]{1,0:T(8,128)S(1)} collective-permute-done((f32[32,512]{1,0:T(8,128)S(1)}, f32[32,512]{1,0:T(8,128)S(1)}, u32[]{:S(2)}, u32[]{:S(2)}) %collective-permute-start.20) | collective-permute-done | bytes 65568 | tf_op jit(solution)/shard_map/ppermute | solution.py:348
  132.4 2.1 %collective-permute-done.30 = f32[32,512]{1,0:T(8,128)S(1)} collective-permute-done((f32[32,512]{1,0:T(8,128)S(1)}, f32[32,512]{1,0:T(8,128)S(1)}, u32[]{:S(2)}, u32[]{:S(2)}) %collective-permute-start.30) | collective-permute-done | bytes 65568 | tf_op jit(solution)/shard_map/ppermute | solution.py:348
  135.2 4.8 %collective-permute-done.21 = f32[32,512]{1,0:T(8,128)S(1)} collective-permute-done((f32[32,512]{1,0:T(8,128)S(1)}, f32[32,512]{1,0:T(8,128)S(1)}, u32[]{:S(2)}, u32[]{:S(2)}) %collective-permute-start.21) | collective-permute-done | bytes 65568 | tf_op jit(solution)/shard_map/ppermute | solution.py:348
  141.0 1.8 collective-permute-done.31
  143.1 2.7 %collective-permute-done.22 = f32[64,512]{1,0:T(8,128)S(1)} collective-permute-done((f32[64,512]{1,0:T(8,128)S(1)}, f32[64,512]{1,0:T(8,128)S(1)}, u32[]{:S(2)}, u32[]{:S(2)}) %collective-permute-start.22) | collective-permute-done | bytes 131104 | tf_op jit(solution)/shard_map/ppermute | solution.py:348
  147.6 2.4 %collective-permute-done.32 = f32[64,512]{1,0:T(8,128)S(1)} collective-permute-done((f32[64,512]{1,0:T(8,128)S(1)}, f32[64,512]{1,0:T(8,128)S(1)}, u32[]{:S(2)}, u32[]{:S(2)}) %collective-permute-start.32) | collective-permute-done | bytes 131104 | tf_op jit(solution)/shard_map/ppermute | solution.py:348
  154.0 5.2 %collective-permute-done.33 = f32[128,512]{1,0:T(8,128)S(1)} collective-permute-done((f32[128,512]{1,0:T(8,128)S(1)}, f32[128,512]{1,0:T(8,128)S(1)}, u32[]{:S(2)}, u32[]{:S(2)}) %collective-permute-start.33) | collective-permute-done | bytes 262176 | tf_op jit(solution)/shard_map/ppermute | solution.py:348
  160.3 4.8 %collective-permute-done.11 = f32[16,512]{1,0:T(8,128)S(1)} collective-permute-done((f32[16,512]{1,0:T(8,128)S(1)}, f32[16,512]{1,0:T(8,128)S(1)}, u32[]{:S(2)}, u32[]{:S(2)}) %collective-permute-start.11) | collective-permute-done | bytes 32800 | tf_op jit(solution)/shard_map/ppermute | solution.py:348
  165.2 4.2 %collective-permute-done.12 = f32[32,512]{1,0:T(8,128)S(1)} collective-permute-done((f32[32,512]{1,0:T(8,128)S(1)}, f32[32,512]{1,0:T(8,128)S(1)}, u32[]{:S(2)}, u32[]{:S(2)}) %collective-permute-start.12) | collective-permute-done | bytes 65568 | tf_op jit(solution)/shard_map/ppermute | solution.py:348
  171.6 3.1 %collective-permute-done.13 = f32[64,512]{1,0:T(8,128)S(1)} collective-permute-done((f32[64,512]{1,0:T(8,128)S(1)}, f32[64,512]{1,0:T(8,128)S(1)}, u32[]{:S(2)}, u32[]{:S(2)}) %collective-permute-start.13) | collective-permute-done | bytes 131104 | tf_op jit(solution)/shard_map/ppermute | solution.py:348
  174.7 1.9 %collective-permute-start.14 = (f32[128,512]{1,0:T(8,128)S(1)}, f32[128,512]{1,0:T(8,128)S(1)}, u32[]{:S(2)}, u32[]{:S(2)}) collective-permute-start(f32[128,512]{1,0:T(8,128)S(1)} %maximum_select_fusion.5), channel_id=1, source_target_pairs={{0,2},{1,5},{2,0},{3,7},{4,6},{5,1},{6,4},{7,3},{8,10},{9,13},{10,... | collective-permute-start | bytes 786440 | tf_op jit(solution)/shard_map/ppermute | solution.py:348
  176.6 4.5 %collective-permute-done.14 = f32[128,512]{1,0:T(8,128)S(1)} collective-permute-done((f32[128,512]{1,0:T(8,128)S(1)}, f32[128,512]{1,0:T(8,128)S(1)}, u32[]{:S(2)}, u32[]{:S(2)}) %collective-permute-start.14) | collective-permute-done | bytes 262176 | tf_op jit(solution)/shard_map/ppermute | solution.py:348
  181.3 2.7 %shard_map.78.refs_0_ = f32[5,512,512]{2,1,0:T(8,128)} custom-call(s32[1]{0:T(128)} %bitcast.refs_2_.core, f32[2,256,512]{2,1,0:T(8,128)} %bitcast.60, f32[2,256,512]{2,1,0:T(8,128)} %collective-permute-done.35.other), custom_call_target="tpu_custom_call" | custom-call | tf_op jit(solution)/shard_map/pallas_call | solution.py:317
  184.0 2.6 %shard_map.79.refs_0_ = f32[5,512,512]{2,1,0:T(8,128)} custom-call(s32[1]{0:T(128)} %bitcast.refs_2_.core, f32[2,256,512]{2,1,0:T(8,128)} %bitcast.58, f32[2,256,512]{2,1,0:T(8,128)} %collective-permute-done.25.other, f32[5,512,512]{2,1,0:T(8,128)} %shard_map.78.refs_0_), custom_call_target="tpu_custom_call", output_to_operand_aliasing={{}: (3, {})} | custom-call | tf_op jit(solution)/shard_map/pallas_call | solution.py:317
  187.4 2.2 %shard_map.80 = f32[5,512,512]{2,1,0:T(8,128)} custom-call(s32[1]{0:T(128)} %bitcast.refs_2_.core, f32[1,256,512]{2,1,0:T(8,128)} %copy-done.15, f32[1,256,512]{2,1,0:T(8,128)} %copy-done.16, f32[5,512,512]{2,1,0:T(8,128)} %shard_map.79.refs_0_), custom_call_target="tpu_custom_call", output_to_operand_aliasing={{}: (3, {})} | custom-call | tf_op jit(solution)/shard_map/pallas_call | solution.py:317
  (116 shorter events, 33.9 us)
Async XLA Ops:
  4.1 13.3 %collective-permute-start.1 = (f32[16,1,512]{2,1,0:T(1,128)}, f32[16,1,512]{2,1,0:T(1,128)S(1)}, u32[]{:S(2)}, u32[]{:S(2)}) collective-permute-start(f32[16,1,512]{2,1,0:T(1,128)} %get-tuple-element.25), channel_id=1, source_target_pairs={{1,0},{2,1},{3,2},{4,3},{5,4},{6,5},{7,6},{9,8},{10,9},{11,10},{12... | collective-permute-start | bytes 98312 | tf_op jit(solution)/shard_map/ppermute | solution.py:17
  9.4 41.3 %collective-permute-start.2 = (f32[4,64,512]{2,1,0:T(8,128)}, f32[4,64,512]{2,1,0:T(8,128)}, u32[]{:S(2)}, u32[]{:S(2)}) collective-permute-start(f32[4,64,512]{2,1,0:T(8,128)} %get-tuple-element.27), channel_id=1, source_target_pairs={{0,8},{8,16},{16,24},{24,0},{1,9},{9,17},{17,25},{25,1},{2,10},{10... | collective-permute-start | bytes 1572872 | tf_op jit(solution)/shard_map/ppermute | solution.py:23
  12.5 38.2 %collective-permute-start.3 = (f32[4,64,512]{2,1,0:T(8,128)}, f32[4,64,512]{2,1,0:T(8,128)}, u32[]{:S(2)}, u32[]{:S(2)}) collective-permute-start(f32[4,64,512]{2,1,0:T(8,128)} %get-tuple-element.28), channel_id=1, source_target_pairs={{0,24},{8,0},{16,8},{24,16},{1,25},{9,1},{17,9},{25,17},{2,26},{10... | collective-permute-start | bytes 1572872 | tf_op jit(solution)/shard_map/ppermute | solution.py:23
  14.6 36.1 %collective-permute-start.4 = (f32[4,64,512]{2,1,0:T(8,128)}, f32[4,64,512]{2,1,0:T(8,128)}, u32[]{:S(2)}, u32[]{:S(2)}) collective-permute-start(f32[4,64,512]{2,1,0:T(8,128)} %get-tuple-element.29), channel_id=1, source_target_pairs={{0,1},{1,2},{2,3},{3,4},{4,5},{5,6},{6,7},{7,0},{8,9},{9,10},{10,1... | collective-permute-start | bytes 1572872 | tf_op jit(solution)/shard_map/ppermute | solution.py:23
  15.4 35.3 %collective-permute-start.5 = (f32[4,64,512]{2,1,0:T(8,128)}, f32[4,64,512]{2,1,0:T(8,128)}, u32[]{:S(2)}, u32[]{:S(2)}) collective-permute-start(f32[4,64,512]{2,1,0:T(8,128)} %get-tuple-element.30), channel_id=1, source_target_pairs={{0,7},{1,0},{2,1},{3,2},{4,3},{5,4},{6,5},{7,6},{8,15},{9,8},{10,9... | collective-permute-start | bytes 1572872 | tf_op jit(solution)/shard_map/ppermute | solution.py:23
  17.5 22.5 %collective-permute-start = (f32[1,32,512]{2,1,0:T(8,128)}, f32[1,32,512]{2,1,0:T(8,128)S(1)}, u32[]{:S(2)}, u32[]{:S(2)}) collective-permute-start(f32[1,32,512]{2,1,0:T(8,128)} %get-tuple-element.24), channel_id=1, source_target_pairs={{8,0},{16,8},{24,16},{9,1},{17,9},{25,17},{10,2},{18,10},{26,18},{... | collective-permute-start | bytes 196616 | tf_op jit(solution)/shard_map/ppermute | solution.py:17
  73.7 19.7 %collective-permute-start.16 = (f32[2,256,512]{2,1,0:T(8,128)}, f32[2,256,512]{2,1,0:T(8,128)}, u32[]{:S(2)}, u32[]{:S(2)}) collective-permute-start(f32[2,256,512]{2,1,0:T(8,128)} %get-tuple-element.40), channel_id=1, source_target_pairs={{0,1},{1,0},{2,3},{3,2},{4,5},{5,4},{6,7},{7,6},{8,9},{9,8},{10,11... | collective-permute-start | bytes 3145736 | tf_op jit(solution)/shard_map/ppermute | solution.py:348
  95.4 18.1 %collective-permute-start.17 = (f32[256,512]{1,0:T(8,128)S(1)}, f32[256,512]{1,0:T(8,128)S(1)}, u32[]{:S(2)}, u32[]{:S(2)}) collective-permute-start(f32[256,512]{1,0:T(8,128)S(1)} %get-tuple-element.46), channel_id=1, source_target_pairs={{0,2},{1,5},{2,0},{3,7},{4,6},{5,1},{6,4},{7,3},{8,10},{9,13},{10,... | collective-permute-start | bytes 1572872 | tf_op jit(solution)/shard_map/ppermute | solution.py:348
  98.6 16.4 %collective-permute-start.27 = (f32[256,512]{1,0:T(8,128)S(1)}, f32[256,512]{1,0:T(8,128)S(1)}, u32[]{:S(2)}, u32[]{:S(2)}) collective-permute-start(f32[256,512]{1,0:T(8,128)S(1)} %get-tuple-element.44), channel_id=1, source_target_pairs={{0,2},{1,5},{2,0},{3,7},{4,6},{5,1},{6,4},{7,3},{8,10},{9,13},{10,... | collective-permute-start | bytes 1572872 | tf_op jit(solution)/shard_map/ppermute | solution.py:348
  113.3 10.7 %collective-permute-start.6 = (f32[1,256,512]{2,1,0:T(8,128)}, f32[1,256,512]{2,1,0:T(8,128)S(1)}, u32[]{:S(2)}, u32[]{:S(2)}) collective-permute-start(f32[1,256,512]{2,1,0:T(8,128)} %get-tuple-element.38), channel_id=1, source_target_pairs={{0,1},{1,0},{2,3},{3,2},{4,5},{5,4},{6,7},{7,6},{8,9},{9,8},{10,11... | collective-permute-start | bytes 1572872 | tf_op jit(solution)/shard_map/ppermute | solution.py:348
  113.5 6.4 %collective-permute-start.18 = (f32[128,512]{1,0:T(8,128)S(1)}, f32[128,512]{1,0:T(8,128)S(1)}, u32[]{:S(2)}, u32[]{:S(2)}) collective-permute-start(f32[128,512]{1,0:T(8,128)S(1)} %get-tuple-element.50), channel_id=1, source_target_pairs={{0,4},{1,9},{2,6},{3,11},{4,0},{5,13},{6,2},{7,15},{8,12},{9,1},{1... | collective-permute-start | bytes 786440 | tf_op jit(solution)/shard_map/ppermute | solution.py:348
  115.1 7.7 %collective-permute-start.28 = (f32[128,512]{1,0:T(8,128)S(1)}, f32[128,512]{1,0:T(8,128)S(1)}, u32[]{:S(2)}, u32[]{:S(2)}) collective-permute-start(f32[128,512]{1,0:T(8,128)S(1)} %get-tuple-element.48), channel_id=1, source_target_pairs={{0,4},{1,9},{2,6},{3,11},{4,0},{5,13},{6,2},{7,15},{8,12},{9,1},{1... | collective-permute-start | bytes 786440 | tf_op jit(solution)/shard_map/ppermute | solution.py:348
  120.0 5.9 %collective-permute-start.19 = (f32[64,512]{1,0:T(8,128)S(1)}, f32[64,512]{1,0:T(8,128)S(1)}, u32[]{:S(2)}, u32[]{:S(2)}) collective-permute-start(f32[64,512]{1,0:T(8,128)S(1)} %get-tuple-element.56), channel_id=1, source_target_pairs={{0,8},{1,17},{2,10},{3,19},{4,12},{5,21},{6,14},{7,23},{8,0},{9,25... | collective-permute-start | bytes 393224 | tf_op jit(solution)/shard_map/ppermute | solution.py:348
  122.8 5.9 %collective-permute-start.29 = (f32[64,512]{1,0:T(8,128)S(1)}, f32[64,512]{1,0:T(8,128)S(1)}, u32[]{:S(2)}, u32[]{:S(2)}) collective-permute-start(f32[64,512]{1,0:T(8,128)S(1)} %get-tuple-element.54), channel_id=1, source_target_pairs={{0,8},{1,17},{2,10},{3,19},{4,12},{5,21},{6,14},{7,23},{8,0},{9,25... | collective-permute-start | bytes 393224 | tf_op jit(solution)/shard_map/ppermute | solution.py:348
  124.1 16.0 %collective-permute-start.7 = (f32[128,512]{1,0:T(8,128)S(1)}, f32[128,512]{1,0:T(8,128)S(1)}, u32[]{:S(2)}, u32[]{:S(2)}) collective-permute-start(f32[128,512]{1,0:T(8,128)S(1)} %get-tuple-element.52), channel_id=1, source_target_pairs={{0,2},{1,5},{2,0},{3,7},{4,6},{5,1},{6,4},{7,3},{8,10},{9,13},{10,... | collective-permute-start | bytes 786440 | tf_op jit(solution)/shard_map/ppermute | solution.py:348
  125.9 5.9 %collective-permute-start.20 = (f32[32,512]{1,0:T(8,128)S(1)}, f32[32,512]{1,0:T(8,128)S(1)}, u32[]{:S(2)}, u32[]{:S(2)}) collective-permute-start(f32[32,512]{1,0:T(8,128)S(1)} %add_bitcast_fusion.9), channel_id=1, source_target_pairs={{0,16},{1,3},{2,18},{3,1},{4,20},{5,7},{6,22},{7,5},{8,24},{9,11},... | collective-permute-start | bytes 196616 | tf_op jit(solution)/shard_map/ppermute | solution.py:348
  128.7 5.8 %collective-permute-start.30 = (f32[32,512]{1,0:T(8,128)S(1)}, f32[32,512]{1,0:T(8,128)S(1)}, u32[]{:S(2)}, u32[]{:S(2)}) collective-permute-start(f32[32,512]{1,0:T(8,128)S(1)} %add_bitcast_fusion.8), channel_id=1, source_target_pairs={{0,16},{1,3},{2,18},{3,1},{4,20},{5,7},{6,22},{7,5},{8,24},{9,11},... | collective-permute-start | bytes 196616 | tf_op jit(solution)/shard_map/ppermute | solution.py:348
  131.9 8.1 %collective-permute-start.21 = (f32[32,512]{1,0:T(8,128)S(1)}, f32[32,512]{1,0:T(8,128)S(1)}, u32[]{:S(2)}, u32[]{:S(2)}) collective-permute-start(f32[32,512]{1,0:T(8,128)S(1)} %bitcast_add_fusion.1), channel_id=1, source_target_pairs={{0,16},{1,3},{2,18},{3,1},{4,20},{5,7},{6,22},{7,5},{8,24},{9,11},... | collective-permute-start | bytes 196616 | tf_op jit(solution)/shard_map/ppermute | solution.py:348
  134.5 8.3 %collective-permute-start.31 = (f32[32,512]{1,0:T(8,128)S(1)}, f32[32,512]{1,0:T(8,128)S(1)}, u32[]{:S(2)}, u32[]{:S(2)}) collective-permute-start(f32[32,512]{1,0:T(8,128)S(1)} %bitcast_add_fusion), channel_id=1, source_target_pairs={{0,16},{1,3},{2,18},{3,1},{4,20},{5,7},{6,22},{7,5},{8,24},{9,11},... | collective-permute-start | bytes 196616 | tf_op jit(solution)/shard_map/ppermute | solution.py:348
  140.0 5.8 %collective-permute-start.22 = (f32[64,512]{1,0:T(8,128)S(1)}, f32[64,512]{1,0:T(8,128)S(1)}, u32[]{:S(2)}, u32[]{:S(2)}) collective-permute-start(f32[64,512]{1,0:T(8,128)S(1)} %maximum_select_fusion.9), channel_id=1, source_target_pairs={{0,8},{1,17},{2,10},{3,19},{4,12},{5,21},{6,14},{7,23},{8,0},{9,25... | collective-permute-start | bytes 393224 | tf_op jit(solution)/shard_map/ppermute | solution.py:348
  140.2 7.3 %collective-permute-start.8 = (f32[64,512]{1,0:T(8,128)S(1)}, f32[64,512]{1,0:T(8,128)S(1)}, u32[]{:S(2)}, u32[]{:S(2)}) collective-permute-start(f32[64,512]{1,0:T(8,128)S(1)} %get-tuple-element.58), channel_id=1, source_target_pairs={{0,4},{1,9},{2,6},{3,11},{4,0},{5,13},{6,2},{7,15},{8,12},{9,1},{1... | collective-permute-start | bytes 393224 | tf_op jit(solution)/shard_map/ppermute | solution.py:348
  142.8 7.1 %collective-permute-start.32 = (f32[64,512]{1,0:T(8,128)S(1)}, f32[64,512]{1,0:T(8,128)S(1)}, u32[]{:S(2)}, u32[]{:S(2)}) collective-permute-start(f32[64,512]{1,0:T(8,128)S(1)} %maximum_select_fusion.10), channel_id=1, source_target_pairs={{0,8},{1,17},{2,10},{3,19},{4,12},{5,21},{6,14},{7,23},{8,0},{9,25... | collective-permute-start | bytes 393224 | tf_op jit(solution)/shard_map/ppermute | solution.py:348
  145.9 6.7 %collective-permute-start.23 = (f32[128,512]{1,0:T(8,128)S(1)}, f32[128,512]{1,0:T(8,128)S(1)}, u32[]{:S(2)}, u32[]{:S(2)}) collective-permute-start(f32[128,512]{1,0:T(8,128)S(1)} %maximum_select_fusion.6), channel_id=1, source_target_pairs={{0,4},{1,9},{2,6},{3,11},{4,0},{5,13},{6,2},{7,15},{8,12},{9,1},{1... | collective-permute-start | bytes 786440 | tf_op jit(solution)/shard_map/ppermute | solution.py:348
  150.0 9.2 %collective-permute-start.33 = (f32[128,512]{1,0:T(8,128)S(1)}, f32[128,512]{1,0:T(8,128)S(1)}, u32[]{:S(2)}, u32[]{:S(2)}) collective-permute-start(f32[128,512]{1,0:T(8,128)S(1)} %maximum_select_fusion.7), channel_id=1, source_target_pairs={{0,4},{1,9},{2,6},{3,11},{4,0},{5,13},{6,2},{7,15},{8,12},{9,1},{1... | collective-permute-start | bytes 786440 | tf_op jit(solution)/shard_map/ppermute | solution.py:348
  152.5 7.7 %collective-permute-start.10 = (f32[16,512]{1,0:T(8,128)S(1)}, f32[16,512]{1,0:T(8,128)S(1)}, u32[]{:S(2)}, u32[]{:S(2)}) collective-permute-start(f32[16,512]{1,0:T(8,128)S(1)} %add_bitcast_fusion.11), channel_id=1, source_target_pairs={{0,16},{1,3},{2,18},{3,1},{4,20},{5,7},{6,22},{7,5},{8,24},{9,11},... | collective-permute-start | bytes 98312 | tf_op jit(solution)/shard_map/ppermute | solution.py:348
  152.6 18.3 %collective-permute-start.24 = (f32[256,512]{1,0:T(8,128)S(1)}, f32[256,512]{1,0:T(8,128)S(1)}, u32[]{:S(2)}, u32[]{:S(2)}) collective-permute-start(f32[256,512]{1,0:T(8,128)S(1)} %maximum_select_fusion.3), channel_id=1, source_target_pairs={{0,2},{1,5},{2,0},{3,7},{4,6},{5,1},{6,4},{7,3},{8,10},{9,13},{10,... | collective-permute-start | bytes 1572872 | tf_op jit(solution)/shard_map/ppermute | solution.py:348
  159.3 11.3 %collective-permute-start.34 = (f32[256,512]{1,0:T(8,128)S(1)}, f32[256,512]{1,0:T(8,128)S(1)}, u32[]{:S(2)}, u32[]{:S(2)}) collective-permute-start(f32[256,512]{1,0:T(8,128)S(1)} %maximum_select_fusion.4), channel_id=1, source_target_pairs={{0,2},{1,5},{2,0},{3,7},{4,6},{5,1},{6,4},{7,3},{8,10},{9,13},{10,... | collective-permute-start | bytes 1572872 | tf_op jit(solution)/shard_map/ppermute | solution.py:348
  169.4 5.2 %collective-permute-start.13 = (f32[64,512]{1,0:T(8,128)S(1)}, f32[64,512]{1,0:T(8,128)S(1)}, u32[]{:S(2)}, u32[]{:S(2)}) collective-permute-start(f32[64,512]{1,0:T(8,128)S(1)} %maximum_select_fusion.8), channel_id=1, source_target_pairs={{0,4},{1,9},{2,6},{3,11},{4,0},{5,13},{6,2},{7,15},{8,12},{9,1},{1... | collective-permute-start | bytes 393224 | tf_op jit(solution)/shard_map/ppermute | solution.py:348
  170.8 10.5 %collective-permute-start.35 = (f32[2,256,512]{2,1,0:T(8,128)S(1)}, f32[2,256,512]{2,1,0:T(8,128)}, u32[]{:S(2)}, u32[]{:S(2)}) collective-permute-start(f32[2,256,512]{2,1,0:T(8,128)S(1)} %bitcast.59), channel_id=1, source_target_pairs={{0,1},{1,0},{2,3},{3,2},{4,5},{5,4},{6,7},{7,6},{8,9},{9,8},{10,11... | collective-permute-start | bytes 3145736 | tf_op jit(solution)/shard_map/ppermute | solution.py:348
  171.0 13.0 %collective-permute-start.25 = (f32[2,256,512]{2,1,0:T(8,128)S(1)}, f32[2,256,512]{2,1,0:T(8,128)}, u32[]{:S(2)}, u32[]{:S(2)}) collective-permute-start(f32[2,256,512]{2,1,0:T(8,128)S(1)} %bitcast.57), channel_id=1, source_target_pairs={{0,1},{1,0},{2,3},{3,2},{4,5},{5,4},{6,7},{7,6},{8,9},{9,8},{10,11... | collective-permute-start | bytes 3145736 | tf_op jit(solution)/shard_map/ppermute | solution.py:348
  174.7 6.4 %collective-permute-start.14 = (f32[128,512]{1,0:T(8,128)S(1)}, f32[128,512]{1,0:T(8,128)S(1)}, u32[]{:S(2)}, u32[]{:S(2)}) collective-permute-start(f32[128,512]{1,0:T(8,128)S(1)} %maximum_select_fusion.5), channel_id=1, source_target_pairs={{0,2},{1,5},{2,0},{3,7},{4,6},{5,1},{6,4},{7,3},{8,10},{9,13},{10,... | collective-permute-start | bytes 786440 | tf_op jit(solution)/shard_map/ppermute | solution.py:348
  181.2 5.4 %collective-permute-start.15 = (f32[1,256,512]{2,1,0:T(8,128)S(1)}, f32[1,256,512]{2,1,0:T(8,128)S(1)}, u32[]{:S(2)}, u32[]{:S(2)}) collective-permute-start(f32[1,256,512]{2,1,0:T(8,128)S(1)} %maximum_select_fusion.2.mine), channel_id=1, source_target_pairs={{0,1},{1,0},{2,3},{3,2},{4,5},{5,4},{6,7},{7,6},{8,9},{9,8},{10,11... | collective-permute-start | bytes 1572872 | tf_op jit(solution)/shard_map/ppermute | solution.py:348
  (22 other events, 246.7 us)

commit v4 on v3

--- a/solution.py
+++ b/solution.py
@@ -298,21 +298,21 @@
 def place_kernel(core, mine, other, *refs):
     out = refs[-1]
     half = mine.shape[1]
+    at = pl.program_id(0)
 
     @pl.when(core[0] == 0)
     def _():
-        out[0, :half] = mine[0]
-        out[0, half:] = other[0]
+        out[0, :half] = mine[at]
+        out[0, half:] = other[at]
 
     @pl.when(core[0] == 1)
     def _():
-        out[0, :half] = other[0]
-        out[0, half:] = mine[0]
+        out[0, :half] = other[at]
+        out[0, half:] = mine[at]
 
 
 def place(core, mine, other, first, terms, filled):
     number, half, width = mine.shape
-    spec = pl.BlockSpec((1, half, width), lambda i, *_: (i, 0, 0))
     extra = [] if filled is None else [filled]
     return pl.pallas_call(
         place_kernel,
@@ -320,11 +320,12 @@
         grid_spec=pltpu.PrefetchScalarGridSpec(
             num_scalar_prefetch=1,
             grid=(number,),
-            in_specs=[spec, spec] + [pl.BlockSpec(memory_space=pl.ANY)] * len(extra),
+            in_specs=[VMEM_SPEC, VMEM_SPEC] + [pl.BlockSpec(memory_space=pl.ANY)] * len(extra),
             out_specs=pl.BlockSpec((1, 2 * half, width), lambda i, *_: (first + i, 0, 0)),
         ),
         input_output_aliases={3: 0} if extra else {},
-    )(core, mine, other, *extra)
+        compiler_params=pltpu.CompilerParams(vmem_limit_bytes=16 << 20),
+    )(core, in_vmem(mine), in_vmem(other), *extra)
 
 
 def bits(axis):

time: 190 us -> 186 us (0.979)
  Pallas kernels: 75.1 us -> 71.4 us
    pallas_call x3, Pallas kernels: 7.53 us -> 3.86 us  [place(): pl.pallas_call(place_kernel, out_shape=jax.ShapeDtypeStruct((terms, 2 * h...]
    unnamed x37 -> x29, local copies, waits for them, and re-layouts: 8.25 us -> 7.42 us
  transfers between devices with their start and end apart: 36 -> 36, of which waited for: 17 -> 18; matrix products, arithmetic and copies ran while one was open for 2% -> 3% of each run, Pallas kernels for 25% -> 24%
where the time goes in v4:
time: 186 us
  Pallas kernels  71.4 us (38%)
  waiting for transfers between devices  68.9 us (37%)
  starting transfers between devices  32.9 us (18%)
  local copies, waits for them, and re-layouts  7.53 us (4%)
  other arithmetic  4.48 us (2%)
    ppermute x30, waiting for transfers between devices, flip(): return lax.ppermute(value, ('gx', 'gy'), pairs)  47.9 us
    pallas_call x3, Pallas kernels, project_terms(): pl.pallas_call(kernel, out_shape=[out, out], grid_spec=pltpu.PrefetchScal...  47.9 us
    ppermute x30, starting transfers between devices, flip(): return lax.ppermute(value, ('gx', 'gy'), pairs)  22.2 us
    ppermute x2, waiting for transfers between devices, from_behind(): lax.ppermute(value, axis, [(source, source + steps) for source in range(l...  21 us
    ppermute x4, starting transfers between devices, passed_along(): return lax.ppermute(value, axis, pairs)  8.1 us
    pallas_call x2, Pallas kernels, gather_sends(): pl.pallas_call(kernel, out_shape=[shape] * number + [jax.ShapeDtypeStruct...  8.05 us
    unnamed x29, local copies, waits for them, and re-layouts  7.42 us
    pallas_call x1, Pallas kernels, die_parts(): pl.pallas_call(die_kernel, out_shape=jax.ShapeDtypeStruct((terms, width,...  6.54 us
  transfers between devices with their start and end apart: 36, of which 18 were waited for; matrix products, arithmetic and copies ran while one was open for 3% of the time, Pallas kernels for 24%

profile of v4, /device:TPU:0, one launch (start us, length us, event | category | flops | bytes accessed | tf_op | source)
XLA Modules:
  0.0 185.7 jit_solution(15721042169414313998)
XLA Ops:
  0.0 4.1 %shard_map.74 = (f32[4,64,512]{2,1,0:T(8,128)}, f32[4,64,512]{2,1,0:T(8,128)}, f32[16,1,512]{2,1,0:T(1,128)}) custom-call(s32[4,4]{1,0:T(4,128)} %bitcast.88, f32[32,64,512]{2,1,0:T(8,128)} %owned, f32[16,32,512]{2,1,0:T(8,128)} %basis.1), custom_call_target="tpu_custom_call" | custom-call | tf_op jit(solution)/shard_map/pallas_call | solution.py:59
  5.4 3.9 %shard_map.73 = (f32[4,64,512]{2,1,0:T(8,128)}, f32[4,64,512]{2,1,0:T(8,128)}, f32[1,32,512]{2,1,0:T(8,128)}) custom-call(s32[4,4]{1,0:T(4,128)} %bitcast.89, f32[32,64,512]{2,1,0:T(8,128)} %owned, f32[16,32,512]{2,1,0:T(8,128)} %basis.1), custom_call_target="tpu_custom_call" | custom-call | tf_op jit(solution)/shard_map/pallas_call | solution.py:59
  9.4 3.1 %collective-permute-start.2 = (f32[4,64,512]{2,1,0:T(8,128)}, f32[4,64,512]{2,1,0:T(8,128)}, u32[]{:S(2)}, u32[]{:S(2)}) collective-permute-start(f32[4,64,512]{2,1,0:T(8,128)} %get-tuple-element.27), channel_id=1, source_target_pairs={{0,8},{8,16},{16,24},{24,0},{1,9},{9,17},{17,25},{25,1},{2,10},{10... | collective-permute-start | bytes 1572872 | tf_op jit(solution)/shard_map/ppermute | solution.py:23
  12.5 2.1 %collective-permute-start.3 = (f32[4,64,512]{2,1,0:T(8,128)}, f32[4,64,512]{2,1,0:T(8,128)}, u32[]{:S(2)}, u32[]{:S(2)}) collective-permute-start(f32[4,64,512]{2,1,0:T(8,128)} %get-tuple-element.28), channel_id=1, source_target_pairs={{0,24},{8,0},{16,8},{24,16},{1,25},{9,1},{17,9},{25,17},{2,26},{10... | collective-permute-start | bytes 1572872 | tf_op jit(solution)/shard_map/ppermute | solution.py:23
  15.4 2.1 %collective-permute-start.5 = (f32[4,64,512]{2,1,0:T(8,128)}, f32[4,64,512]{2,1,0:T(8,128)}, u32[]{:S(2)}, u32[]{:S(2)}) collective-permute-start(f32[4,64,512]{2,1,0:T(8,128)} %get-tuple-element.30), channel_id=1, source_target_pairs={{0,7},{1,0},{2,1},{3,2},{4,3},{5,4},{6,5},{7,6},{8,15},{9,8},{10,9... | collective-permute-start | bytes 1572872 | tf_op jit(solution)/shard_map/ppermute | solution.py:23
  19.0 21.0 %collective-permute-done.next_row = f32[1,32,512]{2,1,0:T(8,128)S(1)} collective-permute-done((f32[1,32,512]{2,1,0:T(8,128)}, f32[1,32,512]{2,1,0:T(8,128)S(1)}, u32[]{:S(2)}, u32[]{:S(2)}) %collective-permute-start) | collective-permute-done | bytes 65568 | tf_op jit(solution)/shard_map/ppermute | solution.py:17
  40.0 6.5 %die_parts.1.refs_3_ = f32[5,512,512]{2,1,0:T(8,128)S(1)} custom-call(f32[16,32,512]{2,1,0:T(8,128)S(1)} %copy-done.4, f32[1,32,512]{2,1,0:T(8,128)S(1)} %collective-permute-done.next_row, f32[16,1,512]{2,1,0:T(1,128)S(1)} %collective-permute-done.1.next_col, f32[5,16,32]{2,1,0:T(8,128)S(1)} %copy-done.12), custom_call_target="tpu_custom_call" | custom-call | flops 4831838208 | bytes 10485760 | tf_op jit(solution)/shard_map/die_parts/pallas_call | solution.py:183
  46.6 2.3 %copy-done.3 = f32[5,512,512]{2,1,0:T(8,128)} copy-done((f32[5,512,512]{2,1,0:T(8,128)}, f32[5,512,512]{2,1,0:T(8,128)S(1)}, u32[]{:S(2)}) %copy-start.3) | copy-done | bytes 5242904
  48.9 1.7 split_own.1
  50.7 3.4 %add_ghosts.1 = (bf16[48,64,512]{2,1,0:T(8,128)(2,1)S(1)}, bf16[48,64,512]{2,1,0:T(8,128)(2,1)S(1)}) custom-call(f32[4,64,512]{2,1,0:T(8,128)} %collective-permute-done.2.refs_0_, f32[4,64,512]{2,1,0:T(8,128)} %collective-permute-done.3.refs_1_, f32[4,64,512]{2,1,0:T(8,128)} %collective-permute-done.4.refs_2_, ...), custom_call_target="tpu_custom_call", output_to_operand_aliasing={{0}: (4, {}), {1}: (5, {})} | custom-call | tf_op jit(solution)/shard_map/add_ghosts/pallas_call | solution.py:129
  54.1 18.7 %shard_map.76 = (f32[2,256,512]{2,1,0:T(8,128)S(1)}, f32[2,256,512]{2,1,0:T(8,128)}) custom-call(s32[5,128]{1,0:T(8,128)S(1)} %reshape.217.refs_0_, s32[5,32]{1,0:T(8,128)S(1)} %copy-done.11, s32[1]{0:T(128)} %bitcast.refs_2_.core, f32[5,512,512]{2,1,0:T(8,128)} %copy-done.3, f32[5,32,64,256]{3,2,1,0:T(8,128)} %refs_4_.5, ...), custom_call_target="tpu_custom_call" | custom-call | flops 12884901888 | bytes 8388608 | tf_op jit(solution)/shard_map/pallas_call | solution.py:266
  73.8 18.2 %shard_map.77 = (f32[2,256,512]{2,1,0:T(8,128)S(1)}, f32[2,256,512]{2,1,0:T(8,128)}) custom-call(s32[5,128]{1,0:T(8,128)S(1)} %reshape.217.refs_0_, s32[5,32]{1,0:T(8,128)S(1)} %copy-done.11, s32[1]{0:T(128)} %bitcast.refs_2_.core, f32[5,512,512]{2,1,0:T(8,128)} %copy-done.3, f32[5,32,64,256]{3,2,1,0:T(8,128)} %refs_4_.5, ...), custom_call_target="tpu_custom_call" | custom-call | flops 12884901888 | bytes 8388608 | tf_op jit(solution)/shard_map/pallas_call | solution.py:266
  93.5 1.9 %dynamic-slice_add_fusion.1 = (f32[1,256,512]{2,1,0:T(8,128)S(1)}, f32[256,512]{1,0:T(8,128)S(1)}) fusion(f32[2,256,512]{2,1,0:T(8,128)} %collective-permute-done.16, s32[]{:T(128)S(6)} %select_n.430, f32[2,256,512]{2,1,0:T(8,128)} %copy-done.8, s32[]{:T(128)S(6)} %select_n.432), kind=kLoop, calls=%fused_computation.8 | loop fusion | flops 262144 | bytes 3145736 | tf_op jit(solution)/shard_map/add | solution.py:366
  95.4 1.6 collective-permute-start.17
  96.9 1.7 dynamic-slice_add_fusion
  99.4 2.2 %copy-done.6 = bf16[8,512,512]{2,1,0:T(8,128)(2,1)S(1)} copy-done((bf16[8,512,512]{2,1,0:T(8,128)(2,1)S(1)}, bf16[8,512,512]{2,1,0:T(8,128)(2,1)}, u32[]{:S(2)}) %copy-start.6) | copy-done | bytes 4194328
  101.6 11.0 %shard_map.75 = (f32[1,256,512]{2,1,0:T(8,128)S(1)}, f32[1,256,512]{2,1,0:T(8,128)}) custom-call(s32[5,128]{1,0:T(8,128)S(1)} %reshape.217.refs_0_, s32[5,32]{1,0:T(8,128)S(1)} %copy-done.11, s32[1]{0:T(128)} %bitcast.refs_2_.core, f32[5,512,512]{2,1,0:T(8,128)} %copy-done.3, f32[5,32,64,256]{3,2,1,0:T(8,128)} %refs_4_.5, ...), custom_call_target="tpu_custom_call" | custom-call | flops 6442450944 | bytes 4194304 | tf_op jit(solution)/shard_map/pallas_call | solution.py:266
  115.8 4.2 %collective-permute-done.18 = f32[128,512]{1,0:T(8,128)S(1)} collective-permute-done((f32[128,512]{1,0:T(8,128)S(1)}, f32[128,512]{1,0:T(8,128)S(1)}, u32[]{:S(2)}, u32[]{:S(2)}) %collective-permute-start.18) | collective-permute-done | bytes 262176 | tf_op jit(solution)/shard_map/ppermute | solution.py:349
  121.2 1.6 collective-permute-done.28
  127.2 1.6 collective-permute-done.29
  130.0 1.9 %collective-permute-done.20 = f32[32,512]{1,0:T(8,128)S(1)} collective-permute-done((f32[32,512]{1,0:T(8,128)S(1)}, f32[32,512]{1,0:T(8,128)S(1)}, u32[]{:S(2)}, u32[]{:S(2)}) %collective-permute-start.20) | collective-permute-done | bytes 65568 | tf_op jit(solution)/shard_map/ppermute | solution.py:349
  132.4 2.1 %collective-permute-done.30 = f32[32,512]{1,0:T(8,128)S(1)} collective-permute-done((f32[32,512]{1,0:T(8,128)S(1)}, f32[32,512]{1,0:T(8,128)S(1)}, u32[]{:S(2)}, u32[]{:S(2)}) %collective-permute-start.30) | collective-permute-done | bytes 65568 | tf_op jit(solution)/shard_map/ppermute | solution.py:349
  135.2 4.4 %collective-permute-done.21 = f32[32,512]{1,0:T(8,128)S(1)} collective-permute-done((f32[32,512]{1,0:T(8,128)S(1)}, f32[32,512]{1,0:T(8,128)S(1)}, u32[]{:S(2)}, u32[]{:S(2)}) %collective-permute-start.21) | collective-permute-done | bytes 65568 | tf_op jit(solution)/shard_map/ppermute | solution.py:349
  141.4 1.7 collective-permute-start.32
  143.1 3.9 %collective-permute-done.22 = f32[64,512]{1,0:T(8,128)S(1)} collective-permute-done((f32[64,512]{1,0:T(8,128)S(1)}, f32[64,512]{1,0:T(8,128)S(1)}, u32[]{:S(2)}, u32[]{:S(2)}) %collective-permute-start.22) | collective-permute-done | bytes 131104 | tf_op jit(solution)/shard_map/ppermute | solution.py:349
  147.6 2.3 %collective-permute-done.32 = f32[64,512]{1,0:T(8,128)S(1)} collective-permute-done((f32[64,512]{1,0:T(8,128)S(1)}, f32[64,512]{1,0:T(8,128)S(1)}, u32[]{:S(2)}, u32[]{:S(2)}) %collective-permute-start.32) | collective-permute-done | bytes 131104 | tf_op jit(solution)/shard_map/ppermute | solution.py:349
  154.2 5.5 %collective-permute-done.33 = f32[128,512]{1,0:T(8,128)S(1)} collective-permute-done((f32[128,512]{1,0:T(8,128)S(1)}, f32[128,512]{1,0:T(8,128)S(1)}, u32[]{:S(2)}, u32[]{:S(2)}) %collective-permute-start.33) | collective-permute-done | bytes 262176 | tf_op jit(solution)/shard_map/ppermute | solution.py:349
  160.4 4.8 %collective-permute-done.11 = f32[16,512]{1,0:T(8,128)S(1)} collective-permute-done((f32[16,512]{1,0:T(8,128)S(1)}, f32[16,512]{1,0:T(8,128)S(1)}, u32[]{:S(2)}, u32[]{:S(2)}) %collective-permute-start.11) | collective-permute-done | bytes 32800 | tf_op jit(solution)/shard_map/ppermute | solution.py:349
  165.2 4.2 %collective-permute-done.12 = f32[32,512]{1,0:T(8,128)S(1)} collective-permute-done((f32[32,512]{1,0:T(8,128)S(1)}, f32[32,512]{1,0:T(8,128)S(1)}, u32[]{:S(2)}, u32[]{:S(2)}) %collective-permute-start.12) | collective-permute-done | bytes 65568 | tf_op jit(solution)/shard_map/ppermute | solution.py:349
  171.5 3.3 %collective-permute-done.13 = f32[64,512]{1,0:T(8,128)S(1)} collective-permute-done((f32[64,512]{1,0:T(8,128)S(1)}, f32[64,512]{1,0:T(8,128)S(1)}, u32[]{:S(2)}, u32[]{:S(2)}) %collective-permute-start.13) | collective-permute-done | bytes 131104 | tf_op jit(solution)/shard_map/ppermute | solution.py:349
  174.9 2.5 %collective-permute-start.14 = (f32[128,512]{1,0:T(8,128)S(1)}, f32[128,512]{1,0:T(8,128)S(1)}, u32[]{:S(2)}, u32[]{:S(2)}) collective-permute-start(f32[128,512]{1,0:T(8,128)S(1)} %maximum_select_fusion.5), channel_id=1, source_target_pairs={{0,2},{1,5},{2,0},{3,7},{4,6},{5,1},{6,4},{7,3},{8,10},{9,13},{10,... | collective-permute-start | bytes 786440 | tf_op jit(solution)/shard_map/ppermute | solution.py:349
  177.3 4.4 %collective-permute-done.14 = f32[128,512]{1,0:T(8,128)S(1)} collective-permute-done((f32[128,512]{1,0:T(8,128)S(1)}, f32[128,512]{1,0:T(8,128)S(1)}, u32[]{:S(2)}, u32[]{:S(2)}) %collective-permute-start.14) | collective-permute-done | bytes 262176 | tf_op jit(solution)/shard_map/ppermute | solution.py:349
  (108 shorter events, 31.4 us)
Async XLA Ops:
  4.1 13.3 %collective-permute-start.1 = (f32[16,1,512]{2,1,0:T(1,128)}, f32[16,1,512]{2,1,0:T(1,128)S(1)}, u32[]{:S(2)}, u32[]{:S(2)}) collective-permute-start(f32[16,1,512]{2,1,0:T(1,128)} %get-tuple-element.25), channel_id=1, source_target_pairs={{1,0},{2,1},{3,2},{4,3},{5,4},{6,5},{7,6},{9,8},{10,9},{11,10},{12... | collective-permute-start | bytes 98312 | tf_op jit(solution)/shard_map/ppermute | solution.py:17
  9.4 41.3 %collective-permute-start.2 = (f32[4,64,512]{2,1,0:T(8,128)}, f32[4,64,512]{2,1,0:T(8,128)}, u32[]{:S(2)}, u32[]{:S(2)}) collective-permute-start(f32[4,64,512]{2,1,0:T(8,128)} %get-tuple-element.27), channel_id=1, source_target_pairs={{0,8},{8,16},{16,24},{24,0},{1,9},{9,17},{17,25},{25,1},{2,10},{10... | collective-permute-start | bytes 1572872 | tf_op jit(solution)/shard_map/ppermute | solution.py:23
  12.5 38.2 %collective-permute-start.3 = (f32[4,64,512]{2,1,0:T(8,128)}, f32[4,64,512]{2,1,0:T(8,128)}, u32[]{:S(2)}, u32[]{:S(2)}) collective-permute-start(f32[4,64,512]{2,1,0:T(8,128)} %get-tuple-element.28), channel_id=1, source_target_pairs={{0,24},{8,0},{16,8},{24,16},{1,25},{9,1},{17,9},{25,17},{2,26},{10... | collective-permute-start | bytes 1572872 | tf_op jit(solution)/shard_map/ppermute | solution.py:23
  14.6 36.1 %collective-permute-start.4 = (f32[4,64,512]{2,1,0:T(8,128)}, f32[4,64,512]{2,1,0:T(8,128)}, u32[]{:S(2)}, u32[]{:S(2)}) collective-permute-start(f32[4,64,512]{2,1,0:T(8,128)} %get-tuple-element.29), channel_id=1, source_target_pairs={{0,1},{1,2},{2,3},{3,4},{4,5},{5,6},{6,7},{7,0},{8,9},{9,10},{10,1... | collective-permute-start | bytes 1572872 | tf_op jit(solution)/shard_map/ppermute | solution.py:23
  15.4 35.3 %collective-permute-start.5 = (f32[4,64,512]{2,1,0:T(8,128)}, f32[4,64,512]{2,1,0:T(8,128)}, u32[]{:S(2)}, u32[]{:S(2)}) collective-permute-start(f32[4,64,512]{2,1,0:T(8,128)} %get-tuple-element.30), channel_id=1, source_target_pairs={{0,7},{1,0},{2,1},{3,2},{4,3},{5,4},{6,5},{7,6},{8,15},{9,8},{10,9... | collective-permute-start | bytes 1572872 | tf_op jit(solution)/shard_map/ppermute | solution.py:23
  17.5 22.5 %collective-permute-start = (f32[1,32,512]{2,1,0:T(8,128)}, f32[1,32,512]{2,1,0:T(8,128)S(1)}, u32[]{:S(2)}, u32[]{:S(2)}) collective-permute-start(f32[1,32,512]{2,1,0:T(8,128)} %get-tuple-element.24), channel_id=1, source_target_pairs={{8,0},{16,8},{24,16},{9,1},{17,9},{25,17},{10,2},{18,10},{26,18},{... | collective-permute-start | bytes 196616 | tf_op jit(solution)/shard_map/ppermute | solution.py:17
  73.8 19.7 %collective-permute-start.16 = (f32[2,256,512]{2,1,0:T(8,128)}, f32[2,256,512]{2,1,0:T(8,128)}, u32[]{:S(2)}, u32[]{:S(2)}) collective-permute-start(f32[2,256,512]{2,1,0:T(8,128)} %get-tuple-element.40), channel_id=1, source_target_pairs={{0,1},{1,0},{2,3},{3,2},{4,5},{5,4},{6,7},{7,6},{8,9},{9,8},{10,11... | collective-permute-start | bytes 3145736 | tf_op jit(solution)/shard_map/ppermute | solution.py:349
  95.4 18.1 %collective-permute-start.17 = (f32[256,512]{1,0:T(8,128)S(1)}, f32[256,512]{1,0:T(8,128)S(1)}, u32[]{:S(2)}, u32[]{:S(2)}) collective-permute-start(f32[256,512]{1,0:T(8,128)S(1)} %get-tuple-element.46), channel_id=1, source_target_pairs={{0,2},{1,5},{2,0},{3,7},{4,6},{5,1},{6,4},{7,3},{8,10},{9,13},{10,... | collective-permute-start | bytes 1572872 | tf_op jit(solution)/shard_map/ppermute | solution.py:349
  98.7 16.4 %collective-permute-start.27 = (f32[256,512]{1,0:T(8,128)S(1)}, f32[256,512]{1,0:T(8,128)S(1)}, u32[]{:S(2)}, u32[]{:S(2)}) collective-permute-start(f32[256,512]{1,0:T(8,128)S(1)} %get-tuple-element.44), channel_id=1, source_target_pairs={{0,2},{1,5},{2,0},{3,7},{4,6},{5,1},{6,4},{7,3},{8,10},{9,13},{10,... | collective-permute-start | bytes 1572872 | tf_op jit(solution)/shard_map/ppermute | solution.py:349
  113.4 10.7 %collective-permute-start.6 = (f32[1,256,512]{2,1,0:T(8,128)}, f32[1,256,512]{2,1,0:T(8,128)S(1)}, u32[]{:S(2)}, u32[]{:S(2)}) collective-permute-start(f32[1,256,512]{2,1,0:T(8,128)} %get-tuple-element.38), channel_id=1, source_target_pairs={{0,1},{1,0},{2,3},{3,2},{4,5},{5,4},{6,7},{7,6},{8,9},{9,8},{10,11... | collective-permute-start | bytes 1572872 | tf_op jit(solution)/shard_map/ppermute | solution.py:349
  113.6 6.4 %collective-permute-start.18 = (f32[128,512]{1,0:T(8,128)S(1)}, f32[128,512]{1,0:T(8,128)S(1)}, u32[]{:S(2)}, u32[]{:S(2)}) collective-permute-start(f32[128,512]{1,0:T(8,128)S(1)} %get-tuple-element.50), channel_id=1, source_target_pairs={{0,4},{1,9},{2,6},{3,11},{4,0},{5,13},{6,2},{7,15},{8,12},{9,1},{1... | collective-permute-start | bytes 786440 | tf_op jit(solution)/shard_map/ppermute | solution.py:349
  115.1 7.7 %collective-permute-start.28 = (f32[128,512]{1,0:T(8,128)S(1)}, f32[128,512]{1,0:T(8,128)S(1)}, u32[]{:S(2)}, u32[]{:S(2)}) collective-permute-start(f32[128,512]{1,0:T(8,128)S(1)} %get-tuple-element.48), channel_id=1, source_target_pairs={{0,4},{1,9},{2,6},{3,11},{4,0},{5,13},{6,2},{7,15},{8,12},{9,1},{1... | collective-permute-start | bytes 786440 | tf_op jit(solution)/shard_map/ppermute | solution.py:349
  120.0 5.9 %collective-permute-start.19 = (f32[64,512]{1,0:T(8,128)S(1)}, f32[64,512]{1,0:T(8,128)S(1)}, u32[]{:S(2)}, u32[]{:S(2)}) collective-permute-start(f32[64,512]{1,0:T(8,128)S(1)} %get-tuple-element.56), channel_id=1, source_target_pairs={{0,8},{1,17},{2,10},{3,19},{4,12},{5,21},{6,14},{7,23},{8,0},{9,25... | collective-permute-start | bytes 393224 | tf_op jit(solution)/shard_map/ppermute | solution.py:349
  122.9 5.9 %collective-permute-start.29 = (f32[64,512]{1,0:T(8,128)S(1)}, f32[64,512]{1,0:T(8,128)S(1)}, u32[]{:S(2)}, u32[]{:S(2)}) collective-permute-start(f32[64,512]{1,0:T(8,128)S(1)} %get-tuple-element.54), channel_id=1, source_target_pairs={{0,8},{1,17},{2,10},{3,19},{4,12},{5,21},{6,14},{7,23},{8,0},{9,25... | collective-permute-start | bytes 393224 | tf_op jit(solution)/shard_map/ppermute | solution.py:349
  124.1 15.6 %collective-permute-start.7 = (f32[128,512]{1,0:T(8,128)S(1)}, f32[128,512]{1,0:T(8,128)S(1)}, u32[]{:S(2)}, u32[]{:S(2)}) collective-permute-start(f32[128,512]{1,0:T(8,128)S(1)} %get-tuple-element.52), channel_id=1, source_target_pairs={{0,2},{1,5},{2,0},{3,7},{4,6},{5,1},{6,4},{7,3},{8,10},{9,13},{10,... | collective-permute-start | bytes 786440 | tf_op jit(solution)/shard_map/ppermute | solution.py:349
  125.9 5.9 %collective-permute-start.20 = (f32[32,512]{1,0:T(8,128)S(1)}, f32[32,512]{1,0:T(8,128)S(1)}, u32[]{:S(2)}, u32[]{:S(2)}) collective-permute-start(f32[32,512]{1,0:T(8,128)S(1)} %add_bitcast_fusion.9), channel_id=1, source_target_pairs={{0,16},{1,3},{2,18},{3,1},{4,20},{5,7},{6,22},{7,5},{8,24},{9,11},... | collective-permute-start | bytes 196616 | tf_op jit(solution)/shard_map/ppermute | solution.py:349
  128.7 5.8 %collective-permute-start.30 = (f32[32,512]{1,0:T(8,128)S(1)}, f32[32,512]{1,0:T(8,128)S(1)}, u32[]{:S(2)}, u32[]{:S(2)}) collective-permute-start(f32[32,512]{1,0:T(8,128)S(1)} %add_bitcast_fusion.8), channel_id=1, source_target_pairs={{0,16},{1,3},{2,18},{3,1},{4,20},{5,7},{6,22},{7,5},{8,24},{9,11},... | collective-permute-start | bytes 196616 | tf_op jit(solution)/shard_map/ppermute | solution.py:349
  131.9 7.7 %collective-permute-start.21 = (f32[32,512]{1,0:T(8,128)S(1)}, f32[32,512]{1,0:T(8,128)S(1)}, u32[]{:S(2)}, u32[]{:S(2)}) collective-permute-start(f32[32,512]{1,0:T(8,128)S(1)} %bitcast_add_fusion.1), channel_id=1, source_target_pairs={{0,16},{1,3},{2,18},{3,1},{4,20},{5,7},{6,22},{7,5},{8,24},{9,11},... | collective-permute-start | bytes 196616 | tf_op jit(solution)/shard_map/ppermute | solution.py:349
  134.5 6.9 %collective-permute-start.31 = (f32[32,512]{1,0:T(8,128)S(1)}, f32[32,512]{1,0:T(8,128)S(1)}, u32[]{:S(2)}, u32[]{:S(2)}) collective-permute-start(f32[32,512]{1,0:T(8,128)S(1)} %bitcast_add_fusion), channel_id=1, source_target_pairs={{0,16},{1,3},{2,18},{3,1},{4,20},{5,7},{6,22},{7,5},{8,24},{9,11},... | collective-permute-start | bytes 196616 | tf_op jit(solution)/shard_map/ppermute | solution.py:349
  139.6 7.4 %collective-permute-start.22 = (f32[64,512]{1,0:T(8,128)S(1)}, f32[64,512]{1,0:T(8,128)S(1)}, u32[]{:S(2)}, u32[]{:S(2)}) collective-permute-start(f32[64,512]{1,0:T(8,128)S(1)} %maximum_select_fusion.9), channel_id=1, source_target_pairs={{0,8},{1,17},{2,10},{3,19},{4,12},{5,21},{6,14},{7,23},{8,0},{9,25... | collective-permute-start | bytes 393224 | tf_op jit(solution)/shard_map/ppermute | solution.py:349
  139.8 7.7 %collective-permute-start.8 = (f32[64,512]{1,0:T(8,128)S(1)}, f32[64,512]{1,0:T(8,128)S(1)}, u32[]{:S(2)}, u32[]{:S(2)}) collective-permute-start(f32[64,512]{1,0:T(8,128)S(1)} %get-tuple-element.58), channel_id=1, source_target_pairs={{0,4},{1,9},{2,6},{3,11},{4,0},{5,13},{6,2},{7,15},{8,12},{9,1},{1... | collective-permute-start | bytes 393224 | tf_op jit(solution)/shard_map/ppermute | solution.py:349
  141.4 8.5 %collective-permute-start.32 = (f32[64,512]{1,0:T(8,128)S(1)}, f32[64,512]{1,0:T(8,128)S(1)}, u32[]{:S(2)}, u32[]{:S(2)}) collective-permute-start(f32[64,512]{1,0:T(8,128)S(1)} %maximum_select_fusion.10), channel_id=1, source_target_pairs={{0,8},{1,17},{2,10},{3,19},{4,12},{5,21},{6,14},{7,23},{8,0},{9,25... | collective-permute-start | bytes 393224 | tf_op jit(solution)/shard_map/ppermute | solution.py:349
  147.1 7.0 %collective-permute-start.23 = (f32[128,512]{1,0:T(8,128)S(1)}, f32[128,512]{1,0:T(8,128)S(1)}, u32[]{:S(2)}, u32[]{:S(2)}) collective-permute-start(f32[128,512]{1,0:T(8,128)S(1)} %maximum_select_fusion.6), channel_id=1, source_target_pairs={{0,4},{1,9},{2,6},{3,11},{4,0},{5,13},{6,2},{7,15},{8,12},{9,1},{1... | collective-permute-start | bytes 786440 | tf_op jit(solution)/shard_map/ppermute | solution.py:349
  147.5 5.0 %collective-permute-start.9 = (f32[32,512]{1,0:T(8,128)S(1)}, f32[32,512]{1,0:T(8,128)S(1)}, u32[]{:S(2)}, u32[]{:S(2)}) collective-permute-start(f32[32,512]{1,0:T(8,128)S(1)} %get-tuple-element.60), channel_id=1, source_target_pairs={{0,8},{1,17},{2,10},{3,19},{4,12},{5,21},{6,14},{7,23},{8,0},{9,25... | collective-permute-start | bytes 196616 | tf_op jit(solution)/shard_map/ppermute | solution.py:349
  149.9 9.8 %collective-permute-start.33 = (f32[128,512]{1,0:T(8,128)S(1)}, f32[128,512]{1,0:T(8,128)S(1)}, u32[]{:S(2)}, u32[]{:S(2)}) collective-permute-start(f32[128,512]{1,0:T(8,128)S(1)} %maximum_select_fusion.7), channel_id=1, source_target_pairs={{0,4},{1,9},{2,6},{3,11},{4,0},{5,13},{6,2},{7,15},{8,12},{9,1},{1... | collective-permute-start | bytes 786440 | tf_op jit(solution)/shard_map/ppermute | solution.py:349
  152.5 7.7 %collective-permute-start.10 = (f32[16,512]{1,0:T(8,128)S(1)}, f32[16,512]{1,0:T(8,128)S(1)}, u32[]{:S(2)}, u32[]{:S(2)}) collective-permute-start(f32[16,512]{1,0:T(8,128)S(1)} %add_bitcast_fusion.11), channel_id=1, source_target_pairs={{0,16},{1,3},{2,18},{3,1},{4,20},{5,7},{6,22},{7,5},{8,24},{9,11},... | collective-permute-start | bytes 98312 | tf_op jit(solution)/shard_map/ppermute | solution.py:349
  154.1 16.7 %collective-permute-start.24 = (f32[256,512]{1,0:T(8,128)S(1)}, f32[256,512]{1,0:T(8,128)S(1)}, u32[]{:S(2)}, u32[]{:S(2)}) collective-permute-start(f32[256,512]{1,0:T(8,128)S(1)} %maximum_select_fusion.3), channel_id=1, source_target_pairs={{0,2},{1,5},{2,0},{3,7},{4,6},{5,1},{6,4},{7,3},{8,10},{9,13},{10,... | collective-permute-start | bytes 1572872 | tf_op jit(solution)/shard_map/ppermute | solution.py:349
  159.8 10.9 %collective-permute-start.34 = (f32[256,512]{1,0:T(8,128)S(1)}, f32[256,512]{1,0:T(8,128)S(1)}, u32[]{:S(2)}, u32[]{:S(2)}) collective-permute-start(f32[256,512]{1,0:T(8,128)S(1)} %maximum_select_fusion.4), channel_id=1, source_target_pairs={{0,2},{1,5},{2,0},{3,7},{4,6},{5,1},{6,4},{7,3},{8,10},{9,13},{10,... | collective-permute-start | bytes 1572872 | tf_op jit(solution)/shard_map/ppermute | solution.py:349
  169.5 5.3 %collective-permute-start.13 = (f32[64,512]{1,0:T(8,128)S(1)}, f32[64,512]{1,0:T(8,128)S(1)}, u32[]{:S(2)}, u32[]{:S(2)}) collective-permute-start(f32[64,512]{1,0:T(8,128)S(1)} %maximum_select_fusion.8), channel_id=1, source_target_pairs={{0,4},{1,9},{2,6},{3,11},{4,0},{5,13},{6,2},{7,15},{8,12},{9,1},{1... | collective-permute-start | bytes 393224 | tf_op jit(solution)/shard_map/ppermute | solution.py:349
  170.8 11.0 %collective-permute-start.35 = (f32[2,256,512]{2,1,0:T(8,128)S(1)}, f32[2,256,512]{2,1,0:T(8,128)S(1)}, u32[]{:S(2)}, u32[]{:S(2)}) collective-permute-start(f32[2,256,512]{2,1,0:T(8,128)S(1)} %bitcast.58), channel_id=1, source_target_pairs={{0,1},{1,0},{2,3},{3,2},{4,5},{5,4},{6,7},{7,6},{8,9},{9,8},{10,11... | collective-permute-start | bytes 3145736 | tf_op jit(solution)/shard_map/ppermute | solution.py:349
  171.0 12.3 %collective-permute-start.25 = (f32[2,256,512]{2,1,0:T(8,128)S(1)}, f32[2,256,512]{2,1,0:T(8,128)S(1)}, u32[]{:S(2)}, u32[]{:S(2)}) collective-permute-start(f32[2,256,512]{2,1,0:T(8,128)S(1)} %bitcast.56), channel_id=1, source_target_pairs={{0,1},{1,0},{2,3},{3,2},{4,5},{5,4},{6,7},{7,6},{8,9},{9,8},{10,11... | collective-permute-start | bytes 3145736 | tf_op jit(solution)/shard_map/ppermute | solution.py:349
  174.9 6.8 %collective-permute-start.14 = (f32[128,512]{1,0:T(8,128)S(1)}, f32[128,512]{1,0:T(8,128)S(1)}, u32[]{:S(2)}, u32[]{:S(2)}) collective-permute-start(f32[128,512]{1,0:T(8,128)S(1)} %maximum_select_fusion.5), channel_id=1, source_target_pairs={{0,2},{1,5},{2,0},{3,7},{4,6},{5,1},{6,4},{7,3},{8,10},{9,13},{10,... | collective-permute-start | bytes 786440 | tf_op jit(solution)/shard_map/ppermute | solution.py:349
  (18 other events, 214.9 us)
